TPU v7x, 32 devices: a whole 2x2x4 slice. The times are simulated.
32 devices in a mesh: dp: 16 (over z, y, core), tensor: 2 (over x).
Axes of the slice: x: 2, y: 2, z: 4, core: 2. Of those that a mesh axis runs over, the one named last changes fastest.
Arguments:
- layer_input: bfloat16 [32768, 1024], P(('dp', 'tensor')), may hold values from -6 to 6
- attention_norm: float32 [1024], replicated, may hold values from 0.25 to 1.75
- query_weight: bfloat16 [1024, 2048], P('dp', 'tensor'), may hold values from -0.1875 to 0.1875
- key_matrix: bfloat16 [1024, 1024], P('dp', 'tensor'), may hold values from -0.1875 to 0.1875
- value_matrix: bfloat16 [1024, 1024], P('dp', 'tensor'), may hold values from -0.1875 to 0.1875
- query_norm: float32 [128], replicated, may hold values from 0.25 to 1.75
- key_norm: float32 [128], replicated, may hold values from 0.25 to 1.75
- output_weight: bfloat16 [2048, 1024], P('tensor', 'dp'), may hold values from -0.5 to 0.5
- feedforward_norm: float32 [1024], replicated, may hold values from 0.25 to 1.75
- gate_weight: bfloat16 [1024, 3072], P('dp', 'tensor'), may hold values from -0.1875 to 0.1875
- up_weight: bfloat16 [1024, 3072], P('dp', 'tensor'), may hold values from -0.1875 to 0.1875
- down_weight: bfloat16 [3072, 1024], P('tensor', 'dp'), may hold values from -0.109375 to 0.109375
- out_grad: bfloat16 [32768, 1024], P(('dp', 'tensor')), may hold values from -6 to 6
Outputs:
- layer_output: bfloat16 [32768, 1024], P(('dp', 'tensor'))
- input_grad: float32 [32768, 1024], P(('dp', 'tensor'))
- attention_norm_grad: float32 [1024], replicated
- query_weight_grad: float32 [1024, 2048], P('dp', 'tensor')
- key_weight_grad: float32 [1024, 1024], P('dp', 'tensor')
- value_weight_grad: float32 [1024, 1024], P('dp', 'tensor')
- query_norm_grad: float32 [128], replicated
- key_norm_grad: float32 [128], replicated
- output_weight_grad: float32 [2048, 1024], P('tensor', 'dp')
- feedforward_norm_grad: float32 [1024], replicated
- gate_weight_grad: float32 [1024, 3072], P('dp', 'tensor')
- up_weight_grad: float32 [1024, 3072], P('dp', 'tensor')
- down_weight_grad: float32 [3072, 1024], P('tensor', 'dp')
All inputs are finite; a program needn't handle non-finite values.
Results may differ from a plain program's by a relative error of at most 0.019.
Values may be sent and summed in bfloat16 or wider, within the bound.
No kernel may reach another device: no remote copies, remote signals or barrier semaphores. Data moves between devices by JAX's collectives and lax.ppermute only.
A program may use at most 320 MiB of HBM per device.

v0:
```python
import jax
import jax.numpy as jnp
from jax import lax
from jax.sharding import PartitionSpec as P

HEAD_SIZE = 128
SEQ_LEN = 2048


epsilon = 1e-06
rope_base = 1000000.0
masked_score = -1e30


def rms_norm(values, gain):
    return values * lax.rsqrt(jnp.mean(values * values, axis=-1, keepdims=True) + epsilon) * gain


def rope_tables(sequence_length):
    position = jnp.arange(sequence_length).astype(jnp.float32)
    inverse = jnp.power(
        rope_base, -jnp.arange(HEAD_SIZE // 2).astype(jnp.float32) * (2.0 / HEAD_SIZE)
    )
    angles = position[:, None] * inverse[None, :]
    return (jnp.cos(angles), jnp.sin(angles))


def rotary(values, cosine, sine):
    half = values.shape[-1] // 2
    first = values[..., :half]
    second = values[..., half:]
    cos_wide = cosine[:, None, :]
    sin_wide = sine[:, None, :]
    return jnp.concatenate(
        [first * cos_wide - second * sin_wide, second * cos_wide + first * sin_wide], axis=-1
    )


def contract(left, right, left_dim, right_dim):
    return lax.dot_general(
        left, right, (((left_dim,), (right_dim,)), ((), ())), preferred_element_type=jnp.float32
    )


def split_blocks(values, block_slice):
    sequence_length = values.shape[0]
    return values.reshape((sequence_length // block_slice, block_slice) + values.shape[1:])


def block_scores(query_block, start, keys):
    block_slice = query_block.shape[0]
    scores = jnp.einsum(
        "qcgd,kcd->cgqk", query_block, keys, preferred_element_type=jnp.float32
    ) * HEAD_SIZE ** (-0.5)
    rows = start + jnp.arange(block_slice, dtype=jnp.int32)
    columns = jnp.arange(keys.shape[0], dtype=jnp.int32)
    allowed = columns[None, :] <= rows[:, None]
    return jnp.where(allowed, scores, masked_score)


def attend_forward(query_seq, key_seq, value_seq):
    sequence_length = query_seq.shape[0]
    block_slice = min(512, sequence_length)
    starts = jnp.arange(sequence_length // block_slice, dtype=jnp.int32) * block_slice

    def one_block(item):
        query_block, start = item
        scores = block_scores(query_block, start, key_seq)
        top = jnp.max(scores, axis=-1, keepdims=True)
        exps = jnp.exp(scores - top)
        total = jnp.sum(exps, axis=-1, keepdims=True)
        probs = exps / total
        mixed = jnp.einsum(
            "cgqk,kcd->qcgd",
            probs.astype(jnp.bfloat16),
            value_seq,
            preferred_element_type=jnp.float32,
        )
        return (mixed.astype(jnp.bfloat16), top[..., 0] + jnp.log(total[..., 0]))

    mixed, log_total = lax.map(one_block, (split_blocks(query_seq, block_slice), starts))
    return (mixed.reshape(sequence_length, -1), log_total)


def attend_backward(query_seq, key_seq, value_seq, grad_seq, log_total):
    sequence_length = query_seq.shape[0]
    block_slice = min(512, sequence_length)
    starts = jnp.arange(sequence_length // block_slice, dtype=jnp.int32) * block_slice
    zeros = jnp.zeros(key_seq.shape, jnp.float32)

    def one_block(carry, item):
        key_grad, value_grad = carry
        query_block, grad_block, total_block, start = item
        scores = block_scores(query_block, start, key_seq)
        probs = jnp.exp(scores - total_block[..., None])
        prob_grad = jnp.einsum(
            "qcgd,kcd->cgqk", grad_block, value_seq, preferred_element_type=jnp.float32
        )
        delta = jnp.sum(probs * prob_grad, axis=-1, keepdims=True)
        score_grad = (probs * (prob_grad - delta)).astype(jnp.bfloat16)
        query_grad = jnp.einsum(
            "cgqk,kcd->qcgd", score_grad, key_seq, preferred_element_type=jnp.float32
        ) * HEAD_SIZE ** (-0.5)
        key_grad = key_grad + jnp.einsum(
            "cgqk,qcgd->kcd", score_grad, query_block, preferred_element_type=jnp.float32
        ) * HEAD_SIZE ** (-0.5)
        value_grad = value_grad + jnp.einsum(
            "cgqk,qcgd->kcd",
            probs.astype(jnp.bfloat16),
            grad_block,
            preferred_element_type=jnp.float32,
        )
        return ((key_grad, value_grad), query_grad)

    (key_grad, value_grad), query_grad = lax.scan(
        one_block,
        (zeros, zeros),
        (
            split_blocks(query_seq, block_slice),
            split_blocks(grad_seq, block_slice),
            log_total,
            starts,
        ),
    )
    return (query_grad.reshape(query_seq.shape), key_grad, value_grad)


def on_device(
    layer_input,
    attention_norm,
    query_weight,
    key_matrix,
    value_matrix,
    query_norm,
    key_norm,
    output_weight,
    feedforward_norm,
    gate_weight,
    up_weight,
    down_weight,
    out_grad,
):
    tok_rows = layer_input.shape[0]
    group = tok_rows * lax.axis_size("tensor")
    sequences = group // SEQ_LEN
    query_heads = query_weight.shape[1] // HEAD_SIZE
    value_heads = key_matrix.shape[1] // HEAD_SIZE
    head_ratio = query_heads // value_heads
    cosine, sine = rope_tables(SEQ_LEN)

    def prepare(raw, gain):
        return rotary(rms_norm(raw, gain), cosine, sine)

    def gather_attention():
        return (
            lax.all_gather(query_weight, "dp", axis=0, tiled=True),
            lax.all_gather(key_matrix, "dp", axis=0, tiled=True),
            lax.all_gather(value_matrix, "dp", axis=0, tiled=True),
            lax.all_gather(output_weight, "dp", axis=1, tiled=True),
        )

    def gather_feedforward():
        return (
            lax.all_gather(gate_weight, "dp", axis=0, tiled=True),
            lax.all_gather(up_weight, "dp", axis=0, tiled=True),
            lax.all_gather(down_weight, "dp", axis=1, tiled=True),
        )

    input_float = layer_input.astype(jnp.float32)
    full_query, full_key, full_value, full_output = gather_attention()
    attention_layer_input = rms_norm(input_float, attention_norm).astype(jnp.bfloat16)
    attention_all = lax.all_gather(attention_layer_input, "tensor", axis=0, tiled=True)
    query_raw = jnp.dot(attention_all, full_query, preferred_element_type=jnp.float32).reshape(
        sequences, SEQ_LEN, query_heads, HEAD_SIZE
    )
    key_unrotated = jnp.dot(attention_all, full_key, preferred_element_type=jnp.float32).reshape(
        sequences, SEQ_LEN, value_heads, HEAD_SIZE
    )
    value_lowered = jnp.dot(attention_all, full_value, preferred_element_type=jnp.float32).astype(
        jnp.bfloat16
    )
    value_lowered = value_lowered.reshape(sequences, SEQ_LEN, value_heads, HEAD_SIZE)
    query_rotated = (
        prepare(query_raw, query_norm)
        .astype(jnp.bfloat16)
        .reshape(sequences, SEQ_LEN, value_heads, head_ratio, HEAD_SIZE)
    )
    key_rot = prepare(key_unrotated, key_norm).astype(jnp.bfloat16)
    mixed, log_total = lax.map(
        lambda item: attend_forward(item[0], item[1], item[2]),
        (query_rotated, key_rot, value_lowered),
    )
    mixed = mixed.reshape(group, query_heads * HEAD_SIZE)
    residual = input_float + lax.psum_scatter(
        jnp.dot(mixed, full_output, preferred_element_type=jnp.float32),
        "tensor",
        scatter_dimension=0,
        tiled=True,
    )
    ffn_input = rms_norm(residual, feedforward_norm).astype(jnp.bfloat16)
    ffn_all = lax.all_gather(ffn_input, "tensor", axis=0, tiled=True)
    full_gate, full_up, full_down = gather_feedforward()
    gate = jnp.dot(ffn_all, full_gate, preferred_element_type=jnp.float32)
    up_part = jnp.dot(ffn_all, full_up, preferred_element_type=jnp.float32)
    hidden = (jax.nn.silu(gate) * up_part).astype(jnp.bfloat16)
    layer_sum = residual + lax.psum_scatter(
        jnp.dot(hidden, full_down, preferred_element_type=jnp.float32).astype(jnp.bfloat16),
        "tensor",
        scatter_dimension=0,
        tiled=True,
    ).astype(jnp.float32)
    layer_output = layer_sum.astype(jnp.bfloat16)
    grad_float = out_grad.astype(jnp.float32)
    grad_all = lax.all_gather(out_grad, "tensor", axis=0, tiled=True)
    full_gate, full_up, full_down = gather_feedforward()
    down_part = contract(hidden, grad_all, 0, 0)
    hidden_grad = contract(grad_all, full_down, 1, 1)
    swiglu_value, swiglu_pull = jax.vjp(
        lambda gate_in, up_in: jax.nn.silu(gate_in) * up_in, gate, up_part
    )
    gate_grad, up_grad = swiglu_pull(hidden_grad)
    gate_bits = gate_grad.astype(jnp.bfloat16)
    up_bits = up_grad.astype(jnp.bfloat16)
    gate_part = contract(ffn_all, gate_bits, 0, 0)
    up_weight_part = contract(ffn_all, up_bits, 0, 0)
    ffn_input_grad = lax.psum_scatter(
        contract(gate_bits, full_gate, 1, 1) + contract(up_bits, full_up, 1, 1),
        "tensor",
        scatter_dimension=0,
        tiled=True,
    )
    norm_value, norm_two_pull = jax.vjp(rms_norm, residual, feedforward_norm)
    residual_norm_grad, norm_two_grad = norm_two_pull(ffn_input_grad)
    residual_grad = grad_float + residual_norm_grad
    proj_bits = residual_grad.astype(jnp.bfloat16)
    proj_all = lax.all_gather(proj_bits, "tensor", axis=0, tiled=True)
    gate_weight_grad, up_weight_grad, down_weight_grad = (
        lax.psum_scatter(
            gate_part.astype(jnp.bfloat16), "dp", scatter_dimension=0, tiled=True
        ).astype(jnp.float32),
        lax.psum_scatter(
            up_weight_part.astype(jnp.bfloat16), "dp", scatter_dimension=0, tiled=True
        ).astype(jnp.float32),
        lax.psum_scatter(
            down_part.astype(jnp.bfloat16), "dp", scatter_dimension=1, tiled=True
        ).astype(jnp.float32),
    )
    full_query, full_key, full_value, full_output = gather_attention()
    output_part = contract(mixed, proj_all, 0, 0)
    mixed_grad = contract(proj_all, full_output, 1, 1).astype(jnp.bfloat16)
    mixed_grad = mixed_grad.reshape(sequences, SEQ_LEN, value_heads, head_ratio, HEAD_SIZE)
    query_rot_grad, key_rot_grad, value_grad = lax.map(
        lambda item: attend_backward(item[0], item[1], item[2], item[3], item[4]),
        (query_rotated, key_rot, value_lowered, mixed_grad, log_total),
    )
    query_rot_grad = query_rot_grad.reshape(sequences, SEQ_LEN, query_heads, HEAD_SIZE)
    query_value, query_pull = jax.vjp(prepare, query_raw, query_norm)
    query_raw_grad, query_norm_part = query_pull(query_rot_grad)
    key_value, key_pull = jax.vjp(prepare, key_unrotated, key_norm)
    key_raw_grad, key_norm_part = key_pull(key_rot_grad)
    query_bits = query_raw_grad.reshape(group, query_heads * HEAD_SIZE).astype(jnp.bfloat16)
    key_bits = key_raw_grad.reshape(group, value_heads * HEAD_SIZE).astype(jnp.bfloat16)
    value_bits = value_grad.reshape(group, value_heads * HEAD_SIZE).astype(jnp.bfloat16)
    query_part = contract(attention_all, query_bits, 0, 0)
    key_part = contract(attention_all, key_bits, 0, 0)
    value_part = contract(attention_all, value_bits, 0, 0)
    attention_input_grad = lax.psum_scatter(
        (
            contract(query_bits, full_query, 1, 1)
            + contract(key_bits, full_key, 1, 1)
            + contract(value_bits, full_value, 1, 1)
        ).astype(jnp.bfloat16),
        "tensor",
        scatter_dimension=0,
        tiled=True,
    ).astype(jnp.float32)
    query_weight_grad, key_weight_grad, value_weight_grad, output_weight_grad = (
        lax.psum_scatter(
            query_part.astype(jnp.bfloat16), "dp", scatter_dimension=0, tiled=True
        ).astype(jnp.float32),
        lax.psum_scatter(
            key_part.astype(jnp.bfloat16), "dp", scatter_dimension=0, tiled=True
        ).astype(jnp.float32),
        lax.psum_scatter(
            value_part.astype(jnp.bfloat16), "dp", scatter_dimension=0, tiled=True
        ).astype(jnp.float32),
        lax.psum_scatter(
            output_part.astype(jnp.bfloat16), "dp", scatter_dimension=1, tiled=True
        ).astype(jnp.float32),
    )
    first_value, norm_one_pull = jax.vjp(rms_norm, input_float, attention_norm)
    input_norm_grad, norm_one_grad = norm_one_pull(attention_input_grad)
    input_grad = residual_grad + input_norm_grad
    attention_norm_grad, feedforward_norm_grad, query_norm_grad, key_norm_grad = lax.psum(
        (norm_one_grad, norm_two_grad, query_norm_part, key_norm_part), ("dp", "tensor")
    )
    return (
        layer_output,
        input_grad,
        attention_norm_grad,
        query_weight_grad,
        key_weight_grad,
        value_weight_grad,
        query_norm_grad,
        key_norm_grad,
        output_weight_grad,
        feedforward_norm_grad,
        gate_weight_grad,
        up_weight_grad,
        down_weight_grad,
    )


def solution(mesh):
    return jax.shard_map(
        on_device,
        mesh=mesh,
        in_specs=(
            P(("dp", "tensor"), None),
            P(),
            P("dp", "tensor"),
            P("dp", "tensor"),
            P("dp", "tensor"),
            P(),
            P(),
            P("tensor", "dp"),
            P(),
            P("dp", "tensor"),
            P("dp", "tensor"),
            P("tensor", "dp"),
            P(("dp", "tensor"), None),
        ),
        out_specs=(
            P(("dp", "tensor"), None),
            P(("dp", "tensor"), None),
            P(),
            P("dp", "tensor"),
            P("dp", "tensor"),
            P("dp", "tensor"),
            P(),
            P(),
            P("tensor", "dp"),
            P(),
            P("dp", "tensor"),
            P("dp", "tensor"),
            P("tensor", "dp"),
        ),
        check_vma=False,
    )
```

profile of v0, /device:TPU:0, one launch (start us, length us, event | category | flops | bytes accessed | tf_op | source)
XLA Modules:
  0.0 1861.7 jit_solution(3756011116326885370)
XLA Ops:
  20.3 34.0 %all-gather.14.cloned.1.call-done = bf16[1024,1024]{1,0:T(8,128)(2,1)} async-done(((bf16[64,1024]{1,0:T(8,128)(2,1)}), bf16[1024,1024]{1,0:T(8,128)(2,1)}) %all-gather.14.cloned.1.call-update) | async-done | bytes 2097168 | tf_op jit(solution)/shard_map/all_gather | solution.py:156
  54.3 57.7 %all-gather.12.cloned.1.call-done = bf16[2048,1024]{1,0:T(8,128)(2,1)} async-done(((bf16[1024,1024]{1,0:T(8,128)(2,1)}), bf16[2048,1024]{1,0:T(8,128)(2,1)}) %all-gather.12.cloned.1.call-update) | async-done | bytes 4194320 | tf_op jit(solution)/shard_map/all_gather | solution.py:172
  132.9 19.2 %all-gather.18.cloned.1.call-done = bf16[1024,512]{1,0:T(8,128)(2,1)} async-done(((bf16[64,512]{1,0:T(8,128)(2,1)}), bf16[1024,512]{1,0:T(8,128)(2,1)}) %all-gather.18.cloned.1.call-update) | async-done | bytes 1048592 | tf_op jit(solution)/shard_map/all_gather | solution.py:158
  161.3 29.7 %all-gather.16.cloned.1.call-done = bf16[1024,512]{1,0:T(8,128)(2,1)} async-done(((bf16[64,512]{1,0:T(8,128)(2,1)}), bf16[1024,512]{1,0:T(8,128)(2,1)}) %all-gather.16.cloned.1.call-update) | async-done | bytes 1048592 | tf_op jit(solution)/shard_map/all_gather | solution.py:157
  245.2 197.8 %while.47 = (s32[]{:T(128)}, bf16[4,512,4,2,128]{4,3,2,1,0:T(2,128)(2,1)}, f32[4,4,2,512]{3,2,1,0:T(2,128)}, s32[4]{0:T(128)S(1)}, bf16[4,512,4,2,128]{4,1,3,2,0...) while((s32[]{:T(128)}, ...), condition=%wide.region_6.7_spmd, body=%wide.region_3.6_spmd.sunk | while | flops 4397199872 | bytes 113381496 | solution.py:81
  247.1 15.3 bitcast_reduce_fusion.2
  262.4 15.1 fusion.124
  277.5 14.5 fusion.125
  296.5 15.3 bitcast_reduce_fusion.2
  311.8 15.1 fusion.124
  326.9 14.5 fusion.125
  346.0 15.3 bitcast_reduce_fusion.2
  361.3 15.1 fusion.124
  376.4 14.5 fusion.125
  395.4 15.3 bitcast_reduce_fusion.2
  410.7 15.1 fusion.124
  425.8 14.5 fusion.125
  451.3 10.7 fusion.61
  462.8 97.6 %reduce-scatter.12.cloned.1.call-done = f32[1024,1024]{1,0:T(8,128)} async-done(((f32[2048,1024]{1,0:T(8,128)}), f32[1024,1024]{1,0:T(8,128)}) %reduce-scatter.12.cloned.1.call-update) | async-done | bytes 4194320 | tf_op jit(solution)/shard_map/reduce_scatter | solution.py:194
  569.1 39.1 %all-gather.26.cloned.1.call-done = bf16[1024,1536]{1,0:T(8,128)(2,1)} async-done(((bf16[64,1536]{1,0:T(8,128)(2,1)}), bf16[1024,1536]{1,0:T(8,128)(2,1)}) %all-gather.26.cloned.1.call-update) | async-done | bytes 3145744 | tf_op jit(solution)/shard_map/all_gather | solution.py:165
  608.2 57.8 %all-gather.22.cloned.1.call-done = bf16[2048,1024]{1,0:T(8,128)(2,1)} async-done(((bf16[1024,1024]{1,0:T(8,128)(2,1)}), bf16[2048,1024]{1,0:T(8,128)(2,1)}) %all-gather.22.cloned.1.call-update) | async-done | bytes 4194320 | tf_op jit(solution)/shard_map/all_gather | solution.py:201
  666.0 12.4 fusion.63
  678.3 35.4 %all-gather.24.cloned.1.call-done = bf16[1024,1536]{1,0:T(8,128)(2,1)} async-done(((bf16[64,1536]{1,0:T(8,128)(2,1)}), bf16[1024,1536]{1,0:T(8,128)(2,1)}) %all-gather.24.cloned.1.call-update) | async-done | bytes 3145744 | tf_op jit(solution)/shard_map/all_gather | solution.py:164
  713.8 12.3 fusion.62
  726.1 44.7 %all-gather.30.cloned.1.call-done = bf16[2048,1024]{1,0:T(8,128)(2,1)} async-done(((bf16[1024,1024]{1,0:T(8,128)(2,1)}), bf16[2048,1024]{1,0:T(8,128)(2,1)}) %all-gather.30.cloned.1.call-update) | async-done | bytes 4194320 | tf_op jit(solution)/shard_map/all_gather | solution.py:214
  770.8 47.8 %all-gather.28.cloned.1.call-done = bf16[1536,1024]{0,1:T(8,128)(2,1)} async-done(((bf16[1536,64]{0,1:T(8,128)(2,1)}), bf16[1536,1024]{0,1:T(8,128)(2,1)}) %all-gather.28.cloned.1.call-update) | async-done | bytes 3145744 | tf_op jit(solution)/shard_map/all_gather | solution.py:166
  818.6 23.9 %multiply_convert_fusion = (bf16[2048,1536]{1,0:T(8,128)(2,1)}, bf16[2048,1536]{1,0:T(8,128)(2,1)}, bf16[2048,1536]{1,0:T(8,128)(2,1)}) fusion(f32[2048,1536]{1,0:T(8,128)} %fusion.62, f32[2048,1536]{1,0:T(8,128)} %fusion.63, bf16[2048,1024]{1,0:T(8,128)(2,1)} %all-gather.30.cloned.1.call-done, bf16[1536,1024]{0,1:T(8,128)(2,1)} %all-gather.28.cloned.1.call-done), kind=kOutput, calls=%fused_computation.55 | convolution fusion | flops 6492782592 | bytes 51380224 | tf_op jit(solution)/shard_map/dot_general | solution.py:40
  842.5 9.9 fusion.64
  861.6 98.1 %reduce-scatter.16.cloned.1.call-done = f32[1024,1024]{1,0:T(8,128)} async-done(((f32[2048,1024]{1,0:T(8,128)}), f32[1024,1024]{1,0:T(8,128)}) %reduce-scatter.16.cloned.1.call-update) | async-done | bytes 4194320 | tf_op jit(solution)/shard_map/reduce_scatter | solution.py:226
  968.3 11.3 convolution_convert_fusion
  979.7 11.8 convolution_convert_fusion.1
  991.6 11.6 convolution_convert_fusion.2
  1003.3 21.9 %all-gather.32.cloned.1.call-done = bf16[2048,1024]{1,0:T(8,128)(2,1)} async-done(((bf16[1024,1024]{1,0:T(8,128)(2,1)}), bf16[2048,1024]{1,0:T(8,128)(2,1)}) %all-gather.32.cloned.1.call-update) | async-done | bytes 4194320 | tf_op jit(solution)/shard_map/all_gather | solution.py:236
  1041.5 432.5 %while.48 = (s32[]{:T(128)}, f32[2048,4,128]{0,2,1:T(8,128)}, f32[2048,4,128]{0,2,1:T(8,128)}, f32[4,512,4,2,128]{4,1,0,3,2:T(8,128)}, bf16[4,512,4,2,128]{4,1,3...) while((s32[]{:T(128)}, f32[2048,4,128]{0,2,1:T(8,128)}, ...), condition=%wide.region_14.15_spmd.clone, body=%wide.region_12.14_spmd.clone.sunk | while | flops 10819727360 | bytes 302076096 | solution.py:115
  1046.5 13.5 fusion.132
  1060.1 24.4 %fusion.133 = (f32[4,2,512]{2,1,0:T(2,128)S(1)}, f32[4,2,512,2048]{3,2,1,0:T(8,128)}) fusion(f32[4,512,2,2048]{3,1,2,0:T(8,128)} %fusion.132, f32[4,2,512]{2,1,0:T(2,128)S(1)} %dynamic-slice_bitcast_fusion.2, bf16[2048,4,128]{2,0,1:T(8,128)(2,1)S(1)} %copy-done.4, bf16[4,512,4,2,128]{4,1,3,2,0:T(8,128)(2,1)} %get-tuple-element.487, s32[]{:T(128)S(6)} %copy.146, ...), kind=kOutput, calls=%fused_computation.23.clone.1 | convolution fusion | flops 2189422592 | bytes 71335936 | tf_op jit(solution)/shard_map/while/body/eval_jaxpr/while/body/eval_jaxpr/qcgd,kcd->cgqk/dot_general | solution.py:52
  1084.5 28.3 %fusion.134 = bf16[4,2,512,2048]{3,2,1,0:T(8,128)(2,1)} fusion(f32[4,2,512,2048]{3,2,1,0:T(8,128)} %get-tuple-element.433, f32[4,512,2,2048]{3,1,2,0:T(8,128)} %fusion.132, f32[4,2,512]{2,1,0:T(2,128)S(1)} %get-tuple-element.434), kind=kLoop, calls=%fused_computation.25.clone.1 | loop fusion | flops 25165824 | bytes 83902464 | tf_op jit(solution)/shard_map/while/body/eval_jaxpr/while/body/eval_jaxpr/convert_element_type | solution.py:100
  1112.8 15.6 bitcast_add_fusion.5
  1128.4 11.2 bitcast_add_fusion.4
  1139.6 9.7 bitcast_dynamic-update-slice_fusion.5
  1153.9 13.2 fusion.132
  1167.1 24.6 %fusion.133 = (f32[4,2,512]{2,1,0:T(2,128)S(1)}, f32[4,2,512,2048]{3,2,1,0:T(8,128)}) fusion(f32[4,512,2,2048]{3,1,2,0:T(8,128)} %fusion.132, f32[4,2,512]{2,1,0:T(2,128)S(1)} %dynamic-slice_bitcast_fusion.2, bf16[2048,4,128]{2,0,1:T(8,128)(2,1)S(1)} %copy-done.4, bf16[4,512,4,2,128]{4,1,3,2,0:T(8,128)(2,1)} %get-tuple-element.487, s32[]{:T(128)S(6)} %copy.146, ...), kind=kOutput, calls=%fused_computation.23.clone.1 | convolution fusion | flops 2189422592 | bytes 71335936 | tf_op jit(solution)/shard_map/while/body/eval_jaxpr/while/body/eval_jaxpr/qcgd,kcd->cgqk/dot_general | solution.py:52
  1191.7 28.2 %fusion.134 = bf16[4,2,512,2048]{3,2,1,0:T(8,128)(2,1)} fusion(f32[4,2,512,2048]{3,2,1,0:T(8,128)} %get-tuple-element.433, f32[4,512,2,2048]{3,1,2,0:T(8,128)} %fusion.132, f32[4,2,512]{2,1,0:T(2,128)S(1)} %get-tuple-element.434), kind=kLoop, calls=%fused_computation.25.clone.1 | loop fusion | flops 25165824 | bytes 83902464 | tf_op jit(solution)/shard_map/while/body/eval_jaxpr/while/body/eval_jaxpr/convert_element_type | solution.py:100
  1219.9 16.5 bitcast_add_fusion.5
  1236.4 12.3 bitcast_add_fusion.4
  1262.9 13.1 fusion.132
  1276.0 24.3 %fusion.133 = (f32[4,2,512]{2,1,0:T(2,128)S(1)}, f32[4,2,512,2048]{3,2,1,0:T(8,128)}) fusion(f32[4,512,2,2048]{3,1,2,0:T(8,128)} %fusion.132, f32[4,2,512]{2,1,0:T(2,128)S(1)} %dynamic-slice_bitcast_fusion.2, bf16[2048,4,128]{2,0,1:T(8,128)(2,1)S(1)} %copy-done.4, bf16[4,512,4,2,128]{4,1,3,2,0:T(8,128)(2,1)} %get-tuple-element.487, s32[]{:T(128)S(6)} %copy.146, ...), kind=kOutput, calls=%fused_computation.23.clone.1 | convolution fusion | flops 2189422592 | bytes 71335936 | tf_op jit(solution)/shard_map/while/body/eval_jaxpr/while/body/eval_jaxpr/qcgd,kcd->cgqk/dot_general | solution.py:52
  1300.4 27.5 %fusion.134 = bf16[4,2,512,2048]{3,2,1,0:T(8,128)(2,1)} fusion(f32[4,2,512,2048]{3,2,1,0:T(8,128)} %get-tuple-element.433, f32[4,512,2,2048]{3,1,2,0:T(8,128)} %fusion.132, f32[4,2,512]{2,1,0:T(2,128)S(1)} %get-tuple-element.434), kind=kLoop, calls=%fused_computation.25.clone.1 | loop fusion | flops 25165824 | bytes 83902464 | tf_op jit(solution)/shard_map/while/body/eval_jaxpr/while/body/eval_jaxpr/convert_element_type | solution.py:100
  1327.8 16.3 bitcast_add_fusion.5
  1344.2 12.3 bitcast_add_fusion.4
  1356.5 9.6 bitcast_dynamic-update-slice_fusion.5
  1370.7 13.1 fusion.132
  1383.8 24.3 %fusion.133 = (f32[4,2,512]{2,1,0:T(2,128)S(1)}, f32[4,2,512,2048]{3,2,1,0:T(8,128)}) fusion(f32[4,512,2,2048]{3,1,2,0:T(8,128)} %fusion.132, f32[4,2,512]{2,1,0:T(2,128)S(1)} %dynamic-slice_bitcast_fusion.2, bf16[2048,4,128]{2,0,1:T(8,128)(2,1)S(1)} %copy-done.4, bf16[4,512,4,2,128]{4,1,3,2,0:T(8,128)(2,1)} %get-tuple-element.487, s32[]{:T(128)S(6)} %copy.146, ...), kind=kOutput, calls=%fused_computation.23.clone.1 | convolution fusion | flops 2189422592 | bytes 71335936 | tf_op jit(solution)/shard_map/while/body/eval_jaxpr/while/body/eval_jaxpr/qcgd,kcd->cgqk/dot_general | solution.py:52
  1408.2 27.5 %fusion.134 = bf16[4,2,512,2048]{3,2,1,0:T(8,128)(2,1)} fusion(f32[4,2,512,2048]{3,2,1,0:T(8,128)} %get-tuple-element.433, f32[4,512,2,2048]{3,1,2,0:T(8,128)} %fusion.132, f32[4,2,512]{2,1,0:T(2,128)S(1)} %get-tuple-element.434), kind=kLoop, calls=%fused_computation.25.clone.1 | loop fusion | flops 25165824 | bytes 83902464 | tf_op jit(solution)/shard_map/while/body/eval_jaxpr/while/body/eval_jaxpr/convert_element_type | solution.py:100
  1435.6 16.3 bitcast_add_fusion.5
  1452.0 12.3 bitcast_add_fusion.4
  1502.9 9.9 multiply_add_fusion.1
  1561.9 11.7 convolution_convert_fusion.3
  1580.5 22.9 %reduce-scatter.24.cloned.1.call-done = bf16[64,512]{1,0:T(8,128)(2,1)} async-done(((bf16[1024,512]{1,0:T(8,128)(2,1)}), bf16[64,512]{1,0:T(8,128)(2,1)}) %reduce-scatter.24.cloned.1.call-update) | async-done | bytes 65552 | tf_op jit(solution)/shard_map/reduce_scatter | solution.py:284
  1604.9 62.8 %reduce-scatter.26.cloned.1.call-done = bf16[1024,64]{0,1:T(8,128)(2,1)} async-done(((bf16[1024,1024]{0,1:T(8,128)(2,1)}), bf16[1024,64]{0,1:T(8,128)(2,1)}) %reduce-scatter.26.cloned.1.call-update) | async-done | bytes 131088 | tf_op jit(solution)/shard_map/reduce_scatter | solution.py:287
  1669.4 63.0 %reduce-scatter.20.cloned.1.call-done = bf16[64,1024]{1,0:T(8,128)(2,1)} async-done(((bf16[1024,1024]{1,0:T(8,128)(2,1)}), bf16[64,1024]{1,0:T(8,128)(2,1)}) %reduce-scatter.20.cloned.1.call-update) | async-done | bytes 131088 | tf_op jit(solution)/shard_map/reduce_scatter | solution.py:278
  1734.0 54.6 %reduce-scatter.18.cloned.1.call-done = bf16[1024,1024]{1,0:T(8,128)(2,1)} async-done(((bf16[2048,1024]{1,0:T(8,128)(2,1)}), bf16[1024,1024]{1,0:T(8,128)(2,1)}) %reduce-scatter.18.cloned.1.call-update) | async-done | bytes 2097168 | tf_op jit(solution)/shard_map/reduce_scatter | solution.py:267
  1791.9 40.1 %all-reduce.4 = (f32[1024]{0:T(1024)}, f32[128]{0:T(128)}, f32[128]{0:T(128)}, f32[1024]{0:T(1024)}) all-reduce(f32[1024]{0:T(1024)S(1)} %get-tuple-element.262, f32[128]{0:T(128)S(1)} %get-tuple-element.256, f32[128]{0:T(128)S(1)} %get-tuple-element.260, f32[1024]{0:T(1024)S(1)} %copy-done.46), channel_id=1, replica_groups=mesh['dp'=16,'tensor'=2] {'dp','tensor'}, use_global_device_ids=true, to_apply=%region_20.21 | all-reduce | flops 2304 | bytes 18432 | tf_op jit(solution)/shard_map/psum | solution.py:294
  1832.0 14.5 reduce-scatter.14.cloned.1.call-done
  (300 shorter events, 305.4 us)
Async XLA Ops:
  7.2 47.1 %all-gather.14.cloned.1.call-start = ((), (), s32[]{:S(2)}) async-start(), calls=%async_computation.12 | async-start | bytes 2228224 | tf_op jit(solution)/shard_map/all_gather | solution.py:156
  7.9 104.0 %all-gather.12.cloned.1.call-start = ((), (), s32[]{:S(2)}) async-start(), calls=%async_computation.11 | async-start | bytes 6291456 | tf_op jit(solution)/shard_map/all_gather | solution.py:172
  14.7 137.4 %all-gather.18.cloned.1.call-start = ((), (), s32[]{:S(2)}) async-start(), calls=%async_computation.14 | async-start | bytes 1114112 | tf_op jit(solution)/shard_map/all_gather | solution.py:158
  15.4 175.5 %all-gather.16.cloned.1.call-start = ((), (), s32[]{:S(2)}) async-start(), calls=%async_computation.13 | async-start | bytes 1114112 | tf_op jit(solution)/shard_map/all_gather | solution.py:157
  16.0 435.2 %all-gather.20.cloned.1.call-start = ((), (), s32[]{:S(2)}) async-start(), calls=%async_computation.15 | async-start | bytes 2228224 | tf_op jit(solution)/shard_map/all_gather | solution.py:159
  16.6 543.8 %reduce-scatter.12.cloned.1.call-start = ((), (), s32[]{:S(2)}) async-start(), calls=%async_computation.16 | async-start | bytes 12582912 | tf_op jit(solution)/shard_map/reduce_scatter | solution.py:194
  18.6 100.7 %copy-start.17 = (f32[2048,64]{0,1:T(8,128)}, f32[2048,64]{0,1:T(8,128)S(1)}, u32[]{:S(2)}) copy-start(f32[2048,64]{0,1:T(8,128)S(1)} %get-tuple-element.321) | copy-start | bytes 1572868
  18.6 100.7 %copy-start.19 = (f32[2048,64]{0,1:T(8,128)}, f32[2048,64]{0,1:T(8,128)S(1)}, u32[]{:S(2)}) copy-start(f32[2048,64]{0,1:T(8,128)S(1)} %get-tuple-element.322) | copy-start | bytes 1572868
  19.0 192.1 %copy-start.13 = (f32[2048,64]{1,0:T(8,128)}, f32[2048,64]{1,0:T(8,128)S(1)}, u32[]{:S(2)}) copy-start(f32[2048,64]{1,0:T(8,128)S(1)} %copy.73) | copy-start | bytes 1572868
  123.7 81.1 %copy-start.29 = (f32[2048,8]{0,1:T(8,128)}, f32[2048,8]{0,1:T(8,128)S(1)}, u32[]{:S(2)}) copy-start(f32[2048,8]{0,1:T(8,128)S(1)} %multiply_reduce_fusion.2) | copy-start | bytes 196612
  204.8 6.2 copy-start.26
  443.0 8.3 copy-start.2
  443.0 8.3 copy-start.56
  462.0 98.4 %copy-start.8 = (bf16[1024,1024]{1,0:T(8,128)(2,1)S(1)}, bf16[1024,1024]{1,0:T(8,128)(2,1)}, u32[]{:S(2)}) copy-start(bf16[1024,1024]{1,0:T(8,128)(2,1)} %param.17) | copy-start | bytes 6291460
  462.0 146.2 %all-gather.26.cloned.1.call-start = ((), (), s32[]{:S(2)}) async-start(), calls=%async_computation.19 | async-start | bytes 3342336 | tf_op jit(solution)/shard_map/all_gather | solution.py:165
  462.8 102.5 %copy-start.37 = (f32[1024]{0:T(1024)S(1)}, f32[1024]{0:T(1024)}, u32[]{:S(2)}) copy-start(f32[1024]{0:T(1024)} %param.25) | copy-start | bytes 12292
  462.8 203.2 %all-gather.22.cloned.1.call-start = ((), (), s32[]{:S(2)}) async-start(), calls=%async_computation.17 | async-start | bytes 6291456 | tf_op jit(solution)/shard_map/all_gather | solution.py:201
  563.2 401.7 %copy-start.35 = (f32[1024]{0:T(1024)}, f32[1024]{0:T(1024)S(1)}, u32[]{:S(2)}) copy-start(f32[1024]{0:T(1024)S(1)} %fusion.57) | copy-start | bytes 12292
  567.0 146.8 %all-gather.24.cloned.1.call-start = ((), (), s32[]{:S(2)}) async-start(), calls=%async_computation.18 | async-start | bytes 3342336 | tf_op jit(solution)/shard_map/all_gather | solution.py:164
  567.8 203.1 %all-gather.30.cloned.1.call-start = ((), (), s32[]{:S(2)}) async-start(), calls=%async_computation.22 | async-start | bytes 6291456 | tf_op jit(solution)/shard_map/all_gather | solution.py:214
  568.3 250.3 %all-gather.28.cloned.1.call-start = ((), (), s32[]{:S(2)}) async-start(), calls=%async_computation.20 | async-start | bytes 3342336 | tf_op jit(solution)/shard_map/all_gather | solution.py:166
  569.1 390.6 %reduce-scatter.16.cloned.1.call-start = ((), (), s32[]{:S(2)}) async-start(), calls=%async_computation.23 | async-start | bytes 12582912 | tf_op jit(solution)/shard_map/reduce_scatter | solution.py:226
  842.5 9.9 copy-start.53
  842.5 9.9 copy-start.58
  861.5 104.0 %copy-start.12 = (bf16[1024,1024]{1,0:T(8,128)(2,1)S(1)}, bf16[1024,1024]{1,0:T(8,128)(2,1)}, u32[]{:S(2)}) copy-start(bf16[1024,1024]{1,0:T(8,128)(2,1)} %param.29) | copy-start | bytes 6291460
  861.5 163.7 %all-gather.32.cloned.1.call-start = ((), (), s32[]{:S(2)}) async-start(), calls=%async_computation.24 | async-start | bytes 6291456 | tf_op jit(solution)/shard_map/all_gather | solution.py:236
  968.3 605.5 %reduce-scatter.32.cloned.1.call-start = ((), (), s32[]{:S(2)}) async-start(), calls=%async_computation.32 | async-start | bytes 3342336 | tf_op jit(solution)/shard_map/reduce_scatter | solution.py:244
  979.7 595.9 %reduce-scatter.30.cloned.1.call-start = ((), (), s32[]{:S(2)}) async-start(), calls=%async_computation.31 | async-start | bytes 3342336 | tf_op jit(solution)/shard_map/reduce_scatter | solution.py:241
  991.5 585.8 %reduce-scatter.28.cloned.1.call-start = ((), (), s32[]{:S(2)}) async-start(), calls=%async_computation.30 | async-start | bytes 3342336 | tf_op jit(solution)/shard_map/reduce_scatter | solution.py:238
  991.6 33.6 %copy-start.55 = (bf16[1024,1024]{0,1:T(8,128)(2,1)S(1)}, bf16[1024,1024]{0,1:T(8,128)(2,1)}, u32[]{:S(2)}) copy-start(bf16[1024,1024]{0,1:T(8,128)(2,1)} %all-gather.20.cloned.1.call-done) | copy-start | bytes 6291460
  1003.2 575.8 %reduce-scatter.22.cloned.1.call-start = ((), (), s32[]{:S(2)}) async-start(), calls=%async_computation.27 | async-start | bytes 1114112 | tf_op jit(solution)/shard_map/reduce_scatter | solution.py:281
  1033.5 8.0 copy-start.3
  1033.5 8.0 copy-start.57
  1046.5 13.6 copy-start.4
  1128.4 11.2 copy-start.5
  1153.9 13.2 copy-start.4
  1236.4 12.3 copy-start.5
  1262.9 13.1 copy-start.4
  1344.2 12.3 copy-start.5
  1370.7 13.1 copy-start.4
  1452.0 12.3 copy-start.5
  1485.4 118.0 %reduce-scatter.24.cloned.1.call-start = ((), (), s32[]{:S(2)}) async-start(), calls=%async_computation.28 | async-start | bytes 1114112 | tf_op jit(solution)/shard_map/reduce_scatter | solution.py:284
  1492.9 10.0 copy-start.14
  1492.9 10.0 copy-start.16
  1492.9 174.9 %reduce-scatter.26.cloned.1.call-start = ((), (), s32[]{:S(2)}) async-start(), calls=%async_computation.29 | async-start | bytes 2228224 | tf_op jit(solution)/shard_map/reduce_scatter | solution.py:287
  1502.8 229.6 %reduce-scatter.20.cloned.1.call-start = ((), (), s32[]{:S(2)}) async-start(), calls=%async_computation.26 | async-start | bytes 2228224 | tf_op jit(solution)/shard_map/reduce_scatter | solution.py:278
  1502.8 10.0 slice-start
  1502.9 11.4 slice-start.1
  1502.9 11.4 copy-start.27
  1502.9 11.4 copy-start.48
  1512.8 10.3 slice-start.2
  1514.2 8.8 copy-start.30
  1514.3 8.8 slice-start.3
  1538.3 10.0 copy-start.25
  1547.8 240.8 %reduce-scatter.18.cloned.1.call-start = ((), (), s32[]{:S(2)}) async-start(), calls=%async_computation.25 | async-start | bytes 6291456 | tf_op jit(solution)/shard_map/reduce_scatter | solution.py:267
  1561.7 284.8 %reduce-scatter.14.cloned.1.call-start = ((), (), s32[]{:S(2)}) async-start(), calls=%async_computation.21 | async-start | bytes 6291456 | tf_op jit(solution)/shard_map/reduce_scatter | solution.py:206
  1573.6 214.9 %copy-start.9 = (bf16[1024,1024]{1,0:T(8,128)(2,1)S(1)}, bf16[1024,1024]{1,0:T(8,128)(2,1)}, u32[]{:S(2)}) copy-start(bf16[1024,1024]{1,0:T(8,128)(2,1)} %param.17) | copy-start | bytes 6291460
  1573.7 214.9 %copy-start.40 = (f32[1024]{0:T(1024)S(1)}, f32[1024]{0:T(1024)}, u32[]{:S(2)}) copy-start(f32[1024]{0:T(1024)} %copy-done.39) | copy-start | bytes 12292
  1573.7 214.9 %copy-start.45 = (f32[1024]{0:T(1024)S(1)}, f32[1024]{0:T(1024)}, u32[]{:S(2)}) copy-start(f32[1024]{0:T(1024)} %param.18) | copy-start | bytes 12292
  1573.7 218.2 %copy-start.46 = (f32[1024]{0:T(1024)S(1)}, f32[1024]{0:T(1024)}, u32[]{:S(2)}) copy-start(f32[1024]{0:T(1024)} %get-tuple-element.258) | copy-start | bytes 12292
  1573.7 258.3 %copy-start.44 = (f32[1024]{0:T(1024)S(1)}, f32[1024]{0:T(1024)}, u32[]{:S(2)}) copy-start(f32[1024]{0:T(1024)} %copy-done.43) | copy-start | bytes 12292
  1573.7 272.8 %copy-start.36 = (f32[1024]{0:T(1024)S(1)}, f32[1024]{0:T(1024)}, u32[]{:S(2)}) copy-start(f32[1024]{0:T(1024)} %copy-done.35) | copy-start | bytes 12292
  1573.7 272.8 %copy-start.38 = (f32[1024]{0:T(1024)S(1)}, f32[1024]{0:T(1024)}, u32[]{:S(2)}) copy-start(f32[1024]{0:T(1024)} %param.25) | copy-start | bytes 12292
  1573.7 272.8 %copy-start.42 = (f32[1024]{0:T(1024)S(1)}, f32[1024]{0:T(1024)}, u32[]{:S(2)}) copy-start(f32[1024]{0:T(1024)} %copy-done.41) | copy-start | bytes 12292
  (27 other events, 78.6 us)
Sparse Core Ops, SparseCore 0:
  10.2 44.0 all-gather.13
  56.4 55.4 all-gather.11
  114.1 37.9 all-gather.17
  154.1 36.8 all-gather.15
  193.0 40.2 all-gather.19
  462.1 98.2 reduce-scatter.11
  563.0 45.2 all-gather.25
  610.4 55.5 all-gather.21
  668.5 45.1 all-gather.23
  715.2 55.5 all-gather.29
  773.4 45.1 all-gather.27
  861.6 98.0 reduce-scatter.15
  968.4 56.7 all-gather.31
  1028.8 66.2 reduce-scatter.31
  1098.8 65.1 reduce-scatter.29
  1167.6 65.2 reduce-scatter.27
  1485.6 57.4 reduce-scatter.21
  1546.9 56.4 reduce-scatter.23
  1607.2 60.5 reduce-scatter.25
  1671.8 60.5 reduce-scatter.19
  1735.2 53.2 reduce-scatter.17
  1791.0 55.5 reduce-scatter.13
where the time goes:
time: 1870 us; the launch traced here: 1860 us
  waiting for transfers between devices  806 us (43%)
  matrix products  612 us (33%)
  other arithmetic  287 us (15%)
  local copies, waits for them, and re-layouts  98.7 us (5%)
  blocking collectives  40.1 us (2%)
    dot_general x8, matrix products, block_scores(): jnp.einsum('qcgd,kcd->cgqk', query_block, keys, preferred_element_type=jn...  159 us
    dot_general x14, matrix products, contract(): lax.dot_general(left, right, (((left_dim,), (right_dim,)), ((), ())), pre...  125 us
    convert_element_type x4, other arithmetic, one_block(): score_grad = (probs * (prob_grad - delta)).astype(jnp.bfloat16)  111 us
    reduce_scatter x1, waiting for transfers between devices, on_device(): lax.psum_scatter(contract(gate_bits, full_gate, 1, 1) + contract(up_bits,...  98.1 us
    reduce_scatter x1, waiting for transfers between devices, on_device(): lax.psum_scatter(jnp.dot(mixed, full_output, preferred_element_type=jnp.f...  97.6 us
    dot_general x4, matrix products, one_block(): jnp.einsum('cgqk,qcgd->kcd', probs.astype(jnp.bfloat16), grad_block, pref...  64.8 us
    reduce_scatter x1, waiting for transfers between devices, on_device(): lax.psum_scatter(query_part.astype(jnp.bfloat16), 'dp', scatter_dimension...  63 us
    reduce_scatter x1, waiting for transfers between devices, on_device(): lax.psum_scatter(output_part.astype(jnp.bfloat16), 'dp', scatter_dimensio...  62.8 us
  transfers between devices with their start and end apart: 22, of which 17 were waited for; matrix products, arithmetic and copies ran while one was open for 49% of the time, Pallas kernels for 0%

commit v1 on v0

v1 whole, which is shorter than its diff:
```python
import math

import jax
import jax.numpy as jnp
from jax import lax
from jax.experimental import pallas as pl
from jax.experimental.pallas import tpu as pltpu
from jax.sharding import PartitionSpec as P

HEAD_SIZE = 128
SEQ_LEN = 2048

epsilon = 1e-06
rope_base = 1000000.0
masked_score = -1e30
LN2 = math.log(2.0)
SCORE_SCALE = HEAD_SIZE ** (-0.5)
GROUP = 4 * HEAD_SIZE
F32 = jnp.float32
BF16 = jnp.bfloat16
VMEM_LIMIT = 60 * 1024 * 1024
HALF = SEQ_LEN // 2


def nn(left, right):
    return lax.dot_general(left, right, (((1,), (0,)), ((), ())), preferred_element_type=F32)


def nt(left, right):
    return lax.dot_general(left, right, (((1,), (1,)), ((), ())), preferred_element_type=F32)


def rope_tables():
    position = jnp.arange(SEQ_LEN).astype(F32)
    inverse = jnp.power(rope_base, -jnp.arange(HEAD_SIZE // 2).astype(F32) * (2.0 / HEAD_SIZE))
    angles = position[:, None] * inverse[None, :]
    cosine, sine = jnp.cos(angles), jnp.sin(angles)
    return (
        jnp.concatenate([cosine, cosine], axis=1),
        jnp.concatenate([-sine, sine], axis=1),
    )


def params(*semantics):
    return pltpu.CompilerParams(dimension_semantics=semantics, vmem_limit_bytes=VMEM_LIMIT)


def whole(shape):
    return pl.BlockSpec(shape, lambda *_: (0,) * len(shape), pipeline_mode=pl.Buffered(1))


def out_weight_spec(width, heads):
    return pl.BlockSpec((width, heads), lambda *_: (0, 2), pipeline_mode=pl.Buffered(1))


def project_kernel(x_ref, gain_ref, w_ref, qn_ref, kn_ref, cos_ref, sin_ref, at_ref, raw_ref, rot_ref):
    x = x_ref[...].astype(F32)
    scale = lax.rsqrt(jnp.mean(x * x, axis=-1, keepdims=True) + epsilon)
    a = (x * scale * gain_ref[...]).astype(BF16)
    at_ref[...] = a.T
    cosine, sine = cos_ref[...], sin_ref[...]
    for group in range(w_ref.shape[1] // GROUP):
        base = group * GROUP
        y = nn(a, w_ref[:, base : base + GROUP])
        raw_ref[:, base : base + GROUP] = y.astype(BF16)
        for head in range(3):
            z = y[:, head * HEAD_SIZE : (head + 1) * HEAD_SIZE]
            gain = kn_ref[...] * (SCORE_SCALE / LN2) if head == 2 else qn_ref[...]
            z = z * lax.rsqrt(jnp.mean(z * z, axis=-1, keepdims=True) + epsilon) * gain
            z = z * cosine + pltpu.roll(z, HEAD_SIZE // 2, 1) * sine
            rot_ref[:, base + head * HEAD_SIZE : base + (head + 1) * HEAD_SIZE] = z.astype(BF16)
        rot_ref[:, base + 3 * HEAD_SIZE : base + GROUP] = y[:, 3 * HEAD_SIZE :].astype(BF16)


def project(x, gain, weights, query_norm, key_norm, cosine, sine):
    tokens, width = x.shape
    columns = weights.shape[1] // 3 * 2
    rows = 256
    return pl.pallas_call(
        project_kernel,
        grid=(tokens // rows,),
        in_specs=[
            pl.BlockSpec((rows, width), lambda i: (i, 0)),
            whole((1, width)),
            whole((width, columns)),
            whole((1, HEAD_SIZE)),
            whole((1, HEAD_SIZE)),
            pl.BlockSpec((rows, HEAD_SIZE), lambda i: (i, 0)),
            pl.BlockSpec((rows, HEAD_SIZE), lambda i: (i, 0)),
        ],
        out_specs=[
            pl.BlockSpec((width, rows), lambda i: (0, i)),
            pl.BlockSpec((rows, columns), lambda i: (i, 0)),
            pl.BlockSpec((rows, columns), lambda i: (i, 0)),
        ],
        out_shape=[
            jax.ShapeDtypeStruct((width, tokens), BF16),
            jax.ShapeDtypeStruct((tokens, columns), BF16),
            jax.ShapeDtypeStruct((tokens, columns), BF16),
        ],
        compiler_params=params("arbitrary"),
        name="project",
    )(x, gain, weights, query_norm, key_norm, cosine, sine)


BLOCK = 512


def split_three(values):
    lane = lax.broadcasted_iota(jnp.int32, values.shape, 1)
    high = values.astype(BF16).astype(F32)
    rest = values - high
    middle = rest.astype(BF16).astype(F32)
    low = rest - middle
    return jnp.where(
        lane == 0, high, jnp.where(lane == 1, middle, jnp.where(lane == 2, low, 0.0))
    ).astype(BF16)


def attend_kernel(first, q_ref, k_ref, v_ref, out_ref, log_ref, v_ones, acc):
    i = pl.program_id(1)

    @pl.when(i == 0)
    def _():
        v_ones[:, :HEAD_SIZE] = v_ref[...]
        v_ones[:, HEAD_SIZE:] = jnp.ones(v_ref.shape, BF16)

    acc[...] = jnp.zeros_like(acc)

    def tile(start, masked):
        keys = k_ref[pl.ds(start, BLOCK), :]
        values = v_ones[pl.ds(start, BLOCK), :]
        for head in range(2):
            s = nt(q_ref[:, head * HEAD_SIZE : (head + 1) * HEAD_SIZE], keys)
            if masked:
                row = lax.broadcasted_iota(jnp.int32, s.shape, 0)
                column = lax.broadcasted_iota(jnp.int32, s.shape, 1)
                s = jnp.where(column <= row, s, masked_score)
            acc[head] += nn(jnp.exp2(s).astype(BF16), values)

    def step(j, carry):
        tile(pl.multiple_of(j * BLOCK, BLOCK), False)
        return carry

    lax.fori_loop(0, i + first, step, 0)
    tile(pl.multiple_of((i + first) * BLOCK, BLOCK), True)
    for head in range(2):
        columns = slice(head * HEAD_SIZE, (head + 1) * HEAD_SIZE)
        total = acc[head, :, HEAD_SIZE:]
        out_ref[:, columns] = (acc[head, :, :HEAD_SIZE] / total).astype(BF16)
        log_ref[:, columns] = split_three(jnp.log(total) * (-1.0 / LN2))


def attend(rot, half):
    groups = rot.shape[1] // GROUP
    width = 2 * HEAD_SIZE
    blocks = HALF // BLOCK
    first = half * blocks
    keys = HALF * (half + 1)
    return pl.pallas_call(
        lambda *refs: attend_kernel(first, *refs),
        grid=(groups, blocks),
        in_specs=[
            pl.BlockSpec((BLOCK, width), lambda c, i: (i + first, 2 * c)),
            pl.BlockSpec((keys, HEAD_SIZE), lambda c, i: (0, 4 * c + 2)),
            pl.BlockSpec((keys, HEAD_SIZE), lambda c, i: (0, 4 * c + 3)),
        ],
        out_specs=[
            pl.BlockSpec((BLOCK, width), lambda c, i: (i, c)),
            pl.BlockSpec((BLOCK, width), lambda c, i: (i, c)),
        ],
        out_shape=[
            jax.ShapeDtypeStruct((HALF, groups * width), BF16),
            jax.ShapeDtypeStruct((HALF, groups * width), BF16),
        ],
        scratch_shapes=[
            pltpu.VMEM((keys, width), BF16),
            pltpu.VMEM((2, BLOCK, width), F32),
        ],
        compiler_params=params("arbitrary", "arbitrary"),
        name="attend",
    )(rot, rot, rot)


def out_project_kernel(mixed_ref, w_ref, out_ref):
    out_ref[...] = nt(mixed_ref[...], w_ref[...]).astype(BF16)


def out_project(mixed, weights):
    rows = 256
    width, heads = weights.shape[0], mixed.shape[1]
    return pl.pallas_call(
        out_project_kernel,
        grid=(HALF // rows,),
        in_specs=[
            pl.BlockSpec((rows, heads), lambda i: (i, 0)),
            out_weight_spec(width, heads),
        ],
        out_specs=pl.BlockSpec((rows, width), lambda i: (i, 0)),
        out_shape=jax.ShapeDtypeStruct((HALF, width), BF16),
        compiler_params=params("arbitrary"),
        name="out_project",
    )(mixed, weights)


ROWS = 256


def attend_back_kernel(
    rot_ref, raw_ref, do_a, do_b, out_a, out_b, log_a, log_b, qn_ref, kn_ref, cos_ref, sin_ref,
    bits_ref, qg_ref, kg_ref,
    q_wide, d_wide, k_wide, v_wide, k_flip, dq_flip, dk, dv,
):
    blocks = SEQ_LEN // BLOCK
    lane = lax.broadcasted_iota(jnp.int32, (ROWS, HEAD_SIZE), 1)
    ones = jnp.where(lane < 3, 1.0, 0.0).astype(BF16)

    def prepare(half, do_ref, out_ref, log_ref):
        def body(r, carry):
            near = pl.ds(pl.multiple_of(r * ROWS, ROWS), ROWS)
            rows = pl.ds(pl.multiple_of(half * HALF + r * ROWS, ROWS), ROWS)
            key = rot_ref[rows, 2 * HEAD_SIZE : 3 * HEAD_SIZE]
            k_wide[rows, :HEAD_SIZE] = key
            k_wide[rows, HEAD_SIZE:] = ones
            v_wide[rows, :HEAD_SIZE] = rot_ref[rows, 3 * HEAD_SIZE :]
            v_wide[rows, HEAD_SIZE:] = ones
            k_flip[:, rows] = key.T
            for head in range(2):
                columns = slice(head * HEAD_SIZE, (head + 1) * HEAD_SIZE)
                q_wide[head, rows, :HEAD_SIZE] = rot_ref[rows, columns]
                q_wide[head, rows, HEAD_SIZE:] = log_ref[near, columns]
                grad = do_ref[near, columns]
                delta = jnp.sum(
                    grad.astype(F32) * out_ref[near, columns].astype(F32), axis=-1, keepdims=True
                )
                d_wide[head, rows, :HEAD_SIZE] = grad
                d_wide[head, rows, HEAD_SIZE:] = split_three(
                    jnp.broadcast_to(-delta, (ROWS, HEAD_SIZE))
                )
            return carry

        lax.fori_loop(0, HALF // ROWS, body, 0)

    prepare(0, do_a, out_a, log_a)
    prepare(1, do_b, out_b, log_b)
    dq_flip[...] = jnp.zeros_like(dq_flip)

    def tile(kv, start, masked, first):
        q_rows = pl.ds(start, BLOCK)
        for head in range(2):
            q = q_wide[head, q_rows, :]
            d = d_wide[head, q_rows, :]
            s = nt(k_wide[kv, :], q)
            if masked:
                row = lax.broadcasted_iota(jnp.int32, s.shape, 0)
                column = lax.broadcasted_iota(jnp.int32, s.shape, 1)
                s = jnp.where(row <= column, s, masked_score)
            p = jnp.exp2(s)
            ds = (p * nt(v_wide[kv, :], d)).astype(BF16)
            new_dv = nn(p.astype(BF16), d[:, :HEAD_SIZE])
            new_dk = nn(ds, q[:, :HEAD_SIZE])
            if first and head == 0:
                dv[kv, :] = new_dv
                dk[kv, :] = new_dk
            else:
                dv[kv, :] += new_dv
                dk[kv, :] += new_dk
            dq_flip[head, :, q_rows] += nn(k_flip[:, kv], ds)

    def key_block(j, carry):
        start = pl.multiple_of(j * BLOCK, BLOCK)
        kv = pl.ds(start, BLOCK)
        tile(kv, start, True, True)

        def query_block(i, inner):
            tile(kv, pl.multiple_of(i * BLOCK, BLOCK), False, False)
            return inner

        return lax.fori_loop(j + 1, blocks, query_block, carry)

    lax.fori_loop(0, blocks, key_block, 0)

    qg_ref[...] = jnp.zeros_like(qg_ref)
    kg_ref[...] = jnp.zeros_like(kg_ref)

    def finish(r, carry):
        rows = pl.ds(pl.multiple_of(r * ROWS, ROWS), ROWS)
        cosine, sine = cos_ref[rows, :], sin_ref[rows, :]
        for head in range(3):
            columns = slice(head * HEAD_SIZE, (head + 1) * HEAD_SIZE)
            if head < 2:
                u = dq_flip[head, :, rows].T * LN2
                gain, total = qn_ref[...], qg_ref
            else:
                u = dk[rows, :] * SCORE_SCALE
                gain, total = kn_ref[...], kg_ref
            u = u * cosine - pltpu.roll(u, HEAD_SIZE // 2, 1) * sine
            x = raw_ref[rows, columns].astype(F32)
            scale = lax.rsqrt(jnp.mean(x * x, axis=-1, keepdims=True) + epsilon)
            x = x * scale
            total[0] += jnp.sum((u * x).reshape(ROWS // 8, 8, HEAD_SIZE), axis=0)
            w = u * gain
            bits_ref[rows, columns] = (
                scale * (w - x * jnp.mean(w * x, axis=-1, keepdims=True))
            ).astype(BF16)
        bits_ref[rows, 3 * HEAD_SIZE :] = dv[rows, :].astype(BF16)
        return carry

    lax.fori_loop(0, SEQ_LEN // ROWS, finish, 0)


def attend_back(rot, raw, grads, outs, logs, query_norm, key_norm, cosine, sine):
    groups = rot.shape[1] // GROUP
    width = 2 * HEAD_SIZE
    return pl.pallas_call(
        attend_back_kernel,
        grid=(groups,),
        in_specs=[
            pl.BlockSpec((SEQ_LEN, GROUP), lambda c: (0, c)),
            pl.BlockSpec((SEQ_LEN, GROUP), lambda c: (0, c)),
            *[pl.BlockSpec((HALF, width), lambda c: (0, c))] * 6,
            whole((1, HEAD_SIZE)),
            whole((1, HEAD_SIZE)),
            whole((SEQ_LEN, HEAD_SIZE)),
            whole((SEQ_LEN, HEAD_SIZE)),
        ],
        out_specs=[
            pl.BlockSpec((SEQ_LEN, GROUP), lambda c: (0, c)),
            pl.BlockSpec((1, 8, HEAD_SIZE), lambda c: (c, 0, 0)),
            pl.BlockSpec((1, 8, HEAD_SIZE), lambda c: (c, 0, 0)),
        ],
        out_shape=[
            jax.ShapeDtypeStruct((SEQ_LEN, groups * GROUP), BF16),
            jax.ShapeDtypeStruct((groups, 8, HEAD_SIZE), F32),
            jax.ShapeDtypeStruct((groups, 8, HEAD_SIZE), F32),
        ],
        scratch_shapes=[
            pltpu.VMEM((2, SEQ_LEN, width), BF16),
            pltpu.VMEM((2, SEQ_LEN, width), BF16),
            pltpu.VMEM((SEQ_LEN, width), BF16),
            pltpu.VMEM((SEQ_LEN, width), BF16),
            pltpu.VMEM((HEAD_SIZE, SEQ_LEN), BF16),
            pltpu.VMEM((2, HEAD_SIZE, SEQ_LEN), F32),
            pltpu.VMEM((SEQ_LEN, HEAD_SIZE), F32),
            pltpu.VMEM((SEQ_LEN, HEAD_SIZE), F32),
        ],
        compiler_params=params("arbitrary"),
        name="attend_back",
    )(rot, raw, *grads, *outs, *logs, query_norm, key_norm, cosine, sine)


def residual_of(x_ref, own_ref, other_ref):
    residual = x_ref[...].astype(F32) + (own_ref[...].astype(F32) + other_ref[...].astype(F32))
    scale = lax.rsqrt(jnp.mean(residual * residual, axis=-1, keepdims=True) + epsilon)
    return residual * scale, scale


def middle_kernel(
    x_ref, own_ref, other_ref, grad_ref, fn_ref, w_ref, down_ref, flip_ref, y_ref, fg_ref
):
    width, columns = w_ref.shape
    hidden = columns // 3
    chunk = 512 if hidden % 512 == 0 else hidden
    rows = x_ref.shape[0]
    normed, scale = residual_of(x_ref, own_ref, other_ref)
    f = (normed * fn_ref[...]).astype(BF16)
    grad = grad_ref[...]
    flip_ref[0] = f.T
    flip_ref[1] = grad.T
    total = jnp.zeros((rows, width), F32)
    f_grad = jnp.zeros((rows, width), F32)
    for start in range(0, hidden, chunk):
        gate_w = w_ref[:, start : start + chunk]
        up_w = w_ref[:, hidden + start : hidden + start + chunk]
        down_w = w_ref[:, 2 * hidden + start : 2 * hidden + start + chunk]
        gate, up = nn(f, gate_w), nn(f, up_w)
        sig = 1.0 / (1.0 + jnp.exp(-gate))
        silu = gate * sig
        low = (silu * up).astype(BF16)
        total += nt(low, down_w)
        hidden_grad = nn(grad, down_w)
        gate_bits = (hidden_grad * up * (sig * (1.0 + gate * (1.0 - sig)))).astype(BF16)
        up_bits = (hidden_grad * silu).astype(BF16)
        y_ref[:, start : start + chunk] = gate_bits
        y_ref[:, hidden + start : hidden + start + chunk] = up_bits
        y_ref[:, 2 * hidden + start : 2 * hidden + start + chunk] = low
        f_grad += nt(gate_bits, gate_w) + nt(up_bits, up_w)
    down_ref[...] = total.astype(BF16)
    fg_ref[...] = f_grad.astype(BF16)


def half_rows(rows, width, half):
    return pl.BlockSpec((rows, width), lambda i: (i + half * (HALF // rows), 0))


def middle(half, x_all, own, other, grad_all, gain, weights):
    width, columns = weights.shape
    rows = 256
    near = pl.BlockSpec((rows, width), lambda i: (i, 0))
    return pl.pallas_call(
        middle_kernel,
        grid=(HALF // rows,),
        in_specs=[
            half_rows(rows, width, half), near, near, half_rows(rows, width, half),
            whole((1, width)), whole(weights.shape),
        ],
        out_specs=[
            near,
            pl.BlockSpec((2, width, rows), lambda i: (0, 0, i)),
            pl.BlockSpec((rows, columns), lambda i: (i, 0)),
            near,
        ],
        out_shape=[
            jax.ShapeDtypeStruct((HALF, width), BF16),
            jax.ShapeDtypeStruct((2, width, HALF), BF16),
            jax.ShapeDtypeStruct((HALF, columns), BF16),
            jax.ShapeDtypeStruct((HALF, width), BF16),
        ],
        compiler_params=params("arbitrary"),
        name="middle",
    )(x_all, own, other, grad_all, gain, weights)


def residual_back_kernel(
    x_ref, own_ref, other_ref, grad_ref, fg_ref, fg_other_ref, fn_ref, w_ref,
    rg_ref, flip_ref, mg_ref, fng_ref,
):
    rows, width = x_ref.shape
    normed, scale = residual_of(x_ref, own_ref, other_ref)
    f_grad = fg_ref[...].astype(F32) + fg_other_ref[...].astype(F32)

    @pl.when(pl.program_id(0) == 0)
    def _():
        fng_ref[...] = jnp.zeros_like(fng_ref)

    fng_ref[...] += jnp.sum((f_grad * normed).reshape(rows // 8, 8, width), axis=0)
    u = f_grad * fn_ref[...]
    residual_grad = grad_ref[...].astype(F32) + scale * (
        u - normed * jnp.mean(u * normed, axis=-1, keepdims=True)
    )
    rg_ref[...] = residual_grad
    proj = residual_grad.astype(BF16)
    flip_ref[...] = proj.T
    mg_ref[...] = nn(proj, w_ref[...]).astype(BF16)


def residual_back(half, x_all, own, other, grad_all, fg, fg_other, gain, weights, heads):
    width = weights.shape[0]
    rows = 256
    near = pl.BlockSpec((rows, width), lambda i: (i, 0))
    return pl.pallas_call(
        residual_back_kernel,
        grid=(HALF // rows,),
        in_specs=[
            half_rows(rows, width, half), near, near, half_rows(rows, width, half), near, near,
            whole((1, width)), out_weight_spec(width, heads),
        ],
        out_specs=[
            near,
            pl.BlockSpec((width, rows), lambda i: (0, i)),
            pl.BlockSpec((rows, heads), lambda i: (i, 0)),
            pl.BlockSpec((8, width), lambda i: (0, 0)),
        ],
        out_shape=[
            jax.ShapeDtypeStruct((HALF, width), F32),
            jax.ShapeDtypeStruct((width, HALF), BF16),
            jax.ShapeDtypeStruct((HALF, heads), BF16),
            jax.ShapeDtypeStruct((8, width), F32),
        ],
        compiler_params=params("arbitrary"),
        name="residual_back",
    )(x_all, own, other, grad_all, fg, fg_other, gain, weights)


def middle_weights_kernel(bound, flip_a, flip_b, y_a, y_b, out_ref):
    which = jnp.where(pl.program_id(0) < bound, 0, 1)
    out_ref[...] = (nn(flip_a[which], y_a[...]) + nn(flip_b[which], y_b[...])).astype(BF16)


def middle_weights(flips, ys):
    width = flips[0].shape[1]
    columns = ys[0].shape[1]
    hidden = columns // 3
    size = 512 if hidden % 512 == 0 else hidden
    bound = 2 * hidden // size
    y_spec = pl.BlockSpec((HALF, size), lambda i: (0, i))
    return pl.pallas_call(
        lambda *refs: middle_weights_kernel(bound, *refs),
        grid=(columns // size,),
        in_specs=[whole(flips[0].shape), whole(flips[1].shape), y_spec, y_spec],
        out_specs=pl.BlockSpec((width, size), lambda i: (0, i)),
        out_shape=jax.ShapeDtypeStruct((width, columns), BF16),
        compiler_params=params("arbitrary"),
        name="middle_weights",
    )(*flips, *ys)


def attention_weights_kernel(
    bound, input_flip, proj_a, proj_b, bits_ref, mixed_a, mixed_b, w_ref, out_ref, sums_ref
):
    i = pl.program_id(0)

    @pl.when(i == 0)
    def _():
        sums_ref[...] = jnp.zeros_like(sums_ref)

    @pl.when(i < bound)
    def _():
        out = nn(input_flip[...], bits_ref[...])
        out_ref[...] = out.astype(BF16)
        product = out * w_ref[...].astype(F32)
        for start in range(0, product.shape[1], 128):
            sums_ref[...] += product[:, start : start + 128]

    @pl.when(i >= bound)
    def _():
        out_ref[...] = (nn(proj_a[...], mixed_a[...]) + nn(proj_b[...], mixed_b[...])).astype(BF16)


def attention_weights(input_flip, projs, bits, mixed, weights):
    width, columns = weights.shape
    heads = columns // 3
    size = math.gcd(512, heads)
    bound = 2 * heads // size
    mixed_spec = pl.BlockSpec((HALF, size), lambda i: (0, jnp.maximum(i - bound, 0)))
    return pl.pallas_call(
        lambda *refs: attention_weights_kernel(bound, *refs),
        grid=(columns // size,),
        in_specs=[
            whole(input_flip.shape), whole(projs[0].shape), whole(projs[1].shape),
            pl.BlockSpec((SEQ_LEN, size), lambda i: (0, jnp.minimum(i, bound - 1))),
            mixed_spec, mixed_spec,
            pl.BlockSpec((width, size), lambda i: (0, i)),
        ],
        out_specs=[
            pl.BlockSpec((width, size), lambda i: (0, i)),
            pl.BlockSpec((width, 128), lambda i: (0, 0)),
        ],
        out_shape=[
            jax.ShapeDtypeStruct((width, columns), BF16),
            jax.ShapeDtypeStruct((width, 128), F32),
        ],
        compiler_params=params("arbitrary"),
        name="attention_weights",
    )(input_flip, *projs, bits, *mixed, weights)


def input_back_kernel(place_ref, bits_ref, w_ref, out_ref):
    out_ref[...] = nt(bits_ref[...], w_ref[...]).astype(BF16)


def input_back(place, tokens, bits, weights):
    width = weights.shape[0]
    columns = bits.shape[1]
    rows = 256
    blocks = tokens // rows
    return pl.pallas_call(
        input_back_kernel,
        grid_spec=pltpu.PrefetchScalarGridSpec(
            num_scalar_prefetch=1,
            grid=(blocks,),
            in_specs=[
                pl.BlockSpec((rows, columns), lambda i, place: (place[0] * blocks + i, 0)),
                whole((width, columns)),
            ],
            out_specs=pl.BlockSpec((rows, width), lambda i, place: (i, 0)),
        ),
        out_shape=jax.ShapeDtypeStruct((tokens, width), BF16),
        compiler_params=params("arbitrary"),
        name="input_back",
    )(place.reshape(1), bits, weights)


def swap(values):
    return lax.ppermute(values, "tensor", [(0, 1), (1, 0)])


def in_order(own, other, axis):
    first = lax.axis_index("tensor") == 0
    return jnp.concatenate(
        [jnp.where(first, own, other), jnp.where(first, other, own)], axis=axis
    )


def gather_tokens(values, ranks):
    if ranks == 2:
        return in_order(values, swap(values), 0)
    return lax.all_gather(values, "tensor", axis=0, tiled=True)


def others_sum(values, ranks):
    if ranks == 2:
        return swap(values)
    own = values.astype(F32)
    return (lax.psum(own, "tensor") - own).astype(BF16)


def own_rows(halves, ranks, me, rows):
    if ranks == 2:
        return jnp.where(me == 0, halves[0], halves[1])
    return lax.dynamic_slice_in_dim(jnp.concatenate(halves, axis=0), me * rows, rows)


def after(values, *events):
    return lax.optimization_barrier((values, *events))[0]


def on_device(
    layer_input,
    attention_norm,
    query_weight,
    key_matrix,
    value_matrix,
    query_norm,
    key_norm,
    output_weight,
    feedforward_norm,
    gate_weight,
    up_weight,
    down_weight,
    out_grad,
):
    ranks = lax.axis_size("tensor")
    me = lax.axis_index("tensor")
    depth = query_weight.shape[0]
    tok_rows, width = layer_input.shape
    groups = key_matrix.shape[1] // HEAD_SIZE
    heads = query_weight.shape[1]
    hidden = gate_weight.shape[1]

    own_attention = jnp.concatenate(
        [
            jnp.concatenate(
                [
                    query_weight.reshape(depth, groups, 2 * HEAD_SIZE),
                    key_matrix.reshape(depth, groups, HEAD_SIZE),
                    value_matrix.reshape(depth, groups, HEAD_SIZE),
                ],
                axis=2,
            ).reshape(depth, groups * GROUP),
            output_weight.T,
        ],
        axis=1,
    )
    attention_w = lax.all_gather(own_attention, "dp", axis=0, tiled=True)
    x_all = gather_tokens(layer_input, ranks)
    own_middle = jnp.concatenate([gate_weight, up_weight, down_weight.T], axis=1)
    middle_w = lax.all_gather(own_middle, "dp", axis=0, tiled=True)
    grad_all = gather_tokens(after(out_grad, x_all), ranks)

    cosine, sine = rope_tables()
    norm_q, norm_k = query_norm[None, :], key_norm[None, :]
    norm_two = feedforward_norm[None, :]
    input_flip, raw, rot = project(
        x_all, attention_norm[None, :], attention_w, norm_q, norm_k, cosine, sine
    )
    mixed, logs, owns, others = [], [], [], []
    for half in range(2):
        out, log = attend(after(rot, *owns), half)
        mixed.append(out)
        logs.append(log)
        owns.append(out_project(out, attention_w))
        others.append(others_sum(owns[half], ranks))

    downs, flips, ys, f_grads, f_others = [], [], [], [], []
    for half in range(2):
        down, flip, y, f_grad = middle(
            half, x_all, owns[half], others[half], grad_all, norm_two, middle_w
        )
        downs.append(down)
        flips.append(flip)
        ys.append(y)
        f_grads.append(f_grad)
        f_others.append(others_sum(f_grad, ranks))
    middle_part = middle_weights(flips, ys)
    middle_grad = lax.psum_scatter(
        middle_part, "dp", scatter_dimension=0, tiled=True
    ).astype(F32)

    f_others[1] = after(f_others[1], middle_part)

    residual_grads, projs, mixed_grads, norm_two_part = [], [], [], 0.0
    for half in range(2):
        residual_grad, proj, mixed_grad, part = residual_back(
            half, x_all, owns[half], others[half], grad_all, f_grads[half], f_others[half],
            norm_two, attention_w, heads,
        )
        residual_grads.append(residual_grad)
        projs.append(proj)
        mixed_grads.append(mixed_grad)
        norm_two_part = norm_two_part + jnp.sum(part, axis=0) / ranks

    bits, query_part, key_part = attend_back(
        rot, raw, mixed_grads, mixed, logs, norm_q, norm_k, cosine, sine
    )

    if ranks == 2:
        send = after(jnp.where(me == 0, downs[1], downs[0]), mixed_grads[1])
        down_sum = own_rows(downs, ranks, me, tok_rows).astype(F32) + swap(send).astype(F32)
    else:
        down_sum = lax.psum_scatter(
            jnp.concatenate(downs, axis=0).astype(F32), "tensor", scatter_dimension=0, tiled=True
        )
    x = layer_input.astype(F32)
    residual = x + (
        own_rows(owns, ranks, me, tok_rows).astype(F32)
        + own_rows(others, ranks, me, tok_rows).astype(F32)
    )
    layer_output = (residual + down_sum).astype(BF16)

    attention_part, sums = attention_weights(input_flip, projs, bits, mixed, attention_w)
    attention_grad = lax.psum_scatter(
        attention_part, "dp", scatter_dimension=0, tiled=True
    ).astype(F32)
    norm_one_part = jnp.sum(sums, axis=1) / attention_norm
    if ranks == 2:
        other = swap(input_back(1 - me, tok_rows, bits, attention_w))
        own = input_back(me, tok_rows, bits, attention_w)
        attention_input_grad = own.astype(F32) + other.astype(F32)
    else:
        attention_input_grad = lax.psum_scatter(
            input_back(jnp.zeros_like(me), SEQ_LEN, bits, attention_w).astype(F32),
            "tensor",
            scatter_dimension=0,
            tiled=True,
        )
    scale = lax.rsqrt(jnp.mean(x * x, axis=-1, keepdims=True) + epsilon)
    normed = x * scale
    u = attention_input_grad * attention_norm
    input_grad = own_rows(residual_grads, ranks, me, tok_rows) + scale * (
        u - normed * jnp.mean(u * normed, axis=-1, keepdims=True)
    )
    attention_norm_grad, feedforward_norm_grad, query_norm_grad, key_norm_grad = lax.psum(
        (
            norm_one_part,
            norm_two_part,
            jnp.sum(query_part, axis=(0, 1)),
            jnp.sum(key_part, axis=(0, 1)),
        ),
        ("dp", "tensor"),
    )
    qkv_grad = attention_grad[:, : groups * GROUP].reshape(depth, groups, GROUP)
    return (
        layer_output,
        input_grad,
        attention_norm_grad,
        qkv_grad[:, :, : 2 * HEAD_SIZE].reshape(depth, -1),
        qkv_grad[:, :, 2 * HEAD_SIZE : 3 * HEAD_SIZE].reshape(depth, -1),
        qkv_grad[:, :, 3 * HEAD_SIZE :].reshape(depth, -1),
        query_norm_grad,
        key_norm_grad,
        attention_grad[:, groups * GROUP :].T,
        feedforward_norm_grad,
        middle_grad[:, :hidden],
        middle_grad[:, hidden : 2 * hidden],
        middle_grad[:, 2 * hidden :].T,
    )


def solution(mesh):
    return jax.shard_map(
        on_device,
        mesh=mesh,
        in_specs=(
            P(("dp", "tensor"), None),
            P(),
            P("dp", "tensor"),
            P("dp", "tensor"),
            P("dp", "tensor"),
            P(),
            P(),
            P("tensor", "dp"),
            P(),
            P("dp", "tensor"),
            P("dp", "tensor"),
            P("tensor", "dp"),
            P(("dp", "tensor"), None),
        ),
        out_specs=(
            P(("dp", "tensor"), None),
            P(("dp", "tensor"), None),
            P(),
            P("dp", "tensor"),
            P("dp", "tensor"),
            P("dp", "tensor"),
            P(),
            P(),
            P("tensor", "dp"),
            P(),
            P("dp", "tensor"),
            P("dp", "tensor"),
            P("tensor", "dp"),
        ),
        check_vma=False,
    )
```

time: 1870 us -> 677 us (0.36)
  waiting for transfers between devices: 806 us -> 167 us
  matrix products: 612 us -> 0 us
  Pallas kernels: 0 us -> 317 us
  other arithmetic: 287 us -> 37.7 us
  local copies, waits for them, and re-layouts: 98.7 us -> 11 us
  blocking collectives: 40.1 us -> 111 us
    dot_general x49 -> x0, matrix products: 612 us -> none  [the longest x8 159 us: block_scores(): jnp.einsum('qcgd,kcd->cgqk', query_block, keys, preferred_element_type=jn...]
    all_gather x11 -> x2, waiting for transfers between devices: 387 us -> 3.17 us  [the longest x1 3.17 us: on_device(): attention_w = lax.all_gather(own_attention, 'dp', axis=0, tiled=True)]
    reduce_scatter x11 -> x2, waiting for transfers between devices: 414 us -> 43.5 us  [the longest x1 43.5 us: on_device(): lax.psum_scatter(middle_part, 'dp', scatter_dimension=0, tiled=True)]
    pallas_call x0 -> x14, Pallas kernels: none -> 317 us  [the longest x1 98.1 us: attend_back(): pl.pallas_call(attend_back_kernel, grid=(groups,), in_specs=[pl.BlockSpec...]
    convert_element_type x18 -> x3, other arithmetic: 143 us -> 1.27 us  [the longest x1 1.21 us: on_device(): middle_grad = lax.psum_scatter(middle_part, 'dp', scatter_dimension=0, ti...]
    ppermute x0 -> x8, waiting for transfers between devices: none -> 120 us  [swap(): return lax.ppermute(values, 'tensor', [(0, 1), (1, 0)])]
    reduce_sum x12 -> x7, other arithmetic: 85.8 us -> 4.38 us  [the longest x1 3.62 us: on_device(): jnp.mean(u * normed, axis=-1, keepdims=True)]
    psum x1, blocking collectives: 40.1 us -> 111 us  [on_device(): lax.psum((norm_one_part, norm_two_part, jnp.sum(query_part, axis=(0, 1)),...]
  transfers between devices with their start and end apart: 22 -> 12, of which waited for: 17 -> 6; matrix products, arithmetic and copies ran while one was open for 49% -> 6% of each run, Pallas kernels for 0% -> 28%
where the time goes in v1:
time: 677 us; the launch traced here: 671 us
  Pallas kernels  317 us (47%)
  waiting for transfers between devices  167 us (25%)
  blocking collectives  111 us (16%)
  other arithmetic  37.7 us (6%)
  between operations  14.5 us (2%)
  starting transfers between devices  12.3 us (2%)
  local copies, waits for them, and re-layouts  11 us (2%)
    ppermute x8, waiting for transfers between devices, swap(): return lax.ppermute(values, 'tensor', [(0, 1), (1, 0)])  120 us
    psum x1, blocking collectives, on_device(): lax.psum((norm_one_part, norm_two_part, jnp.sum(query_part, axis=(0, 1)),...  111 us
    pallas_call x1, Pallas kernels, attend_back(): pl.pallas_call(attend_back_kernel, grid=(groups,), in_specs=[pl.BlockSpec...  98.1 us
    pallas_call x2, Pallas kernels, middle(): pl.pallas_call(middle_kernel, grid=(HALF // rows,), in_specs=[half_rows(r...  60.6 us
    reduce_scatter x1, waiting for transfers between devices, on_device(): lax.psum_scatter(middle_part, 'dp', scatter_dimension=0, tiled=True)  43.5 us
    pallas_call x2, Pallas kernels, attend(): pl.pallas_call(lambda *refs: attend_kernel(first, *refs), grid=(groups, b...  41.1 us
    pallas_call x1, Pallas kernels, middle_weights(): pl.pallas_call(lambda *refs: middle_weights_kernel(bound, *refs), grid=(c...  26.2 us
    pallas_call x2, Pallas kernels, residual_back(): pl.pallas_call(residual_back_kernel, grid=(HALF // rows,), in_specs=[half...  22.4 us
  transfers between devices with their start and end apart: 12, of which 6 were waited for; matrix products, arithmetic and copies ran while one was open for 6% of the time, Pallas kernels for 28%

profile of v1, /device:TPU:0, one launch (start us, length us, event | category | flops | bytes accessed | tf_op | source)
XLA Modules:
  0.0 670.9 jit_solution(10708003195092267790)
XLA Ops:
  7.2 0.0 all-gather.3.cloned.1.call-start
  7.3 1.1 reshape.80
  8.3 0.9 reshape.81
  9.2 1.0 reshape.82
  10.2 0.1 pad_maximum_fusion.6
  10.4 1.7 pad_maximum_fusion.5
  12.1 0.0 all-gather.5.cloned.1.call-start
  12.2 0.9 pad_maximum_fusion.4
  13.1 0.0 reduce-scatter.3.cloned.1.call-start
  13.2 3.0 collective-permute-start
  16.2 45.7 %collective-permute-done = bf16[1024,1024]{1,0:T(8,128)(2,1)} collective-permute-done((bf16[1024,1024]{1,0:T(8,128)(2,1)S(1)}, bf16[1024,1024]{1,0:T(8,128)(2,1)}, u32[]{:S(2)}, u32[]{:S(2)}) %collective-permute-start) | collective-permute-done | bytes 2097184 | tf_op jit(solution)/shard_map/ppermute | solution.py:575
  61.9 1.9 broadcast_select_fusion.4
  63.8 2.5 pad_maximum_fusion.x_ref
  66.2 1.7 collective-permute-start.3
  68.0 3.7 fusion.9
  71.7 2.0 pad_maximum_fusion.2
  73.7 3.2 all-gather.3.cloned.1.call-done.w_ref.refs_6_
  76.8 17.6 %project.1 = (bf16[1024,2048]{1,0:T(8,128)(2,1)}, bf16[2048,2048]{1,0:T(8,128)(2,1)}, bf16[2048,2048]{1,0:T(8,128)(2,1)}) custom-call(bf16[2048,1024]{1,0:T(8,128)(2,1)} %pad_maximum_fusion.x_ref, f32[1,1024]{1,0:T(1,128)} %bitcast.38, bf16[1024,3072]{1,0:T(8,128)(2,1)} %all-gather.3.cloned.1.call-done.w_ref.refs_6_, f32[1,128]{1,0:T(1,128)} %bitcast.39, ...), custom_call_target="tpu_custom_call" | custom-call | tf_op jit(solution)/shard_map/project/pallas_call | solution.py:79
  94.4 13.7 %attend.2 = (bf16[1024,1024]{1,0:T(8,128)(2,1)}, bf16[1024,1024]{1,0:T(8,128)(2,1)}) custom-call(bf16[2048,2048]{1,0:T(8,128)(2,1)} %get-tuple-element.47.refs_0_.refs_1_.refs_2_.rot_ref, bf16[2048,2048]{1,0:T(8,128)(2,1)} %get-tuple-element.47.refs_0_.refs_1_.refs_2_.rot_ref, bf16[2048,2048]{1,0:T(8,128)(2,1)} %get-tuple-element.47.refs_0_.refs_1_.refs_2_.rot_ref), custom_call_target="tpu_custom_call" | custom-call | tf_op jit(solution)/shard_map/attend/pallas_call | solution.py:160
  108.1 6.1 out_project.2.own_ref
  114.2 27.4 %attend.3 = (bf16[1024,1024]{1,0:T(8,128)(2,1)}, bf16[1024,1024]{1,0:T(8,128)(2,1)}) custom-call(bf16[2048,2048]{1,0:T(8,128)(2,1)} %get-tuple-element.47.refs_0_.refs_1_.refs_2_.rot_ref, bf16[2048,2048]{1,0:T(8,128)(2,1)} %get-tuple-element.47.refs_0_.refs_1_.refs_2_.rot_ref, bf16[2048,2048]{1,0:T(8,128)(2,1)} %get-tuple-element.47.refs_0_.refs_1_.refs_2_.rot_ref), custom_call_target="tpu_custom_call" | custom-call | tf_op jit(solution)/shard_map/attend/pallas_call | solution.py:160
  141.6 6.4 out_project.3.own_ref
  148.0 1.6 collective-permute-start.2
  149.6 0.4 collective-permute-start.1
  150.0 2.5 broadcast_select_fusion.1
  152.6 2.5 pad_maximum_fusion.1.grad_ref
  155.1 41.7 %collective-permute-done.2.other_ref = bf16[1024,1024]{1,0:T(8,128)(2,1)} collective-permute-done((bf16[1024,1024]{1,0:T(8,128)(2,1)}, bf16[1024,1024]{1,0:T(8,128)(2,1)}, u32[]{:S(2)}, u32[]{:S(2)}) %collective-permute-start.2) | collective-permute-done | bytes 2097184 | tf_op jit(solution)/shard_map/ppermute | solution.py:575
  196.8 30.5 %middle.3 = (bf16[1024,1024]{1,0:T(8,128)(2,1)}, bf16[2,1024,1024]{2,1,0:T(8,128)(2,1)}, bf16[1024,4608]{1,0:T(8,128)(2,1)}, bf16[1024,1024]{1,0:T(8,128)(2,1)}) custom-call(bf16[2048,1024]{1,0:T(8,128)(2,1)} %pad_maximum_fusion.x_ref, bf16[1024,1024]{1,0:T(8,128)(2,1)} %out_project.3.own_ref, bf16[1024,1024]{1,0:T(8,128)(2,1)} %collective-permute-done.2.other_ref, ...), custom_call_target="tpu_custom_call" | custom-call | tf_op jit(solution)/shard_map/middle/pallas_call | solution.py:400
  227.3 1.6 collective-permute-start.4
  228.9 12.8 %collective-permute-done.1.other_ref = bf16[1024,1024]{1,0:T(8,128)(2,1)} collective-permute-done((bf16[1024,1024]{1,0:T(8,128)(2,1)S(1)}, bf16[1024,1024]{1,0:T(8,128)(2,1)}, u32[]{:S(2)}, u32[]{:S(2)}) %collective-permute-start.1) | collective-permute-done | bytes 2097184 | tf_op jit(solution)/shard_map/ppermute | solution.py:575
  241.7 30.1 %middle.2 = (bf16[1024,1024]{1,0:T(8,128)(2,1)}, bf16[2,1024,1024]{2,1,0:T(8,128)(2,1)}, bf16[1024,4608]{1,0:T(8,128)(2,1)}, bf16[1024,1024]{1,0:T(8,128)(2,1)}) custom-call(bf16[2048,1024]{1,0:T(8,128)(2,1)} %pad_maximum_fusion.x_ref, bf16[1024,1024]{1,0:T(8,128)(2,1)} %out_project.2.own_ref, bf16[1024,1024]{1,0:T(8,128)(2,1)} %collective-permute-done.1.other_ref, ...), custom_call_target="tpu_custom_call" | custom-call | tf_op jit(solution)/shard_map/middle/pallas_call | solution.py:400
  271.9 1.6 collective-permute-start.6
  273.5 26.2 %middle_weights.1 = bf16[1024,4608]{1,0:T(8,128)(2,1)} custom-call(bf16[2,1024,1024]{2,1,0:T(8,128)(2,1)} %get-tuple-element.53.refs_0_, bf16[2,1024,1024]{2,1,0:T(8,128)(2,1)} %get-tuple-element.54.refs_1_, bf16[1024,4608]{1,0:T(8,128)(2,1)} %get-tuple-element.55.refs_2_, bf16[1024,4608]{1,0:T(8,128)(2,1)} %get-tuple-element.56.refs_3_), custom_call_target="tpu_custom_call" | custom-call | tf_op jit(solution)/shard_map/middle_weights/pallas_call | solution.py:487
  299.7 11.7 %residual_back.2 = (f32[1024,1024]{1,0:T(8,128)}, bf16[1024,1024]{1,0:T(8,128)(2,1)}, bf16[1024,1024]{1,0:T(8,128)(2,1)}, f32[8,1024]{1,0:T(8,128)}) custom-call(bf16[2048,1024]{1,0:T(8,128)(2,1)} %pad_maximum_fusion.x_ref, bf16[1024,1024]{1,0:T(8,128)(2,1)} %out_project.3.own_ref, bf16[1024,1024]{1,0:T(8,128)(2,1)} %collective-permute-done.2.other_ref, ...), custom_call_target="tpu_custom_call" | custom-call | tf_op jit(solution)/shard_map/residual_back/pallas_call | solution.py:451
  311.4 19.4 %collective-permute-done.6.fg_other_ref = bf16[1024,1024]{1,0:T(8,128)(2,1)S(1)} collective-permute-done((bf16[1024,1024]{1,0:T(8,128)(2,1)}, bf16[1024,1024]{1,0:T(8,128)(2,1)S(1)}, u32[]{:S(2)}, u32[]{:S(2)}) %collective-permute-start.6) | collective-permute-done | bytes 2097184 | tf_op jit(solution)/shard_map/ppermute | solution.py:575
  330.7 1.4 copy-done.8
  332.1 10.7 %residual_back.3 = (f32[1024,1024]{1,0:T(8,128)}, bf16[1024,1024]{1,0:T(8,128)(2,1)}, bf16[1024,1024]{1,0:T(8,128)(2,1)}, f32[8,1024]{1,0:T(8,128)}) custom-call(bf16[2048,1024]{1,0:T(8,128)(2,1)} %pad_maximum_fusion.x_ref, bf16[1024,1024]{1,0:T(8,128)(2,1)} %out_project.2.own_ref, bf16[1024,1024]{1,0:T(8,128)(2,1)} %collective-permute-done.1.other_ref, ...), custom_call_target="tpu_custom_call" | custom-call | tf_op jit(solution)/shard_map/residual_back/pallas_call | solution.py:451
  342.8 98.1 %attend_back.1 = (bf16[2048,2048]{1,0:T(8,128)(2,1)}, f32[4,8,128]{2,1,0:T(8,128)}, f32[4,8,128]{2,1,0:T(8,128)}) custom-call(bf16[2048,2048]{1,0:T(8,128)(2,1)} %get-tuple-element.47.refs_0_.refs_1_.refs_2_.rot_ref, bf16[2048,2048]{1,0:T(8,128)(2,1)} %get-tuple-element.63.raw_ref, bf16[1024,1024]{1,0:T(8,128)(2,1)} %get-tuple-element.64.do_a, ...), custom_call_target="tpu_custom_call" | custom-call | tf_op jit(solution)/shard_map/attend_back/pallas_call | solution.py:315
  440.9 20.5 %attention_weights.1 = (bf16[1024,3072]{1,0:T(8,128)(2,1)}, f32[1024,128]{1,0:T(8,128)}) custom-call(bf16[1024,2048]{1,0:T(8,128)(2,1)} %get-tuple-element.68.refs_0_, bf16[1024,1024]{1,0:T(8,128)(2,1)} %get-tuple-element.69.refs_1_, bf16[1024,1024]{1,0:T(8,128)(2,1)} %get-tuple-element.70.refs_2_, bf16[2048,2048]{1,0:T(8,128)(2,1)} %get-tuple-element.67.bits_ref.refs_3_, ...), custom_call_target="tpu_custom_call" | custom-call | tf_op jit(solution)/shard_map/attention_weights/pallas_call | solution.py:526
  461.5 0.0 reduce-scatter.5.cloned.1.call-start
  461.5 0.5 reduce-scatter.5.cloned.1.call-update
  462.1 9.0 %input_back.3 = bf16[1024,1024]{1,0:T(8,128)(2,1)} custom-call(s32[1]{0:T(128)} %bitcast.7.place_ref, bf16[2048,2048]{1,0:T(8,128)(2,1)} %get-tuple-element.67.bits_ref.refs_3_, bf16[1024,3072]{1,0:T(8,128)(2,1)} %all-gather.3.cloned.1.call-done.w_ref.refs_6_), custom_call_target="tpu_custom_call" | custom-call | tf_op jit(solution)/shard_map/input_back/pallas_call | solution.py:557
  471.1 1.6 collective-permute-start.7
  472.7 3.4 broadcast_select_fusion.2
  476.2 0.5 collective-permute-start.5
  476.6 0.5 fusion.8
  477.2 0.1 copy-done.9
  477.2 0.2 reduce_sum.65
  477.5 9.0 %input_back.2 = bf16[1024,1024]{1,0:T(8,128)(2,1)} custom-call(s32[1]{0:T(128)} %bitcast.6.place_ref, bf16[2048,2048]{1,0:T(8,128)(2,1)} %get-tuple-element.67.bits_ref.refs_3_, bf16[1024,3072]{1,0:T(8,128)(2,1)} %all-gather.3.cloned.1.call-done.w_ref.refs_6_), custom_call_target="tpu_custom_call" | custom-call | tf_op jit(solution)/shard_map/input_back/pallas_call | solution.py:557
  486.6 111.5 %all-reduce = (f32[1024]{0:T(1024)}, f32[128]{0:T(128)}, f32[128]{0:T(128)}, f32[1024]{0:T(1024)}) all-reduce(f32[1024]{0:T(1024)S(1)} %div.15, f32[128]{0:T(128)S(1)} %reduce_sum.66, f32[128]{0:T(128)S(1)} %reduce_sum.67, f32[1024]{0:T(1024)S(1)} %add_multiply_fusion.1), channel_id=1, replica_groups=mesh['dp'=16,'tensor'=2] {'dp','tensor'}, use_global_device_ids=true, to_apply=%region_3.4 | all-reduce | flops 2304 | bytes 18432 | tf_op jit(solution)/shard_map/psum | solution.py:733
  598.1 3.6 fusion.2
  601.7 0.5 copy-done.5
  602.2 10.9 %fusion.5 = (f32[1024,1024]{1,0:T(8,128)}, bf16[1024,1024]{1,0:T(8,128)(2,1)}) fusion(bf16[1024,1024]{1,0:T(8,128)(2,1)S(1)} %copy-done.4, f32[1024,1024]{1,0:T(8,128)} %get-tuple-element.61, f32[1024,1024]{1,0:T(8,128)} %get-tuple-element.62, bf16[1024,1024]{1,0:T(8,128)(2,1)} %collective-permute-done.7, bf16[1024,1024]{1,0:T(8,128)(2,1)S(1)} %copy-done.5, ...), kind=kLoop, calls=%fused_computation.8 | loop fusion | flops 24117248 | bytes 35663872 | tf_op jit(solution)/shard_map/add | solution.py:730
  613.1 1.1 slice.32
  614.2 0.4 reshape.86
  614.6 0.8 copy.27
  615.4 0.7 copy.32
  616.0 0.7 copy.33
  616.7 0.1 convert_element_type.66
  616.8 0.7 slice_bitcast_fusion.1
  617.5 43.5 %reduce-scatter.5.cloned.1.call-done = bf16[64,4608]{1,0:T(8,128)(2,1)} async-done(((bf16[1024,4608]{1,0:T(8,128)(2,1)}), bf16[64,4608]{1,0:T(8,128)(2,1)}) %reduce-scatter.5.cloned.1.call-update) | async-done | bytes 589840 | tf_op jit(solution)/shard_map/reduce_scatter | solution.py:676
  661.0 1.2 convert_element_type.67
  662.2 0.8 slice_bitcast_fusion
  663.0 1.0 fusion.10
  (55 shorter events, 0.4 us)
Async XLA Ops:
  7.2 5.0 copy-start.10
  7.2 5.0 copy-start.12
  7.2 5.0 copy-start.11
  7.2 69.6 %all-gather.3.cloned.1.call-start = ((), (), s32[]{:S(2)}) async-start(), calls=%async_computation.2 | async-start | bytes 6684672 | tf_op jit(solution)/shard_map/all_gather | solution.py:645
  9.2 4.0 copy-start.3
  12.1 184.7 %all-gather.5.cloned.1.call-start = ((), (), s32[]{:S(2)}) async-start(), calls=%async_computation.3 | async-start | bytes 10027008 | tf_op jit(solution)/shard_map/all_gather | solution.py:648
  13.1 600.0 %reduce-scatter.3.cloned.1.call-start = ((), (), s32[]{:S(2)}) async-start(), calls=%async_computation.4 | async-start | bytes 6684672 | tf_op jit(solution)/shard_map/reduce_scatter | solution.py:712
  13.2 48.7 %collective-permute-start = (bf16[1024,1024]{1,0:T(8,128)(2,1)S(1)}, bf16[1024,1024]{1,0:T(8,128)(2,1)}, u32[]{:S(2)}, u32[]{:S(2)}) collective-permute-start(bf16[1024,1024]{1,0:T(8,128)(2,1)S(1)} %copy-done.3), channel_id=1, source_target_pairs={{0,1},{1,0},{2,3},{3,2},{4,5},{5,4},{6,7},{7,6},{8,9},{9,8},{10,11... | collective-permute-start | bytes 6291464 | tf_op jit(solution)/shard_map/ppermute | solution.py:575
  66.2 83.8 %collective-permute-start.3 = (bf16[1024,1024]{1,0:T(8,128)(2,1)}, bf16[1024,1024]{1,0:T(8,128)(2,1)}, u32[]{:S(2)}, u32[]{:S(2)}) collective-permute-start(bf16[1024,1024]{1,0:T(8,128)(2,1)} %param.25), channel_id=1, source_target_pairs={{0,1},{1,0},{2,3},{3,2},{4,5},{5,4},{6,7},{7,6},{8,9},{9,8},{10,11... | collective-permute-start | bytes 6291464 | tf_op jit(solution)/shard_map/ppermute | solution.py:575
  141.6 8.1 %copy-start = (bf16[1024,1024]{1,0:T(8,128)(2,1)S(1)}, bf16[1024,1024]{1,0:T(8,128)(2,1)}, u32[]{:S(2)}) copy-start(bf16[1024,1024]{1,0:T(8,128)(2,1)} %out_project.2.own_ref) | copy-start | bytes 6291460
  148.0 48.8 %collective-permute-start.2 = (bf16[1024,1024]{1,0:T(8,128)(2,1)}, bf16[1024,1024]{1,0:T(8,128)(2,1)}, u32[]{:S(2)}, u32[]{:S(2)}) collective-permute-start(bf16[1024,1024]{1,0:T(8,128)(2,1)} %out_project.3.own_ref), channel_id=1, source_target_pairs={{0,1},{1,0},{2,3},{3,2},{4,5},{5,4},{6,7},{7,6},{8,9},{9,8},{10,11... | collective-permute-start | bytes 6291464 | tf_op jit(solution)/shard_map/ppermute | solution.py:575
  149.6 92.1 %collective-permute-start.1 = (bf16[1024,1024]{1,0:T(8,128)(2,1)S(1)}, bf16[1024,1024]{1,0:T(8,128)(2,1)}, u32[]{:S(2)}, u32[]{:S(2)}) collective-permute-start(bf16[1024,1024]{1,0:T(8,128)(2,1)S(1)} %copy-done), channel_id=1, source_target_pairs={{0,1},{1,0},{2,3},{3,2},{4,5},{5,4},{6,7},{7,6},{8,9},{9,8},{10,11... | collective-permute-start | bytes 6291464 | tf_op jit(solution)/shard_map/ppermute | solution.py:575
  227.3 72.4 %collective-permute-start.4 = (bf16[1024,1024]{1,0:T(8,128)(2,1)}, bf16[1024,1024]{1,0:T(8,128)(2,1)}, u32[]{:S(2)}, u32[]{:S(2)}) collective-permute-start(bf16[1024,1024]{1,0:T(8,128)(2,1)} %get-tuple-element.52.fg_ref), channel_id=1, source_target_pairs={{0,1},{1,0},{2,3},{3,2},{4,5},{5,4},{6,7},{7,6},{8,9},{9,8},{10,11... | collective-permute-start | bytes 6291464 | tf_op jit(solution)/shard_map/ppermute | solution.py:575
  271.9 58.9 %collective-permute-start.6 = (bf16[1024,1024]{1,0:T(8,128)(2,1)}, bf16[1024,1024]{1,0:T(8,128)(2,1)S(1)}, u32[]{:S(2)}, u32[]{:S(2)}) collective-permute-start(bf16[1024,1024]{1,0:T(8,128)(2,1)} %get-tuple-element.60.fg_ref), channel_id=1, source_target_pairs={{0,1},{1,0},{2,3},{3,2},{4,5},{5,4},{6,7},{7,6},{8,9},{9,8},{10,11... | collective-permute-start | bytes 6291464 | tf_op jit(solution)/shard_map/ppermute | solution.py:575
  330.7 1.4 copy-start.8
  461.5 199.5 %reduce-scatter.5.cloned.1.call-start = ((), (), s32[]{:S(2)}) async-start(), calls=%async_computation.5 | async-start | bytes 10027008 | tf_op jit(solution)/shard_map/reduce_scatter | solution.py:676
  471.1 127.0 %collective-permute-start.7 = (bf16[1024,1024]{1,0:T(8,128)(2,1)}, bf16[1024,1024]{1,0:T(8,128)(2,1)}, u32[]{:S(2)}, u32[]{:S(2)}) collective-permute-start(bf16[1024,1024]{1,0:T(8,128)(2,1)} %input_back.3), channel_id=1, source_target_pairs={{0,1},{1,0},{2,3},{3,2},{4,5},{5,4},{6,7},{7,6},{8,9},{9,8},{10,11... | collective-permute-start | bytes 6291464 | tf_op jit(solution)/shard_map/ppermute | solution.py:575
  472.7 3.9 copy-start.4
  476.1 1.0 copy-start.14
  476.1 1.0 copy-start.15
  476.1 1.1 copy-start.9
  476.1 1.3 copy-start.13
  476.1 1.3 copy-start.17
  476.2 1.4 copy-start.16
  476.2 125.5 %collective-permute-start.5 = (bf16[1024,1024]{1,0:T(8,128)(2,1)}, bf16[1024,1024]{1,0:T(8,128)(2,1)}, u32[]{:S(2)}, u32[]{:S(2)}) collective-permute-start(bf16[1024,1024]{1,0:T(8,128)(2,1)} %broadcast_select_fusion.2), channel_id=1, source_target_pairs={{0,1},{1,0},{2,3},{3,2},{4,5},{5,4},{6,7},{7,6},{8,9},{9,8},{10,11... | collective-permute-start | bytes 6291464 | tf_op jit(solution)/shard_map/ppermute | solution.py:575
  598.1 3.7 copy-start.1
  598.1 3.7 copy-start.2
  598.1 4.2 copy-start.5
  613.1 3.6 copy-start.7
  661.0 2.0 copy-start.6
Sparse Core Ops, SparseCore 0:
  12.3 64.5 all-gather.2
  79.1 80.0 all-gather.4
  461.6 84.2 reduce-scatter.2
  550.4 110.5 reduce-scatter.4

commit v2 on v1

--- a/solution.py
+++ b/solution.py
@@ -43,6 +43,10 @@
 
 def params(*semantics):
     return pltpu.CompilerParams(dimension_semantics=semantics, vmem_limit_bytes=VMEM_LIMIT)
+
+
+def cost(flops, rate):
+    return pl.CostEstimate(flops=int(flops * (1000.0 / rate)), bytes_accessed=0, transcendentals=0)
 
 
 def whole(shape):
@@ -99,6 +103,7 @@
             jax.ShapeDtypeStruct((tokens, columns), BF16),
         ],
         compiler_params=params("arbitrary"),
+        cost_estimate=cost(2 * tokens * width * columns, 500),
         name="project",
     )(x, gain, weights, query_norm, key_norm, cosine, sine)
 
@@ -127,23 +132,25 @@
 
     acc[...] = jnp.zeros_like(acc)
 
-    def tile(start, masked):
-        keys = k_ref[pl.ds(start, BLOCK), :]
-        values = v_ones[pl.ds(start, BLOCK), :]
+    def tile(row, rows, start, size, masked):
+        keys = k_ref[pl.ds(start, size), :]
+        values = v_ones[pl.ds(start, size), :]
         for head in range(2):
-            s = nt(q_ref[:, head * HEAD_SIZE : (head + 1) * HEAD_SIZE], keys)
+            s = nt(q_ref[row : row + rows, head * HEAD_SIZE : (head + 1) * HEAD_SIZE], keys)
             if masked:
-                row = lax.broadcasted_iota(jnp.int32, s.shape, 0)
-                column = lax.broadcasted_iota(jnp.int32, s.shape, 1)
-                s = jnp.where(column <= row, s, masked_score)
-            acc[head] += nn(jnp.exp2(s).astype(BF16), values)
+                query = lax.broadcasted_iota(jnp.int32, s.shape, 0)
+                key = lax.broadcasted_iota(jnp.int32, s.shape, 1)
+                s = jnp.where(key <= query + (size - rows), s, masked_score)
+            acc[head, row : row + rows] += nn(jnp.exp2(s).astype(BF16), values)
 
     def step(j, carry):
-        tile(pl.multiple_of(j * BLOCK, BLOCK), False)
+        tile(0, BLOCK, pl.multiple_of(j * BLOCK, BLOCK), BLOCK, False)
         return carry
 
     lax.fori_loop(0, i + first, step, 0)
-    tile(pl.multiple_of((i + first) * BLOCK, BLOCK), True)
+    start = pl.multiple_of((i + first) * BLOCK, BLOCK)
+    tile(0, BLOCK // 2, start, BLOCK // 2, True)
+    tile(BLOCK // 2, BLOCK // 2, start, BLOCK, True)
     for head in range(2):
         columns = slice(head * HEAD_SIZE, (head + 1) * HEAD_SIZE)
         total = acc[head, :, HEAD_SIZE:]
@@ -178,6 +185,7 @@
             pltpu.VMEM((2, BLOCK, width), F32),
         ],
         compiler_params=params("arbitrary", "arbitrary"),
+        cost_estimate=cost(4 * HALF * keys * groups * width, 500),
         name="attend",
     )(rot, rot, rot)
 
@@ -199,6 +207,7 @@
         out_specs=pl.BlockSpec((rows, width), lambda i: (i, 0)),
         out_shape=jax.ShapeDtypeStruct((HALF, width), BF16),
         compiler_params=params("arbitrary"),
+        cost_estimate=cost(2 * HALF * width * heads, 350),
         name="out_project",
     )(mixed, weights)
 
@@ -245,8 +254,8 @@
     prepare(1, do_b, out_b, log_b)
     dq_flip[...] = jnp.zeros_like(dq_flip)
 
-    def tile(kv, start, masked, first):
-        q_rows = pl.ds(start, BLOCK)
+    def tile(kv_start, kv_size, start, size, masked):
+        kv, q_rows = pl.ds(kv_start, kv_size), pl.ds(start, size)
         for head in range(2):
             q = q_wide[head, q_rows, :]
             d = d_wide[head, q_rows, :]
@@ -259,7 +268,7 @@
             ds = (p * nt(v_wide[kv, :], d)).astype(BF16)
             new_dv = nn(p.astype(BF16), d[:, :HEAD_SIZE])
             new_dk = nn(ds, q[:, :HEAD_SIZE])
-            if first and head == 0:
+            if masked and head == 0:
                 dv[kv, :] = new_dv
                 dk[kv, :] = new_dk
             else:
@@ -267,13 +276,16 @@
                 dk[kv, :] += new_dk
             dq_flip[head, :, q_rows] += nn(k_flip[:, kv], ds)
 
+    part = BLOCK // 2
+
     def key_block(j, carry):
         start = pl.multiple_of(j * BLOCK, BLOCK)
-        kv = pl.ds(start, BLOCK)
-        tile(kv, start, True, True)
+        later = pl.multiple_of(j * BLOCK + part, part)
+        tile(start, part, start, BLOCK, True)
+        tile(later, part, later, part, True)
 
         def query_block(i, inner):
-            tile(kv, pl.multiple_of(i * BLOCK, BLOCK), False, False)
+            tile(start, BLOCK, pl.multiple_of(i * BLOCK, BLOCK), BLOCK, False)
             return inner
 
         return lax.fori_loop(j + 1, blocks, query_block, carry)
@@ -345,6 +357,7 @@
             pltpu.VMEM((SEQ_LEN, HEAD_SIZE), F32),
         ],
         compiler_params=params("arbitrary"),
+        cost_estimate=cost(5 * SEQ_LEN * SEQ_LEN * groups * width, 80),
         name="attend_back",
     )(rot, raw, *grads, *outs, *logs, query_norm, key_norm, cosine, sine)
 
@@ -417,6 +430,7 @@
             jax.ShapeDtypeStruct((HALF, width), BF16),
         ],
         compiler_params=params("arbitrary"),
+        cost_estimate=cost(4 * HALF * width * columns, 2500),
         name="middle",
     )(x_all, own, other, grad_all, gain, weights)
 
@@ -468,31 +482,38 @@
             jax.ShapeDtypeStruct((8, width), F32),
         ],
         compiler_params=params("arbitrary"),
+        cost_estimate=cost(2 * HALF * width * heads, 190),
         name="residual_back",
     )(x_all, own, other, grad_all, fg, fg_other, gain, weights)
 
 
-def middle_weights_kernel(bound, flip_a, flip_b, y_a, y_b, out_ref):
-    which = jnp.where(pl.program_id(0) < bound, 0, 1)
-    out_ref[...] = (nn(flip_a[which], y_a[...]) + nn(flip_b[which], y_b[...])).astype(BF16)
-
-
-def middle_weights(flips, ys):
+def middle_weights_kernel(which, flip_a, flip_b, y_a, y_b, *rest):
+    rest[-1][...] = (nn(flip_a[which], y_a[...]) + nn(flip_b[which], y_b[...])).astype(BF16)
+
+
+def middle_weights(flips, ys, down, *partial):
     width = flips[0].shape[1]
     columns = ys[0].shape[1]
     hidden = columns // 3
     size = 512 if hidden % 512 == 0 else hidden
     bound = 2 * hidden // size
-    y_spec = pl.BlockSpec((HALF, size), lambda i: (0, i))
+    first, blocks = (bound, columns // size - bound) if down else (0, bound)
+    which = 1 if down else 0
+    spec = pl.BlockSpec((HALF, size), lambda i: (0, i + first))
+    flip_spec = pl.BlockSpec(
+        (1, width, HALF), lambda i: (which, 0, 0), pipeline_mode=pl.Buffered(1)
+    )
     return pl.pallas_call(
-        lambda *refs: middle_weights_kernel(bound, *refs),
-        grid=(columns // size,),
-        in_specs=[whole(flips[0].shape), whole(flips[1].shape), y_spec, y_spec],
-        out_specs=pl.BlockSpec((width, size), lambda i: (0, i)),
+        lambda *refs: middle_weights_kernel(0, *refs),
+        grid=(blocks,),
+        in_specs=[flip_spec, flip_spec, spec, spec] + [pl.BlockSpec(memory_space=pl.ANY)] * len(partial),
+        out_specs=pl.BlockSpec((width, size), lambda i: (0, i + first)),
         out_shape=jax.ShapeDtypeStruct((width, columns), BF16),
+        input_output_aliases={4: 0} if partial else {},
         compiler_params=params("arbitrary"),
-        name="middle_weights",
-    )(*flips, *ys)
+        cost_estimate=cost(2 * SEQ_LEN * width * size * blocks, 3000),
+        name="down_weights" if down else "gate_up_weights",
+    )(*flips, *ys, *partial)
 
 
 def attention_weights_kernel(
@@ -541,6 +562,7 @@
             jax.ShapeDtypeStruct((width, 128), F32),
         ],
         compiler_params=params("arbitrary"),
+        cost_estimate=cost(2 * SEQ_LEN * width * columns, 640),
         name="attention_weights",
     )(input_flip, *projs, bits, *mixed, weights)
 
@@ -567,6 +589,7 @@
         ),
         out_shape=jax.ShapeDtypeStruct((tokens, width), BF16),
         compiler_params=params("arbitrary"),
+        cost_estimate=cost(2 * tokens * width * columns, 480),
         name="input_back",
     )(place.reshape(1), bits, weights)
 
@@ -582,10 +605,14 @@
     )
 
 
-def gather_tokens(values, ranks):
+def send_tokens(values, ranks):
     if ranks == 2:
-        return in_order(values, swap(values), 0)
+        return swap(values)
     return lax.all_gather(values, "tensor", axis=0, tiled=True)
+
+
+def all_tokens(own, sent, ranks):
+    return in_order(own, sent, 0) if ranks == 2 else sent
 
 
 def others_sum(values, ranks):
@@ -599,6 +626,17 @@
     if ranks == 2:
         return jnp.where(me == 0, halves[0], halves[1])
     return lax.dynamic_slice_in_dim(jnp.concatenate(halves, axis=0), me * rows, rows)
+
+
+def sum_over_all(values, devices):
+    if devices & (devices - 1):
+        return lax.psum(values, ("dp", "tensor"))
+    step = 1
+    while step < devices:
+        pairs = [(device, device ^ step) for device in range(devices)]
+        values = values + lax.ppermute(values, ("dp", "tensor"), pairs)
+        step *= 2
+    return values
 
 
 def after(values, *events):
@@ -643,10 +681,10 @@
         axis=1,
     )
     attention_w = lax.all_gather(own_attention, "dp", axis=0, tiled=True)
-    x_all = gather_tokens(layer_input, ranks)
+    x_all = all_tokens(layer_input, send_tokens(layer_input, ranks), ranks)
     own_middle = jnp.concatenate([gate_weight, up_weight, down_weight.T], axis=1)
     middle_w = lax.all_gather(own_middle, "dp", axis=0, tiled=True)
-    grad_all = gather_tokens(after(out_grad, x_all), ranks)
+    grad_sent = send_tokens(after(out_grad, x_all), ranks)
 
     cosine, sine = rope_tables()
     norm_q, norm_k = query_norm[None, :], key_norm[None, :]
@@ -660,29 +698,33 @@
         mixed.append(out)
         logs.append(log)
         owns.append(out_project(out, attention_w))
-        others.append(others_sum(owns[half], ranks))
+        others.append(others_sum(after(owns[half], *others), ranks))
+
+    grad_all = all_tokens(after(out_grad, owns[0]), grad_sent, ranks)
 
     downs, flips, ys, f_grads, f_others = [], [], [], [], []
     for half in range(2):
         down, flip, y, f_grad = middle(
-            half, x_all, owns[half], others[half], grad_all, norm_two, middle_w
+            half, after(x_all, *downs), owns[half], others[half], grad_all, norm_two, middle_w
         )
         downs.append(down)
         flips.append(flip)
         ys.append(y)
         f_grads.append(f_grad)
-        f_others.append(others_sum(f_grad, ranks))
-    middle_part = middle_weights(flips, ys)
-    middle_grad = lax.psum_scatter(
-        middle_part, "dp", scatter_dimension=0, tiled=True
-    ).astype(F32)
+        if half == 0:
+            f_others.append(others_sum(f_grad, ranks))
+    down_part = middle_weights(flips, ys, True)
+    f_others.append(others_sum(after(f_grads[1], f_others[0], down_part), ranks))
+    middle_part = middle_weights(flips, ys, False, down_part)
+    middle_sum = lax.psum_scatter(middle_part, "dp", scatter_dimension=0, tiled=True)
+    middle_grad = middle_sum.astype(F32)
 
     f_others[1] = after(f_others[1], middle_part)
 
     residual_grads, projs, mixed_grads, norm_two_part = [], [], [], 0.0
     for half in range(2):
         residual_grad, proj, mixed_grad, part = residual_back(
-            half, x_all, owns[half], others[half], grad_all, f_grads[half], f_others[half],
+            half, after(x_all, *projs), owns[half], others[half], grad_all, f_grads[half], f_others[half],
             norm_two, attention_w, heads,
         )
         residual_grads.append(residual_grad)
@@ -696,7 +738,9 @@
 
     if ranks == 2:
         send = after(jnp.where(me == 0, downs[1], downs[0]), mixed_grads[1])
-        down_sum = own_rows(downs, ranks, me, tok_rows).astype(F32) + swap(send).astype(F32)
+        down_other = swap(send)
+        bits = after(bits, down_other)
+        down_sum = own_rows(downs, ranks, me, tok_rows).astype(F32) + down_other.astype(F32)
     else:
         down_sum = lax.psum_scatter(
             jnp.concatenate(downs, axis=0).astype(F32), "tensor", scatter_dimension=0, tiled=True
@@ -708,6 +752,7 @@
     )
     layer_output = (residual + down_sum).astype(BF16)
 
+    bits = after(bits, middle_sum)
     attention_part, sums = attention_weights(input_flip, projs, bits, mixed, attention_w)
     attention_grad = lax.psum_scatter(
         attention_part, "dp", scatter_dimension=0, tiled=True
@@ -730,14 +775,19 @@
     input_grad = own_rows(residual_grads, ranks, me, tok_rows) + scale * (
         u - normed * jnp.mean(u * normed, axis=-1, keepdims=True)
     )
-    attention_norm_grad, feedforward_norm_grad, query_norm_grad, key_norm_grad = lax.psum(
-        (
-            norm_one_part,
-            norm_two_part,
-            jnp.sum(query_part, axis=(0, 1)),
-            jnp.sum(key_part, axis=(0, 1)),
-        ),
-        ("dp", "tensor"),
+    sums = sum_over_all(
+        jnp.concatenate(
+            [
+                norm_one_part,
+                norm_two_part,
+                jnp.sum(query_part, axis=(0, 1)),
+                jnp.sum(key_part, axis=(0, 1)),
+            ]
+        ).reshape(-1, HEAD_SIZE),
+        lax.axis_size("dp") * ranks,
+    ).reshape(-1)
+    attention_norm_grad, feedforward_norm_grad, query_norm_grad, key_norm_grad = jnp.split(
+        sums, [width, 2 * width, 2 * width + HEAD_SIZE]
     )
     qkv_grad = attention_grad[:, : groups * GROUP].reshape(depth, groups, GROUP)
     return (

time: 677 us -> 532 us (0.79)
  blocking collectives: 111 us -> 0 us
  waiting for transfers between devices: 167 us -> 123 us
    psum x1 -> x0, blocking collectives: 111 us -> none  [on_device(): lax.psum((norm_one_part, norm_two_part, jnp.sum(query_part, axis=(0, 1)),...]
    reduce_scatter x1, waiting for transfers between devices: 43.5 us -> 0.02 us  [on_device(): lax.psum_scatter(middle_part, 'dp', scatter_dimension=0, tiled=True)]
    ppermute x8, waiting for transfers between devices: 120 us -> 101 us  [swap(): return lax.ppermute(values, 'tensor', [(0, 1), (1, 0)])]
    pallas_call x1 -> x2, Pallas kernels: 26.2 us -> 29 us  [middle_weights(): pl.pallas_call(lambda *refs: middle_weights_kernel(0, *refs), grid=(block...]
  transfers between devices with their start and end apart: 12 -> 17, of which waited for: 6 -> 11; matrix products, arithmetic and copies ran while one was open for 6% -> 7% of each run, Pallas kernels for 28% -> 57%
where the time goes in v2:
time: 532 us; the launch traced here: 526 us
  Pallas kernels  319 us (60%)
  waiting for transfers between devices  123 us (23%)
  other arithmetic  37.9 us (7%)
  starting transfers between devices  17.8 us (3%)
  between operations  14.3 us (3%)
  local copies, waits for them, and re-layouts  13.8 us (3%)
    ppermute x8, waiting for transfers between devices, swap(): return lax.ppermute(values, 'tensor', [(0, 1), (1, 0)])  101 us
    pallas_call x1, Pallas kernels, attend_back(): pl.pallas_call(attend_back_kernel, grid=(groups,), in_specs=[pl.BlockSpec...  97.2 us
    pallas_call x2, Pallas kernels, middle(): pl.pallas_call(middle_kernel, grid=(HALF // rows,), in_specs=[half_rows(r...  60.9 us
    pallas_call x2, Pallas kernels, attend(): pl.pallas_call(lambda *refs: attend_kernel(first, *refs), grid=(groups, b...  40.1 us
    pallas_call x2, Pallas kernels, middle_weights(): pl.pallas_call(lambda *refs: middle_weights_kernel(0, *refs), grid=(block...  29 us
    pallas_call x2, Pallas kernels, residual_back(): pl.pallas_call(residual_back_kernel, grid=(HALF // rows,), in_specs=[half...  24 us
    pallas_call x1, Pallas kernels, attention_weights(): pl.pallas_call(lambda *refs: attention_weights_kernel(bound, *refs), grid...  20.5 us
    pallas_call x2, Pallas kernels, input_back(): pl.pallas_call(input_back_kernel, grid_spec=pltpu.PrefetchScalarGridSpec(...  18.3 us
  transfers between devices with their start and end apart: 17, of which 11 were waited for; matrix products, arithmetic and copies ran while one was open for 7% of the time, Pallas kernels for 57%

profile of v2, /device:TPU:0, one launch (start us, length us, event | category | flops | bytes accessed | tf_op | source)
XLA Modules:
  0.0 526.0 jit_solution(16656319025500894090)
XLA Ops:
  7.3 1.0 reshape.90
  8.2 0.9 reshape.89
  9.1 1.1 reshape.88
  10.4 1.7 pad_maximum_fusion.5
  12.2 0.9 pad_maximum_fusion.4
  13.2 3.0 collective-permute-start
  16.2 3.7 fusion.9
  19.9 2.1 pad_maximum_fusion.2
  22.0 39.9 %collective-permute-done = bf16[1024,1024]{1,0:T(8,128)(2,1)} collective-permute-done((bf16[1024,1024]{1,0:T(8,128)(2,1)S(1)}, bf16[1024,1024]{1,0:T(8,128)(2,1)}, u32[]{:S(2)}, u32[]{:S(2)}) %collective-permute-start) | collective-permute-done | bytes 2097184 | tf_op jit(solution)/shard_map/ppermute | solution.py:598
  61.9 1.9 broadcast_select_fusion.4
  63.8 2.5 pad_maximum_fusion.x_ref
  66.3 1.8 collective-permute-start.3
  68.1 8.7 %all-gather.3.cloned.1.call-done.w_ref.refs_6_ = bf16[1024,3072]{1,0:T(8,128)(2,1)} async-done(((bf16[64,3072]{1,0:T(8,128)(2,1)}), bf16[1024,3072]{1,0:T(8,128)(2,1)}) %all-gather.3.cloned.1.call-update) | async-done | bytes 6291472 | tf_op jit(solution)/shard_map/all_gather | solution.py:683
  76.8 17.3 %project.1 = (bf16[1024,2048]{1,0:T(8,128)(2,1)}, bf16[2048,2048]{1,0:T(8,128)(2,1)}, bf16[2048,2048]{1,0:T(8,128)(2,1)}) custom-call(bf16[2048,1024]{1,0:T(8,128)(2,1)} %pad_maximum_fusion.x_ref, f32[1,1024]{1,0:T(1,128)} %bitcast.48, bf16[1024,3072]{1,0:T(8,128)(2,1)} %all-gather.3.cloned.1.call-done.w_ref.refs_6_, f32[1,128]{1,0:T(1,128)} %bitcast.53, ...), custom_call_target="tpu_custom_call" | custom-call | flops 17179869184 | tf_op jit(solution)/shard_map/project/pallas_call | solution.py:83
  94.1 13.3 %attend.2 = (bf16[1024,1024]{1,0:T(8,128)(2,1)}, bf16[1024,1024]{1,0:T(8,128)(2,1)}) custom-call(bf16[2048,2048]{1,0:T(8,128)(2,1)} %get-tuple-element.54.refs_0_.refs_1_.refs_2_.rot_ref, bf16[2048,2048]{1,0:T(8,128)(2,1)} %get-tuple-element.54.refs_0_.refs_1_.refs_2_.rot_ref, bf16[2048,2048]{1,0:T(8,128)(2,1)} %get-tuple-element.54.refs_0_.refs_1_.refs_2_.rot_ref), custom_call_target="tpu_custom_call" | custom-call | flops 8589934592 | tf_op jit(solution)/shard_map/attend/pallas_call | solution.py:167
  107.4 6.1 %out_project.2.own_ref = bf16[1024,1024]{1,0:T(8,128)(2,1)} custom-call(bf16[1024,1024]{1,0:T(8,128)(2,1)} %get-tuple-element.53.mixed_ref.out_a.refs_4_, bf16[1024,3072]{1,0:T(8,128)(2,1)} %all-gather.3.cloned.1.call-done.w_ref.refs_6_), custom_call_target="tpu_custom_call" | custom-call | flops 6135667712 | tf_op jit(solution)/shard_map/out_project/pallas_call | solution.py:200
  113.5 1.5 collective-permute-start.1
  115.0 3.8 broadcast_select_fusion.1
  118.8 26.8 %attend.3 = (bf16[1024,1024]{1,0:T(8,128)(2,1)}, bf16[1024,1024]{1,0:T(8,128)(2,1)}) custom-call(bf16[2048,2048]{1,0:T(8,128)(2,1)} %get-tuple-element.54.refs_0_.refs_1_.refs_2_.rot_ref, bf16[2048,2048]{1,0:T(8,128)(2,1)} %get-tuple-element.54.refs_0_.refs_1_.refs_2_.rot_ref, bf16[2048,2048]{1,0:T(8,128)(2,1)} %get-tuple-element.54.refs_0_.refs_1_.refs_2_.rot_ref), custom_call_target="tpu_custom_call" | custom-call | flops 17179869184 | tf_op jit(solution)/shard_map/attend/pallas_call | solution.py:167
  145.6 6.1 %out_project.3.own_ref = bf16[1024,1024]{1,0:T(8,128)(2,1)} custom-call(bf16[1024,1024]{1,0:T(8,128)(2,1)} %get-tuple-element.55.mixed_ref.out_b.refs_5_, bf16[1024,3072]{1,0:T(8,128)(2,1)} %all-gather.3.cloned.1.call-done.w_ref.refs_6_), custom_call_target="tpu_custom_call" | custom-call | flops 6135667712 | tf_op jit(solution)/shard_map/out_project/pallas_call | solution.py:200
  151.7 9.9 %collective-permute-done.1.other_ref = bf16[1024,1024]{1,0:T(8,128)(2,1)} collective-permute-done((bf16[1024,1024]{1,0:T(8,128)(2,1)}, bf16[1024,1024]{1,0:T(8,128)(2,1)}, u32[]{:S(2)}, u32[]{:S(2)}) %collective-permute-start.1) | collective-permute-done | bytes 2097184 | tf_op jit(solution)/shard_map/ppermute | solution.py:598
  161.6 1.4 collective-permute-start.2
  163.1 4.0 pad_maximum_fusion.1.grad_ref
  167.1 30.6 %middle.2 = (bf16[1024,1024]{1,0:T(8,128)(2,1)}, bf16[2,1024,1024]{2,1,0:T(8,128)(2,1)}, bf16[1024,4608]{1,0:T(8,128)(2,1)}, bf16[1024,1024]{1,0:T(8,128)(2,1)}) custom-call(bf16[2048,1024]{1,0:T(8,128)(2,1)} %pad_maximum_fusion.x_ref, bf16[1024,1024]{1,0:T(8,128)(2,1)} %out_project.2.own_ref, bf16[1024,1024]{1,0:T(8,128)(2,1)} %collective-permute-done.1.other_ref, ...), custom_call_target="tpu_custom_call" | custom-call | flops 7730940928 | tf_op jit(solution)/shard_map/middle/pallas_call | solution.py:413
  197.6 0.6 collective-permute-start.4
  198.3 12.2 %collective-permute-done.2.other_ref = bf16[1024,1024]{1,0:T(8,128)(2,1)} collective-permute-done((bf16[1024,1024]{1,0:T(8,128)(2,1)}, bf16[1024,1024]{1,0:T(8,128)(2,1)}, u32[]{:S(2)}, u32[]{:S(2)}) %collective-permute-start.2) | collective-permute-done | bytes 2097184 | tf_op jit(solution)/shard_map/ppermute | solution.py:598
  210.5 30.3 %middle.3 = (bf16[1024,1024]{1,0:T(8,128)(2,1)}, bf16[2,1024,1024]{2,1,0:T(8,128)(2,1)}, bf16[1024,4608]{1,0:T(8,128)(2,1)}, bf16[1024,1024]{1,0:T(8,128)(2,1)}) custom-call(bf16[2048,1024]{1,0:T(8,128)(2,1)} %pad_maximum_fusion.x_ref, bf16[1024,1024]{1,0:T(8,128)(2,1)} %out_project.3.own_ref, bf16[1024,1024]{1,0:T(8,128)(2,1)} %collective-permute-done.2.other_ref, ...), custom_call_target="tpu_custom_call" | custom-call | flops 7730940928 | tf_op jit(solution)/shard_map/middle/pallas_call | solution.py:413
  240.8 10.9 %down_weights.1.refs_4_ = bf16[1024,4608]{1,0:T(8,128)(2,1)} custom-call(bf16[2,1024,1024]{2,1,0:T(8,128)(2,1)} %get-tuple-element.66.refs_0_, bf16[2,1024,1024]{2,1,0:T(8,128)(2,1)} %get-tuple-element.67.refs_1_, bf16[1024,4608]{1,0:T(8,128)(2,1)} %get-tuple-element.68.refs_2_, bf16[1024,4608]{1,0:T(8,128)(2,1)} %get-tuple-element.69.refs_3_), custom_call_target="tpu_custom_call" | custom-call | flops 2147483648 | tf_op jit(solution)/shard_map/down_weights/pallas_call | solution.py:506
  251.7 2.1 collective-permute-done.4.fg_other_ref
  253.9 1.4 collective-permute-start.5
  255.3 18.1 %gate_up_weights.1 = bf16[1024,4608]{1,0:T(8,128)(2,1)} custom-call(bf16[2,1024,1024]{2,1,0:T(8,128)(2,1)} %get-tuple-element.66.refs_0_, bf16[2,1024,1024]{2,1,0:T(8,128)(2,1)} %get-tuple-element.67.refs_1_, bf16[1024,4608]{1,0:T(8,128)(2,1)} %get-tuple-element.68.refs_2_, ...), custom_call_target="tpu_custom_call", output_to_operand_aliasing={{}: (4, {})} | custom-call | flops 4294967296 | tf_op jit(solution)/shard_map/gate_up_weights/pallas_call | solution.py:506
  273.5 1.5 copy-done.2
  275.0 3.2 broadcast_select_fusion.2
  278.2 12.6 %residual_back.2 = (f32[1024,1024]{1,0:T(8,128)}, bf16[1024,1024]{1,0:T(8,128)(2,1)}, bf16[1024,1024]{1,0:T(8,128)(2,1)}, f32[8,1024]{1,0:T(8,128)}) custom-call(bf16[2048,1024]{1,0:T(8,128)(2,1)} %pad_maximum_fusion.x_ref, bf16[1024,1024]{1,0:T(8,128)(2,1)} %out_project.2.own_ref, bf16[1024,1024]{1,0:T(8,128)(2,1)} %collective-permute-done.1.other_ref, ...), custom_call_target="tpu_custom_call" | custom-call | flops 11302545408 | tf_op jit(solution)/shard_map/residual_back/pallas_call | solution.py:465
  290.7 9.6 %collective-permute-done.5.fg_other_ref = bf16[1024,1024]{1,0:T(8,128)(2,1)} collective-permute-done((bf16[1024,1024]{1,0:T(8,128)(2,1)}, bf16[1024,1024]{1,0:T(8,128)(2,1)}, u32[]{:S(2)}, u32[]{:S(2)}) %collective-permute-start.5) | collective-permute-done | bytes 2097184 | tf_op jit(solution)/shard_map/ppermute | solution.py:598
  300.3 11.4 %residual_back.3 = (f32[1024,1024]{1,0:T(8,128)}, bf16[1024,1024]{1,0:T(8,128)(2,1)}, bf16[1024,1024]{1,0:T(8,128)(2,1)}, f32[8,1024]{1,0:T(8,128)}) custom-call(bf16[2048,1024]{1,0:T(8,128)(2,1)} %pad_maximum_fusion.x_ref, bf16[1024,1024]{1,0:T(8,128)(2,1)} %out_project.3.own_ref, bf16[1024,1024]{1,0:T(8,128)(2,1)} %collective-permute-done.2.other_ref, ...), custom_call_target="tpu_custom_call" | custom-call | flops 11302545408 | tf_op jit(solution)/shard_map/residual_back/pallas_call | solution.py:465
  311.7 1.4 collective-permute-start.6
  313.1 97.2 %attend_back.1 = (bf16[2048,2048]{1,0:T(8,128)(2,1)}, f32[4,8,128]{2,1,0:T(8,128)}, f32[4,8,128]{2,1,0:T(8,128)}) custom-call(bf16[2048,2048]{1,0:T(8,128)(2,1)} %get-tuple-element.54.refs_0_.refs_1_.refs_2_.rot_ref, bf16[2048,2048]{1,0:T(8,128)(2,1)} %get-tuple-element.76.raw_ref, bf16[1024,1024]{1,0:T(8,128)(2,1)} %get-tuple-element.77.do_a, ...), custom_call_target="tpu_custom_call" | custom-call | flops 268435456000 | tf_op jit(solution)/shard_map/attend_back/pallas_call | solution.py:327
  410.4 20.5 %attention_weights.1 = (bf16[1024,3072]{1,0:T(8,128)(2,1)}, f32[1024,128]{1,0:T(8,128)}) custom-call(bf16[1024,2048]{1,0:T(8,128)(2,1)} %get-tuple-element.83.refs_0_, bf16[1024,1024]{1,0:T(8,128)(2,1)} %get-tuple-element.63.refs_1_, bf16[1024,1024]{1,0:T(8,128)(2,1)} %get-tuple-element.84.refs_2_, bf16[2048,2048]{1,0:T(8,128)(2,1)} %get-tuple-element.82.bits_ref.refs_3_, ...), custom_call_target="tpu_custom_call" | custom-call | flops 20132659200 | tf_op jit(solution)/shard_map/attention_weights/pallas_call | solution.py:547
  430.9 1.6 copy-done.1
  432.5 0.5 fusion.8
  433.9 0.7 collective-permute-start.8
  434.6 3.1 collective-permute-done.8
  437.6 9.1 %input_back.3 = bf16[1024,1024]{1,0:T(8,128)(2,1)} custom-call(s32[1]{0:T(128)} %bitcast.7.place_ref, bf16[2048,2048]{1,0:T(8,128)(2,1)} %get-tuple-element.82.bits_ref.refs_3_, bf16[1024,3072]{1,0:T(8,128)(2,1)} %all-gather.3.cloned.1.call-done.w_ref.refs_6_), custom_call_target="tpu_custom_call" | custom-call | flops 8947848192 | tf_op jit(solution)/shard_map/input_back/pallas_call | solution.py:579
  446.8 0.6 collective-permute-start.7
  447.4 1.1 collective-permute-start.10
  448.5 9.1 %input_back.2 = bf16[1024,1024]{1,0:T(8,128)(2,1)} custom-call(s32[1]{0:T(128)} %bitcast.6.place_ref, bf16[2048,2048]{1,0:T(8,128)(2,1)} %get-tuple-element.82.bits_ref.refs_3_, bf16[1024,3072]{1,0:T(8,128)(2,1)} %all-gather.3.cloned.1.call-done.w_ref.refs_6_), custom_call_target="tpu_custom_call" | custom-call | flops 8947848192 | tf_op jit(solution)/shard_map/input_back/pallas_call | solution.py:579
  457.6 1.7 collective-permute-start.11
  459.3 1.0 fusion.11
  460.4 1.0 collective-permute-done.11
  461.4 2.3 collective-permute-start.12
  463.7 0.8 slice_bitcast_fusion
  464.5 1.9 collective-permute-done.12
  466.4 0.5 slice_bitcast_fusion.4
  466.9 0.6 slice_bitcast_fusion.2
  467.5 27.6 %collective-permute-done.7 = bf16[1024,1024]{1,0:T(8,128)(2,1)} collective-permute-done((bf16[1024,1024]{1,0:T(8,128)(2,1)}, bf16[1024,1024]{1,0:T(8,128)(2,1)}, u32[]{:S(2)}, u32[]{:S(2)}) %collective-permute-start.7) | collective-permute-done | bytes 2097184 | tf_op jit(solution)/shard_map/ppermute | solution.py:598
  495.1 2.8 fusion.2
  498.0 10.3 %fusion.5 = (f32[1024,1024]{1,0:T(8,128)}, bf16[1024,1024]{1,0:T(8,128)(2,1)}) fusion(bf16[1024,1024]{1,0:T(8,128)(2,1)S(1)} %copy-done.1, f32[1024,1024]{1,0:T(8,128)S(1)} %copy-done.6, f32[1024,1024]{1,0:T(8,128)} %get-tuple-element.75, bf16[1024,1024]{1,0:T(8,128)(2,1)} %collective-permute-done.7, bf16[1024,1024]{1,0:T(8,128)(2,1)S(1)} %copy-done.5, ...), kind=kLoop, calls=%fused_computation.8 | loop fusion | flops 24117248 | bytes 35663872 | tf_op jit(solution)/shard_map/add | solution.py:775
  508.3 6.6 %reduce-scatter.5.cloned.1.call-done = bf16[64,3072]{1,0:T(8,128)(2,1)} async-done(((bf16[1024,3072]{1,0:T(8,128)(2,1)}), bf16[64,3072]{1,0:T(8,128)(2,1)}) %reduce-scatter.5.cloned.1.call-update) | async-done | bytes 393232 | tf_op jit(solution)/shard_map/reduce_scatter | solution.py:757
  514.9 1.1 slice.36
  516.4 0.8 copy.28
  517.2 0.7 copy.34
  517.8 0.7 copy.33
  518.5 0.7 slice_bitcast_fusion.1
  (75 shorter events, 1.9 us)
Async XLA Ops:
  7.2 5.0 copy-start.11
  7.2 5.0 copy-start.12
  7.2 5.0 copy-start.13
  7.2 69.6 %all-gather.3.cloned.1.call-start = ((), (), s32[]{:S(2)}) async-start(), calls=%async_computation.2 | async-start | bytes 6684672 | tf_op jit(solution)/shard_map/all_gather | solution.py:683
  9.1 4.1 copy-start
  12.1 154.9 %all-gather.5.cloned.1.call-start = ((), (), s32[]{:S(2)}) async-start(), calls=%async_computation.3 | async-start | bytes 10027008 | tf_op jit(solution)/shard_map/all_gather | solution.py:686
  13.1 397.3 %reduce-scatter.3.cloned.1.call-start = ((), (), s32[]{:S(2)}) async-start(), calls=%async_computation.4 | async-start | bytes 10027008 | tf_op jit(solution)/shard_map/reduce_scatter | solution.py:719
  13.2 48.7 %collective-permute-start = (bf16[1024,1024]{1,0:T(8,128)(2,1)S(1)}, bf16[1024,1024]{1,0:T(8,128)(2,1)}, u32[]{:S(2)}, u32[]{:S(2)}) collective-permute-start(bf16[1024,1024]{1,0:T(8,128)(2,1)S(1)} %copy-done), channel_id=1, source_target_pairs={{0,1},{1,0},{2,3},{3,2},{4,5},{5,4},{6,7},{7,6},{8,9},{9,8},{10,11... | collective-permute-start | bytes 6291464 | tf_op jit(solution)/shard_map/ppermute | solution.py:598
  63.8 2.5 copy-start.9
  66.3 48.7 %collective-permute-start.3 = (bf16[1024,1024]{1,0:T(8,128)(2,1)S(1)}, bf16[1024,1024]{1,0:T(8,128)(2,1)}, u32[]{:S(2)}, u32[]{:S(2)}) collective-permute-start(bf16[1024,1024]{1,0:T(8,128)(2,1)S(1)} %copy-done.9), channel_id=1, source_target_pairs={{0,1},{1,0},{2,3},{3,2},{4,5},{5,4},{6,7},{7,6},{8,9},{9,8},{10,11... | collective-permute-start | bytes 6291464 | tf_op jit(solution)/shard_map/ppermute | solution.py:598
  113.5 48.1 %collective-permute-start.1 = (bf16[1024,1024]{1,0:T(8,128)(2,1)}, bf16[1024,1024]{1,0:T(8,128)(2,1)}, u32[]{:S(2)}, u32[]{:S(2)}) collective-permute-start(bf16[1024,1024]{1,0:T(8,128)(2,1)} %out_project.2.own_ref), channel_id=1, source_target_pairs={{0,1},{1,0},{2,3},{3,2},{4,5},{5,4},{6,7},{7,6},{8,9},{9,8},{10,11... | collective-permute-start | bytes 6291464 | tf_op jit(solution)/shard_map/ppermute | solution.py:598
  161.6 48.9 %collective-permute-start.2 = (bf16[1024,1024]{1,0:T(8,128)(2,1)}, bf16[1024,1024]{1,0:T(8,128)(2,1)}, u32[]{:S(2)}, u32[]{:S(2)}) collective-permute-start(bf16[1024,1024]{1,0:T(8,128)(2,1)} %out_project.3.own_ref), channel_id=1, source_target_pairs={{0,1},{1,0},{2,3},{3,2},{4,5},{5,4},{6,7},{7,6},{8,9},{9,8},{10,11... | collective-permute-start | bytes 6291464 | tf_op jit(solution)/shard_map/ppermute | solution.py:598
  197.6 56.2 %collective-permute-start.4 = (bf16[1024,1024]{1,0:T(8,128)(2,1)}, bf16[1024,1024]{1,0:T(8,128)(2,1)}, u32[]{:S(2)}, u32[]{:S(2)}) collective-permute-start(bf16[1024,1024]{1,0:T(8,128)(2,1)} %get-tuple-element.62.fg_ref), channel_id=1, source_target_pairs={{0,1},{1,0},{2,3},{3,2},{4,5},{5,4},{6,7},{7,6},{8,9},{9,8},{10,11... | collective-permute-start | bytes 6291464 | tf_op jit(solution)/shard_map/ppermute | solution.py:598
  253.9 46.4 %collective-permute-start.5 = (bf16[1024,1024]{1,0:T(8,128)(2,1)}, bf16[1024,1024]{1,0:T(8,128)(2,1)}, u32[]{:S(2)}, u32[]{:S(2)}) collective-permute-start(bf16[1024,1024]{1,0:T(8,128)(2,1)} %get-tuple-element.70.fg_ref), channel_id=1, source_target_pairs={{0,1},{1,0},{2,3},{3,2},{4,5},{5,4},{6,7},{7,6},{8,9},{9,8},{10,11... | collective-permute-start | bytes 6291464 | tf_op jit(solution)/shard_map/ppermute | solution.py:598
  273.4 1.6 copy-start.2
  273.4 241.5 %reduce-scatter.5.cloned.1.call-start = ((), (), s32[]{:S(2)}) async-start(), calls=%async_computation.5 | async-start | bytes 6684672 | tf_op jit(solution)/shard_map/reduce_scatter | solution.py:757
  311.7 98.6 %collective-permute-start.6 = (bf16[1024,1024]{1,0:T(8,128)(2,1)}, bf16[1024,1024]{1,0:T(8,128)(2,1)}, u32[]{:S(2)}, u32[]{:S(2)}) collective-permute-start(bf16[1024,1024]{1,0:T(8,128)(2,1)} %broadcast_select_fusion.2), channel_id=1, source_target_pairs={{0,1},{1,0},{2,3},{3,2},{4,5},{5,4},{6,7},{7,6},{8,9},{9,8},{10,11... | collective-permute-start | bytes 6291464 | tf_op jit(solution)/shard_map/ppermute | solution.py:598
  430.9 1.6 copy-start.1
  432.5 0.8 copy-start.15
  432.5 0.8 copy-start.18
  432.5 0.8 copy-start.17
  432.5 0.8 copy-start.16
  432.5 1.1 copy-start.10
  432.5 1.3 copy-start.14
  433.9 3.8 collective-permute-start.8
  437.6 9.7 %collective-permute-start.9 = (f32[18,128]{1,0:T(8,128)S(1)}, f32[18,128]{1,0:T(8,128)S(1)}, u32[]{:S(2)}, u32[]{:S(2)}) collective-permute-start(f32[18,128]{1,0:T(8,128)S(1)} %fusion.10), channel_id=1, source_target_pairs={{0,2},{1,3},{2,0},{3,1},{4,6},{5,7},{6,4},{7,5},{8,10},{9,11},{10,... | collective-permute-start | bytes 27656 | tf_op jit(solution)/shard_map/ppermute | solution.py:637
  446.8 48.3 %collective-permute-start.7 = (bf16[1024,1024]{1,0:T(8,128)(2,1)}, bf16[1024,1024]{1,0:T(8,128)(2,1)}, u32[]{:S(2)}, u32[]{:S(2)}) collective-permute-start(bf16[1024,1024]{1,0:T(8,128)(2,1)} %input_back.3), channel_id=1, source_target_pairs={{0,1},{1,0},{2,3},{3,2},{4,5},{5,4},{6,7},{7,6},{8,9},{9,8},{10,11... | collective-permute-start | bytes 6291464 | tf_op jit(solution)/shard_map/ppermute | solution.py:598
  447.4 10.2 %collective-permute-start.10 = (f32[18,128]{1,0:T(8,128)S(1)}, f32[18,128]{1,0:T(8,128)S(1)}, u32[]{:S(2)}, u32[]{:S(2)}) collective-permute-start(f32[18,128]{1,0:T(8,128)S(1)} %fusion.13), channel_id=1, source_target_pairs={{0,4},{1,5},{2,6},{3,7},{4,0},{5,1},{6,2},{7,3},{8,12},{9,13},{10,... | collective-permute-start | bytes 27656 | tf_op jit(solution)/shard_map/ppermute | solution.py:637
  448.5 10.9 %copy-start.7 = (bf16[64,4608]{1,0:T(8,128)(2,1)S(1)}, bf16[64,4608]{1,0:T(8,128)(2,1)}, u32[]{:S(2)}) copy-start(bf16[64,4608]{1,0:T(8,128)(2,1)} %reduce-scatter.3.cloned.1.call-done) | copy-start | bytes 1769476
  457.6 37.5 %copy-start.5 = (bf16[1024,1024]{1,0:T(8,128)(2,1)S(1)}, bf16[1024,1024]{1,0:T(8,128)(2,1)}, u32[]{:S(2)}) copy-start(bf16[1024,1024]{1,0:T(8,128)(2,1)} %input_back.2) | copy-start | bytes 6291460
  457.6 3.8 collective-permute-start.11
  460.3 37.6 %copy-start.6 = (f32[1024,1024]{1,0:T(8,128)S(1)}, f32[1024,1024]{1,0:T(8,128)}, u32[]{:S(2)}) copy-start(f32[1024,1024]{1,0:T(8,128)} %get-tuple-element.74) | copy-start | bytes 12582916
  461.4 5.0 collective-permute-start.12
  467.5 30.4 %copy-start.3 = (bf16[1024,1024]{1,0:T(8,128)(2,1)S(1)}, bf16[1024,1024]{1,0:T(8,128)(2,1)}, u32[]{:S(2)}) copy-start(bf16[1024,1024]{1,0:T(8,128)(2,1)} %get-tuple-element.59) | copy-start | bytes 6291460
  467.5 30.4 %copy-start.4 = (bf16[1024,1024]{1,0:T(8,128)(2,1)S(1)}, bf16[1024,1024]{1,0:T(8,128)(2,1)}, u32[]{:S(2)}) copy-start(bf16[1024,1024]{1,0:T(8,128)(2,1)} %get-tuple-element.61) | copy-start | bytes 6291460
  514.9 3.6 copy-start.8
Sparse Core Ops, SparseCore 0:
  12.3 64.5 all-gather.2
  79.1 80.0 all-gather.4
  273.5 109.0 reduce-scatter.2
  431.1 83.7 reduce-scatter.4

commit v3 on v2

--- a/solution.py
+++ b/solution.py
@@ -28,6 +28,11 @@
 
 def nt(left, right):
     return lax.dot_general(left, right, (((1,), (1,)), ((), ())), preferred_element_type=F32)
+
+
+def row_mean(values):
+    ones = jnp.full((HEAD_SIZE, HEAD_SIZE), 1.0 / HEAD_SIZE, BF16)
+    return nn(values.astype(BF16), ones)
 
 
 def rope_tables():
@@ -218,34 +223,25 @@
 def attend_back_kernel(
     rot_ref, raw_ref, do_a, do_b, out_a, out_b, log_a, log_b, qn_ref, kn_ref, cos_ref, sin_ref,
     bits_ref, qg_ref, kg_ref,
-    q_wide, d_wide, k_wide, v_wide, k_flip, dq_flip, dk, dv,
+    grads, log_row, delta_row, k_flip, dq_flip, dk, dv,
 ):
     blocks = SEQ_LEN // BLOCK
-    lane = lax.broadcasted_iota(jnp.int32, (ROWS, HEAD_SIZE), 1)
-    ones = jnp.where(lane < 3, 1.0, 0.0).astype(BF16)
+    ones = jnp.ones((8, HEAD_SIZE), BF16)
 
     def prepare(half, do_ref, out_ref, log_ref):
         def body(r, carry):
             near = pl.ds(pl.multiple_of(r * ROWS, ROWS), ROWS)
             rows = pl.ds(pl.multiple_of(half * HALF + r * ROWS, ROWS), ROWS)
-            key = rot_ref[rows, 2 * HEAD_SIZE : 3 * HEAD_SIZE]
-            k_wide[rows, :HEAD_SIZE] = key
-            k_wide[rows, HEAD_SIZE:] = ones
-            v_wide[rows, :HEAD_SIZE] = rot_ref[rows, 3 * HEAD_SIZE :]
-            v_wide[rows, HEAD_SIZE:] = ones
-            k_flip[:, rows] = key.T
+            k_flip[:, rows] = rot_ref[rows, 2 * HEAD_SIZE : 3 * HEAD_SIZE].T
+            grad = do_ref[near, :]
+            grads[rows, :] = grad
+            product = grad.astype(F32) * out_ref[near, :].astype(F32)
+            high = product.astype(BF16)
+            low = (product - high.astype(F32)).astype(BF16)
             for head in range(2):
                 columns = slice(head * HEAD_SIZE, (head + 1) * HEAD_SIZE)
-                q_wide[head, rows, :HEAD_SIZE] = rot_ref[rows, columns]
-                q_wide[head, rows, HEAD_SIZE:] = log_ref[near, columns]
-                grad = do_ref[near, columns]
-                delta = jnp.sum(
-                    grad.astype(F32) * out_ref[near, columns].astype(F32), axis=-1, keepdims=True
-                )
-                d_wide[head, rows, :HEAD_SIZE] = grad
-                d_wide[head, rows, HEAD_SIZE:] = split_three(
-                    jnp.broadcast_to(-delta, (ROWS, HEAD_SIZE))
-                )
+                log_row[head, :, rows] = nt(ones, log_ref[near, columns])
+                delta_row[head, :, rows] = nt(ones, high[:, columns]) + nt(ones, low[:, columns])
             return carry
 
         lax.fori_loop(0, HALF // ROWS, body, 0)
@@ -256,18 +252,21 @@
 
     def tile(kv_start, kv_size, start, size, masked):
         kv, q_rows = pl.ds(kv_start, kv_size), pl.ds(start, size)
+        keys = rot_ref[kv, 2 * HEAD_SIZE : 3 * HEAD_SIZE]
+        values = rot_ref[kv, 3 * HEAD_SIZE :]
         for head in range(2):
-            q = q_wide[head, q_rows, :]
-            d = d_wide[head, q_rows, :]
-            s = nt(k_wide[kv, :], q)
+            columns = slice(head * HEAD_SIZE, (head + 1) * HEAD_SIZE)
+            q = rot_ref[q_rows, columns]
+            d = grads[q_rows, columns]
+            s = nt(keys, q) + log_row[head, :1, q_rows]
             if masked:
                 row = lax.broadcasted_iota(jnp.int32, s.shape, 0)
                 column = lax.broadcasted_iota(jnp.int32, s.shape, 1)
                 s = jnp.where(row <= column, s, masked_score)
             p = jnp.exp2(s)
-            ds = (p * nt(v_wide[kv, :], d)).astype(BF16)
-            new_dv = nn(p.astype(BF16), d[:, :HEAD_SIZE])
-            new_dk = nn(ds, q[:, :HEAD_SIZE])
+            ds = (p * (nt(values, d) - delta_row[head, :1, q_rows])).astype(BF16)
+            new_dv = nn(p.astype(BF16), d)
+            new_dk = nn(ds, q)
             if masked and head == 0:
                 dv[kv, :] = new_dv
                 dk[kv, :] = new_dk
@@ -308,12 +307,12 @@
                 gain, total = kn_ref[...], kg_ref
             u = u * cosine - pltpu.roll(u, HEAD_SIZE // 2, 1) * sine
             x = raw_ref[rows, columns].astype(F32)
-            scale = lax.rsqrt(jnp.mean(x * x, axis=-1, keepdims=True) + epsilon)
+            scale = lax.rsqrt(row_mean(x * x) + epsilon)
             x = x * scale
             total[0] += jnp.sum((u * x).reshape(ROWS // 8, 8, HEAD_SIZE), axis=0)
             w = u * gain
             bits_ref[rows, columns] = (
-                scale * (w - x * jnp.mean(w * x, axis=-1, keepdims=True))
+                scale * (w - x * row_mean(w * x))
             ).astype(BF16)
         bits_ref[rows, 3 * HEAD_SIZE :] = dv[rows, :].astype(BF16)
         return carry
@@ -347,10 +346,9 @@
             jax.ShapeDtypeStruct((groups, 8, HEAD_SIZE), F32),
         ],
         scratch_shapes=[
-            pltpu.VMEM((2, SEQ_LEN, width), BF16),
-            pltpu.VMEM((2, SEQ_LEN, width), BF16),
             pltpu.VMEM((SEQ_LEN, width), BF16),
-            pltpu.VMEM((SEQ_LEN, width), BF16),
+            pltpu.VMEM((2, 8, SEQ_LEN), F32),
+            pltpu.VMEM((2, 8, SEQ_LEN), F32),
             pltpu.VMEM((HEAD_SIZE, SEQ_LEN), BF16),
             pltpu.VMEM((2, HEAD_SIZE, SEQ_LEN), F32),
             pltpu.VMEM((SEQ_LEN, HEAD_SIZE), F32),

time: 532 us -> 518 us (0.974)
  Pallas kernels: 319 us -> 306 us
    pallas_call x1, Pallas kernels: 97.2 us -> 83.6 us  [attend_back(): pl.pallas_call(attend_back_kernel, grid=(groups,), in_specs=[pl.BlockSpec...]
  transfers between devices with their start and end apart: 17 -> 17, of which waited for: 11 -> 11; matrix products, arithmetic and copies ran while one was open for 7% -> 8% of each run, Pallas kernels for 57% -> 56%
where the time goes in v3:
time: 518 us; the launch traced here: 512 us
  Pallas kernels  306 us (59%)
  waiting for transfers between devices  123 us (24%)
  other arithmetic  37.9 us (7%)
  starting transfers between devices  17.8 us (3%)
  between operations  14.3 us (3%)
  local copies, waits for them, and re-layouts  13.8 us (3%)
    ppermute x8, waiting for transfers between devices, swap(): return lax.ppermute(values, 'tensor', [(0, 1), (1, 0)])  101 us
    pallas_call x1, Pallas kernels, attend_back(): pl.pallas_call(attend_back_kernel, grid=(groups,), in_specs=[pl.BlockSpec...  83.6 us
    pallas_call x2, Pallas kernels, middle(): pl.pallas_call(middle_kernel, grid=(HALF // rows,), in_specs=[half_rows(r...  60.9 us
    pallas_call x2, Pallas kernels, attend(): pl.pallas_call(lambda *refs: attend_kernel(first, *refs), grid=(groups, b...  40.1 us
    pallas_call x2, Pallas kernels, middle_weights(): pl.pallas_call(lambda *refs: middle_weights_kernel(0, *refs), grid=(block...  29 us
    pallas_call x2, Pallas kernels, residual_back(): pl.pallas_call(residual_back_kernel, grid=(HALF // rows,), in_specs=[half...  24 us
    pallas_call x1, Pallas kernels, attention_weights(): pl.pallas_call(lambda *refs: attention_weights_kernel(bound, *refs), grid...  20.5 us
    pallas_call x2, Pallas kernels, input_back(): pl.pallas_call(input_back_kernel, grid_spec=pltpu.PrefetchScalarGridSpec(...  18.3 us
  transfers between devices with their start and end apart: 17, of which 11 were waited for; matrix products, arithmetic and copies ran while one was open for 8% of the time, Pallas kernels for 56%

profile of v3, /device:TPU:0, one launch (start us, length us, event | category | flops | bytes accessed | tf_op | source)
XLA Modules:
  0.0 512.4 jit_solution(8274532809837376428)
XLA Ops:
  7.3 1.0 reshape.90
  8.2 0.9 reshape.89
  9.1 1.1 reshape.88
  10.4 1.7 pad_maximum_fusion.5
  12.2 0.9 pad_maximum_fusion.4
  13.2 3.0 collective-permute-start
  16.2 3.7 fusion.9
  19.9 2.1 pad_maximum_fusion.2
  22.0 39.9 %collective-permute-done = bf16[1024,1024]{1,0:T(8,128)(2,1)} collective-permute-done((bf16[1024,1024]{1,0:T(8,128)(2,1)S(1)}, bf16[1024,1024]{1,0:T(8,128)(2,1)}, u32[]{:S(2)}, u32[]{:S(2)}) %collective-permute-start) | collective-permute-done | bytes 2097184 | tf_op jit(solution)/shard_map/ppermute | solution.py:596
  61.9 1.9 broadcast_select_fusion.4
  63.8 2.5 pad_maximum_fusion.x_ref
  66.3 1.8 collective-permute-start.3
  68.1 8.7 %all-gather.3.cloned.1.call-done.w_ref.refs_6_ = bf16[1024,3072]{1,0:T(8,128)(2,1)} async-done(((bf16[64,3072]{1,0:T(8,128)(2,1)}), bf16[1024,3072]{1,0:T(8,128)(2,1)}) %all-gather.3.cloned.1.call-update) | async-done | bytes 6291472 | tf_op jit(solution)/shard_map/all_gather | solution.py:681
  76.8 17.3 %project.1 = (bf16[1024,2048]{1,0:T(8,128)(2,1)}, bf16[2048,2048]{1,0:T(8,128)(2,1)}, bf16[2048,2048]{1,0:T(8,128)(2,1)}) custom-call(bf16[2048,1024]{1,0:T(8,128)(2,1)} %pad_maximum_fusion.x_ref, f32[1,1024]{1,0:T(1,128)} %bitcast.48, bf16[1024,3072]{1,0:T(8,128)(2,1)} %all-gather.3.cloned.1.call-done.w_ref.refs_6_, f32[1,128]{1,0:T(1,128)} %bitcast.53, ...), custom_call_target="tpu_custom_call" | custom-call | flops 17179869184 | tf_op jit(solution)/shard_map/project/pallas_call | solution.py:88
  94.1 13.3 %attend.2 = (bf16[1024,1024]{1,0:T(8,128)(2,1)}, bf16[1024,1024]{1,0:T(8,128)(2,1)}) custom-call(bf16[2048,2048]{1,0:T(8,128)(2,1)} %get-tuple-element.54.refs_0_.refs_1_.refs_2_.rot_ref, bf16[2048,2048]{1,0:T(8,128)(2,1)} %get-tuple-element.54.refs_0_.refs_1_.refs_2_.rot_ref, bf16[2048,2048]{1,0:T(8,128)(2,1)} %get-tuple-element.54.refs_0_.refs_1_.refs_2_.rot_ref), custom_call_target="tpu_custom_call" | custom-call | flops 8589934592 | tf_op jit(solution)/shard_map/attend/pallas_call | solution.py:172
  107.4 6.1 %out_project.2.own_ref = bf16[1024,1024]{1,0:T(8,128)(2,1)} custom-call(bf16[1024,1024]{1,0:T(8,128)(2,1)} %get-tuple-element.53.mixed_ref.out_a.refs_4_, bf16[1024,3072]{1,0:T(8,128)(2,1)} %all-gather.3.cloned.1.call-done.w_ref.refs_6_), custom_call_target="tpu_custom_call" | custom-call | flops 6135667712 | tf_op jit(solution)/shard_map/out_project/pallas_call | solution.py:205
  113.5 1.5 collective-permute-start.1
  115.0 3.8 broadcast_select_fusion.1
  118.8 26.8 %attend.3 = (bf16[1024,1024]{1,0:T(8,128)(2,1)}, bf16[1024,1024]{1,0:T(8,128)(2,1)}) custom-call(bf16[2048,2048]{1,0:T(8,128)(2,1)} %get-tuple-element.54.refs_0_.refs_1_.refs_2_.rot_ref, bf16[2048,2048]{1,0:T(8,128)(2,1)} %get-tuple-element.54.refs_0_.refs_1_.refs_2_.rot_ref, bf16[2048,2048]{1,0:T(8,128)(2,1)} %get-tuple-element.54.refs_0_.refs_1_.refs_2_.rot_ref), custom_call_target="tpu_custom_call" | custom-call | flops 17179869184 | tf_op jit(solution)/shard_map/attend/pallas_call | solution.py:172
  145.6 6.1 %out_project.3.own_ref = bf16[1024,1024]{1,0:T(8,128)(2,1)} custom-call(bf16[1024,1024]{1,0:T(8,128)(2,1)} %get-tuple-element.55.mixed_ref.out_b.refs_5_, bf16[1024,3072]{1,0:T(8,128)(2,1)} %all-gather.3.cloned.1.call-done.w_ref.refs_6_), custom_call_target="tpu_custom_call" | custom-call | flops 6135667712 | tf_op jit(solution)/shard_map/out_project/pallas_call | solution.py:205
  151.7 9.9 %collective-permute-done.1.other_ref = bf16[1024,1024]{1,0:T(8,128)(2,1)} collective-permute-done((bf16[1024,1024]{1,0:T(8,128)(2,1)}, bf16[1024,1024]{1,0:T(8,128)(2,1)}, u32[]{:S(2)}, u32[]{:S(2)}) %collective-permute-start.1) | collective-permute-done | bytes 2097184 | tf_op jit(solution)/shard_map/ppermute | solution.py:596
  161.6 1.4 collective-permute-start.2
  163.1 4.0 pad_maximum_fusion.1.grad_ref
  167.1 30.6 %middle.2 = (bf16[1024,1024]{1,0:T(8,128)(2,1)}, bf16[2,1024,1024]{2,1,0:T(8,128)(2,1)}, bf16[1024,4608]{1,0:T(8,128)(2,1)}, bf16[1024,1024]{1,0:T(8,128)(2,1)}) custom-call(bf16[2048,1024]{1,0:T(8,128)(2,1)} %pad_maximum_fusion.x_ref, bf16[1024,1024]{1,0:T(8,128)(2,1)} %out_project.2.own_ref, bf16[1024,1024]{1,0:T(8,128)(2,1)} %collective-permute-done.1.other_ref, ...), custom_call_target="tpu_custom_call" | custom-call | flops 7730940928 | tf_op jit(solution)/shard_map/middle/pallas_call | solution.py:411
  197.6 0.6 collective-permute-start.4
  198.3 12.2 %collective-permute-done.2.other_ref = bf16[1024,1024]{1,0:T(8,128)(2,1)} collective-permute-done((bf16[1024,1024]{1,0:T(8,128)(2,1)}, bf16[1024,1024]{1,0:T(8,128)(2,1)}, u32[]{:S(2)}, u32[]{:S(2)}) %collective-permute-start.2) | collective-permute-done | bytes 2097184 | tf_op jit(solution)/shard_map/ppermute | solution.py:596
  210.5 30.3 %middle.3 = (bf16[1024,1024]{1,0:T(8,128)(2,1)}, bf16[2,1024,1024]{2,1,0:T(8,128)(2,1)}, bf16[1024,4608]{1,0:T(8,128)(2,1)}, bf16[1024,1024]{1,0:T(8,128)(2,1)}) custom-call(bf16[2048,1024]{1,0:T(8,128)(2,1)} %pad_maximum_fusion.x_ref, bf16[1024,1024]{1,0:T(8,128)(2,1)} %out_project.3.own_ref, bf16[1024,1024]{1,0:T(8,128)(2,1)} %collective-permute-done.2.other_ref, ...), custom_call_target="tpu_custom_call" | custom-call | flops 7730940928 | tf_op jit(solution)/shard_map/middle/pallas_call | solution.py:411
  240.8 10.9 %down_weights.1.refs_4_ = bf16[1024,4608]{1,0:T(8,128)(2,1)} custom-call(bf16[2,1024,1024]{2,1,0:T(8,128)(2,1)} %get-tuple-element.66.refs_0_, bf16[2,1024,1024]{2,1,0:T(8,128)(2,1)} %get-tuple-element.67.refs_1_, bf16[1024,4608]{1,0:T(8,128)(2,1)} %get-tuple-element.68.refs_2_, bf16[1024,4608]{1,0:T(8,128)(2,1)} %get-tuple-element.69.refs_3_), custom_call_target="tpu_custom_call" | custom-call | flops 2147483648 | tf_op jit(solution)/shard_map/down_weights/pallas_call | solution.py:504
  251.7 2.1 collective-permute-done.4.fg_other_ref
  253.9 1.4 collective-permute-start.5
  255.3 18.1 %gate_up_weights.1 = bf16[1024,4608]{1,0:T(8,128)(2,1)} custom-call(bf16[2,1024,1024]{2,1,0:T(8,128)(2,1)} %get-tuple-element.66.refs_0_, bf16[2,1024,1024]{2,1,0:T(8,128)(2,1)} %get-tuple-element.67.refs_1_, bf16[1024,4608]{1,0:T(8,128)(2,1)} %get-tuple-element.68.refs_2_, ...), custom_call_target="tpu_custom_call", output_to_operand_aliasing={{}: (4, {})} | custom-call | flops 4294967296 | tf_op jit(solution)/shard_map/gate_up_weights/pallas_call | solution.py:504
  273.5 1.5 copy-done.2
  275.0 3.2 broadcast_select_fusion.2
  278.2 12.6 %residual_back.2 = (f32[1024,1024]{1,0:T(8,128)}, bf16[1024,1024]{1,0:T(8,128)(2,1)}, bf16[1024,1024]{1,0:T(8,128)(2,1)}, f32[8,1024]{1,0:T(8,128)}) custom-call(bf16[2048,1024]{1,0:T(8,128)(2,1)} %pad_maximum_fusion.x_ref, bf16[1024,1024]{1,0:T(8,128)(2,1)} %out_project.2.own_ref, bf16[1024,1024]{1,0:T(8,128)(2,1)} %collective-permute-done.1.other_ref, ...), custom_call_target="tpu_custom_call" | custom-call | flops 11302545408 | tf_op jit(solution)/shard_map/residual_back/pallas_call | solution.py:463
  290.7 9.6 %collective-permute-done.5.fg_other_ref = bf16[1024,1024]{1,0:T(8,128)(2,1)} collective-permute-done((bf16[1024,1024]{1,0:T(8,128)(2,1)}, bf16[1024,1024]{1,0:T(8,128)(2,1)}, u32[]{:S(2)}, u32[]{:S(2)}) %collective-permute-start.5) | collective-permute-done | bytes 2097184 | tf_op jit(solution)/shard_map/ppermute | solution.py:596
  300.3 11.4 %residual_back.3 = (f32[1024,1024]{1,0:T(8,128)}, bf16[1024,1024]{1,0:T(8,128)(2,1)}, bf16[1024,1024]{1,0:T(8,128)(2,1)}, f32[8,1024]{1,0:T(8,128)}) custom-call(bf16[2048,1024]{1,0:T(8,128)(2,1)} %pad_maximum_fusion.x_ref, bf16[1024,1024]{1,0:T(8,128)(2,1)} %out_project.3.own_ref, bf16[1024,1024]{1,0:T(8,128)(2,1)} %collective-permute-done.2.other_ref, ...), custom_call_target="tpu_custom_call" | custom-call | flops 11302545408 | tf_op jit(solution)/shard_map/residual_back/pallas_call | solution.py:463
  311.7 1.4 collective-permute-start.6
  313.1 83.6 %attend_back.1 = (bf16[2048,2048]{1,0:T(8,128)(2,1)}, f32[4,8,128]{2,1,0:T(8,128)}, f32[4,8,128]{2,1,0:T(8,128)}) custom-call(bf16[2048,2048]{1,0:T(8,128)(2,1)} %get-tuple-element.54.refs_0_.refs_1_.refs_2_.rot_ref, bf16[2048,2048]{1,0:T(8,128)(2,1)} %get-tuple-element.76.raw_ref, bf16[1024,1024]{1,0:T(8,128)(2,1)} %get-tuple-element.77.do_a, ...), custom_call_target="tpu_custom_call" | custom-call | flops 268435456000 | tf_op jit(solution)/shard_map/attend_back/pallas_call | solution.py:326
  396.7 20.5 %attention_weights.1 = (bf16[1024,3072]{1,0:T(8,128)(2,1)}, f32[1024,128]{1,0:T(8,128)}) custom-call(bf16[1024,2048]{1,0:T(8,128)(2,1)} %get-tuple-element.83.refs_0_, bf16[1024,1024]{1,0:T(8,128)(2,1)} %get-tuple-element.63.refs_1_, bf16[1024,1024]{1,0:T(8,128)(2,1)} %get-tuple-element.84.refs_2_, bf16[2048,2048]{1,0:T(8,128)(2,1)} %get-tuple-element.82.bits_ref.refs_3_, ...), custom_call_target="tpu_custom_call" | custom-call | flops 20132659200 | tf_op jit(solution)/shard_map/attention_weights/pallas_call | solution.py:545
  417.3 1.6 copy-done.1
  418.9 0.5 fusion.8
  420.2 0.7 collective-permute-start.8
  420.9 3.0 collective-permute-done.8
  424.0 9.1 %input_back.3 = bf16[1024,1024]{1,0:T(8,128)(2,1)} custom-call(s32[1]{0:T(128)} %bitcast.7.place_ref, bf16[2048,2048]{1,0:T(8,128)(2,1)} %get-tuple-element.82.bits_ref.refs_3_, bf16[1024,3072]{1,0:T(8,128)(2,1)} %all-gather.3.cloned.1.call-done.w_ref.refs_6_), custom_call_target="tpu_custom_call" | custom-call | flops 8947848192 | tf_op jit(solution)/shard_map/input_back/pallas_call | solution.py:577
  433.1 0.6 collective-permute-start.7
  433.8 1.1 collective-permute-start.10
  434.8 9.1 %input_back.2 = bf16[1024,1024]{1,0:T(8,128)(2,1)} custom-call(s32[1]{0:T(128)} %bitcast.6.place_ref, bf16[2048,2048]{1,0:T(8,128)(2,1)} %get-tuple-element.82.bits_ref.refs_3_, bf16[1024,3072]{1,0:T(8,128)(2,1)} %all-gather.3.cloned.1.call-done.w_ref.refs_6_), custom_call_target="tpu_custom_call" | custom-call | flops 8947848192 | tf_op jit(solution)/shard_map/input_back/pallas_call | solution.py:577
  444.0 1.7 collective-permute-start.11
  445.7 1.0 fusion.11
  446.8 1.0 collective-permute-done.11
  447.8 2.3 collective-permute-start.12
  450.1 0.8 slice_bitcast_fusion
  450.9 1.9 collective-permute-done.12
  452.8 0.5 slice_bitcast_fusion.4
  453.3 0.6 slice_bitcast_fusion.2
  453.9 27.6 %collective-permute-done.7 = bf16[1024,1024]{1,0:T(8,128)(2,1)} collective-permute-done((bf16[1024,1024]{1,0:T(8,128)(2,1)}, bf16[1024,1024]{1,0:T(8,128)(2,1)}, u32[]{:S(2)}, u32[]{:S(2)}) %collective-permute-start.7) | collective-permute-done | bytes 2097184 | tf_op jit(solution)/shard_map/ppermute | solution.py:596
  481.5 2.8 fusion.2
  484.3 10.3 %fusion.5 = (f32[1024,1024]{1,0:T(8,128)}, bf16[1024,1024]{1,0:T(8,128)(2,1)}) fusion(bf16[1024,1024]{1,0:T(8,128)(2,1)S(1)} %copy-done.1, f32[1024,1024]{1,0:T(8,128)S(1)} %copy-done.6, f32[1024,1024]{1,0:T(8,128)} %get-tuple-element.75, bf16[1024,1024]{1,0:T(8,128)(2,1)} %collective-permute-done.7, bf16[1024,1024]{1,0:T(8,128)(2,1)S(1)} %copy-done.5, ...), kind=kLoop, calls=%fused_computation.8 | loop fusion | flops 24117248 | bytes 35663872 | tf_op jit(solution)/shard_map/add | solution.py:773
  494.7 6.6 %reduce-scatter.5.cloned.1.call-done = bf16[64,3072]{1,0:T(8,128)(2,1)} async-done(((bf16[1024,3072]{1,0:T(8,128)(2,1)}), bf16[64,3072]{1,0:T(8,128)(2,1)}) %reduce-scatter.5.cloned.1.call-update) | async-done | bytes 393232 | tf_op jit(solution)/shard_map/reduce_scatter | solution.py:755
  501.3 1.1 slice.36
  502.8 0.8 copy.28
  503.5 0.7 copy.34
  504.2 0.7 copy.33
  504.9 0.7 slice_bitcast_fusion.1
  (75 shorter events, 1.9 us)
Async XLA Ops:
  7.2 5.0 copy-start.11
  7.2 5.0 copy-start.12
  7.2 5.0 copy-start.13
  7.2 69.6 %all-gather.3.cloned.1.call-start = ((), (), s32[]{:S(2)}) async-start(), calls=%async_computation.2 | async-start | bytes 6684672 | tf_op jit(solution)/shard_map/all_gather | solution.py:681
  9.1 4.1 copy-start
  12.1 154.9 %all-gather.5.cloned.1.call-start = ((), (), s32[]{:S(2)}) async-start(), calls=%async_computation.3 | async-start | bytes 10027008 | tf_op jit(solution)/shard_map/all_gather | solution.py:684
  13.1 383.6 %reduce-scatter.3.cloned.1.call-start = ((), (), s32[]{:S(2)}) async-start(), calls=%async_computation.4 | async-start | bytes 10027008 | tf_op jit(solution)/shard_map/reduce_scatter | solution.py:717
  13.2 48.7 %collective-permute-start = (bf16[1024,1024]{1,0:T(8,128)(2,1)S(1)}, bf16[1024,1024]{1,0:T(8,128)(2,1)}, u32[]{:S(2)}, u32[]{:S(2)}) collective-permute-start(bf16[1024,1024]{1,0:T(8,128)(2,1)S(1)} %copy-done), channel_id=1, source_target_pairs={{0,1},{1,0},{2,3},{3,2},{4,5},{5,4},{6,7},{7,6},{8,9},{9,8},{10,11... | collective-permute-start | bytes 6291464 | tf_op jit(solution)/shard_map/ppermute | solution.py:596
  63.8 2.5 copy-start.9
  66.3 48.7 %collective-permute-start.3 = (bf16[1024,1024]{1,0:T(8,128)(2,1)S(1)}, bf16[1024,1024]{1,0:T(8,128)(2,1)}, u32[]{:S(2)}, u32[]{:S(2)}) collective-permute-start(bf16[1024,1024]{1,0:T(8,128)(2,1)S(1)} %copy-done.9), channel_id=1, source_target_pairs={{0,1},{1,0},{2,3},{3,2},{4,5},{5,4},{6,7},{7,6},{8,9},{9,8},{10,11... | collective-permute-start | bytes 6291464 | tf_op jit(solution)/shard_map/ppermute | solution.py:596
  113.5 48.1 %collective-permute-start.1 = (bf16[1024,1024]{1,0:T(8,128)(2,1)}, bf16[1024,1024]{1,0:T(8,128)(2,1)}, u32[]{:S(2)}, u32[]{:S(2)}) collective-permute-start(bf16[1024,1024]{1,0:T(8,128)(2,1)} %out_project.2.own_ref), channel_id=1, source_target_pairs={{0,1},{1,0},{2,3},{3,2},{4,5},{5,4},{6,7},{7,6},{8,9},{9,8},{10,11... | collective-permute-start | bytes 6291464 | tf_op jit(solution)/shard_map/ppermute | solution.py:596
  161.6 48.9 %collective-permute-start.2 = (bf16[1024,1024]{1,0:T(8,128)(2,1)}, bf16[1024,1024]{1,0:T(8,128)(2,1)}, u32[]{:S(2)}, u32[]{:S(2)}) collective-permute-start(bf16[1024,1024]{1,0:T(8,128)(2,1)} %out_project.3.own_ref), channel_id=1, source_target_pairs={{0,1},{1,0},{2,3},{3,2},{4,5},{5,4},{6,7},{7,6},{8,9},{9,8},{10,11... | collective-permute-start | bytes 6291464 | tf_op jit(solution)/shard_map/ppermute | solution.py:596
  197.6 56.2 %collective-permute-start.4 = (bf16[1024,1024]{1,0:T(8,128)(2,1)}, bf16[1024,1024]{1,0:T(8,128)(2,1)}, u32[]{:S(2)}, u32[]{:S(2)}) collective-permute-start(bf16[1024,1024]{1,0:T(8,128)(2,1)} %get-tuple-element.62.fg_ref), channel_id=1, source_target_pairs={{0,1},{1,0},{2,3},{3,2},{4,5},{5,4},{6,7},{7,6},{8,9},{9,8},{10,11... | collective-permute-start | bytes 6291464 | tf_op jit(solution)/shard_map/ppermute | solution.py:596
  253.9 46.4 %collective-permute-start.5 = (bf16[1024,1024]{1,0:T(8,128)(2,1)}, bf16[1024,1024]{1,0:T(8,128)(2,1)}, u32[]{:S(2)}, u32[]{:S(2)}) collective-permute-start(bf16[1024,1024]{1,0:T(8,128)(2,1)} %get-tuple-element.70.fg_ref), channel_id=1, source_target_pairs={{0,1},{1,0},{2,3},{3,2},{4,5},{5,4},{6,7},{7,6},{8,9},{9,8},{10,11... | collective-permute-start | bytes 6291464 | tf_op jit(solution)/shard_map/ppermute | solution.py:596
  273.4 1.6 copy-start.2
  273.4 227.9 %reduce-scatter.5.cloned.1.call-start = ((), (), s32[]{:S(2)}) async-start(), calls=%async_computation.5 | async-start | bytes 6684672 | tf_op jit(solution)/shard_map/reduce_scatter | solution.py:755
  311.7 85.0 %collective-permute-start.6 = (bf16[1024,1024]{1,0:T(8,128)(2,1)}, bf16[1024,1024]{1,0:T(8,128)(2,1)}, u32[]{:S(2)}, u32[]{:S(2)}) collective-permute-start(bf16[1024,1024]{1,0:T(8,128)(2,1)} %broadcast_select_fusion.2), channel_id=1, source_target_pairs={{0,1},{1,0},{2,3},{3,2},{4,5},{5,4},{6,7},{7,6},{8,9},{9,8},{10,11... | collective-permute-start | bytes 6291464 | tf_op jit(solution)/shard_map/ppermute | solution.py:596
  417.3 1.6 copy-start.1
  418.9 0.8 copy-start.15
  418.9 0.8 copy-start.18
  418.9 0.8 copy-start.17
  418.9 0.8 copy-start.16
  418.9 1.1 copy-start.10
  418.9 1.3 copy-start.14
  420.2 3.8 collective-permute-start.8
  424.0 9.8 %collective-permute-start.9 = (f32[18,128]{1,0:T(8,128)S(1)}, f32[18,128]{1,0:T(8,128)S(1)}, u32[]{:S(2)}, u32[]{:S(2)}) collective-permute-start(f32[18,128]{1,0:T(8,128)S(1)} %fusion.10), channel_id=1, source_target_pairs={{0,2},{1,3},{2,0},{3,1},{4,6},{5,7},{6,4},{7,5},{8,10},{9,11},{10,... | collective-permute-start | bytes 27656 | tf_op jit(solution)/shard_map/ppermute | solution.py:635
  433.1 48.3 %collective-permute-start.7 = (bf16[1024,1024]{1,0:T(8,128)(2,1)}, bf16[1024,1024]{1,0:T(8,128)(2,1)}, u32[]{:S(2)}, u32[]{:S(2)}) collective-permute-start(bf16[1024,1024]{1,0:T(8,128)(2,1)} %input_back.3), channel_id=1, source_target_pairs={{0,1},{1,0},{2,3},{3,2},{4,5},{5,4},{6,7},{7,6},{8,9},{9,8},{10,11... | collective-permute-start | bytes 6291464 | tf_op jit(solution)/shard_map/ppermute | solution.py:596
  433.8 10.2 %collective-permute-start.10 = (f32[18,128]{1,0:T(8,128)S(1)}, f32[18,128]{1,0:T(8,128)S(1)}, u32[]{:S(2)}, u32[]{:S(2)}) collective-permute-start(f32[18,128]{1,0:T(8,128)S(1)} %fusion.13), channel_id=1, source_target_pairs={{0,4},{1,5},{2,6},{3,7},{4,0},{5,1},{6,2},{7,3},{8,12},{9,13},{10,... | collective-permute-start | bytes 27656 | tf_op jit(solution)/shard_map/ppermute | solution.py:635
  434.8 10.9 %copy-start.7 = (bf16[64,4608]{1,0:T(8,128)(2,1)S(1)}, bf16[64,4608]{1,0:T(8,128)(2,1)}, u32[]{:S(2)}) copy-start(bf16[64,4608]{1,0:T(8,128)(2,1)} %reduce-scatter.3.cloned.1.call-done) | copy-start | bytes 1769476
  444.0 37.5 %copy-start.5 = (bf16[1024,1024]{1,0:T(8,128)(2,1)S(1)}, bf16[1024,1024]{1,0:T(8,128)(2,1)}, u32[]{:S(2)}) copy-start(bf16[1024,1024]{1,0:T(8,128)(2,1)} %input_back.2) | copy-start | bytes 6291460
  444.0 3.8 collective-permute-start.11
  446.7 37.6 %copy-start.6 = (f32[1024,1024]{1,0:T(8,128)S(1)}, f32[1024,1024]{1,0:T(8,128)}, u32[]{:S(2)}) copy-start(f32[1024,1024]{1,0:T(8,128)} %get-tuple-element.74) | copy-start | bytes 12582916
  447.8 5.0 collective-permute-start.12
  453.9 30.4 %copy-start.3 = (bf16[1024,1024]{1,0:T(8,128)(2,1)S(1)}, bf16[1024,1024]{1,0:T(8,128)(2,1)}, u32[]{:S(2)}) copy-start(bf16[1024,1024]{1,0:T(8,128)(2,1)} %get-tuple-element.59) | copy-start | bytes 6291460
  453.9 30.4 %copy-start.4 = (bf16[1024,1024]{1,0:T(8,128)(2,1)S(1)}, bf16[1024,1024]{1,0:T(8,128)(2,1)}, u32[]{:S(2)}) copy-start(bf16[1024,1024]{1,0:T(8,128)(2,1)} %get-tuple-element.61) | copy-start | bytes 6291460
  501.3 3.6 copy-start.8
Sparse Core Ops, SparseCore 0:
  12.3 64.5 all-gather.2
  79.1 80.0 all-gather.4
  273.5 109.0 reduce-scatter.2
  417.4 83.7 reduce-scatter.4

commit v4 on v3

--- a/solution.py
+++ b/solution.py
@@ -406,7 +406,7 @@
 
 def middle(half, x_all, own, other, grad_all, gain, weights):
     width, columns = weights.shape
-    rows = 256
+    rows = 512
     near = pl.BlockSpec((rows, width), lambda i: (i, 0))
     return pl.pallas_call(
         middle_kernel,
@@ -679,10 +679,11 @@
         axis=1,
     )
     attention_w = lax.all_gather(own_attention, "dp", axis=0, tiled=True)
-    x_all = all_tokens(layer_input, send_tokens(layer_input, ranks), ranks)
+    x_sent = send_tokens(layer_input, ranks)
+    x_all = all_tokens(layer_input, x_sent, ranks)
     own_middle = jnp.concatenate([gate_weight, up_weight, down_weight.T], axis=1)
     middle_w = lax.all_gather(own_middle, "dp", axis=0, tiled=True)
-    grad_sent = send_tokens(after(out_grad, x_all), ranks)
+    grad_sent = send_tokens(after(out_grad, x_sent), ranks)
 
     cosine, sine = rope_tables()
     norm_q, norm_k = query_norm[None, :], key_norm[None, :]

time: 518 us -> 518 us (level)
  no operation moved by 1% of the time
where the time goes in v4:
time: 518 us; the launch traced here: 512 us
  Pallas kernels  307 us (59%)
  waiting for transfers between devices  122 us (24%)
  other arithmetic  37.9 us (7%)
  starting transfers between devices  17.8 us (3%)
  between operations  14.4 us (3%)
  local copies, waits for them, and re-layouts  13.8 us (3%)
    ppermute x8, waiting for transfers between devices, swap(): return lax.ppermute(values, 'tensor', [(0, 1), (1, 0)])  101 us
    pallas_call x1, Pallas kernels, attend_back(): pl.pallas_call(attend_back_kernel, grid=(groups,), in_specs=[pl.BlockSpec...  83.6 us
    pallas_call x2, Pallas kernels, middle(): pl.pallas_call(middle_kernel, grid=(HALF // rows,), in_specs=[half_rows(r...  61.7 us
    pallas_call x2, Pallas kernels, attend(): pl.pallas_call(lambda *refs: attend_kernel(first, *refs), grid=(groups, b...  40.1 us
    pallas_call x2, Pallas kernels, middle_weights(): pl.pallas_call(lambda *refs: middle_weights_kernel(0, *refs), grid=(block...  29 us
    pallas_call x2, Pallas kernels, residual_back(): pl.pallas_call(residual_back_kernel, grid=(HALF // rows,), in_specs=[half...  24 us
    pallas_call x1, Pallas kernels, attention_weights(): pl.pallas_call(lambda *refs: attention_weights_kernel(bound, *refs), grid...  20.5 us
    pallas_call x2, Pallas kernels, input_back(): pl.pallas_call(input_back_kernel, grid_spec=pltpu.PrefetchScalarGridSpec(...  18.3 us
  transfers between devices with their start and end apart: 17, of which 11 were waited for; matrix products, arithmetic and copies ran while one was open for 8% of the time, Pallas kernels for 56%

profile of v4, /device:TPU:0, one launch (start us, length us, event | category | flops | bytes accessed | tf_op | source)
XLA Modules:
  0.0 512.4 jit_solution(15424518088195890835)
XLA Ops:
  7.3 1.0 reshape.90
  8.2 0.9 reshape.89
  9.1 1.1 reshape.88
  10.4 1.7 pad_maximum_fusion.5
  12.2 0.9 pad_maximum_fusion.4
  13.2 3.0 collective-permute-start
  16.2 3.7 fusion.9
  19.9 2.1 pad_maximum_fusion.2
  22.0 39.9 %collective-permute-done = bf16[1024,1024]{1,0:T(8,128)(2,1)} collective-permute-done((bf16[1024,1024]{1,0:T(8,128)(2,1)S(1)}, bf16[1024,1024]{1,0:T(8,128)(2,1)}, u32[]{:S(2)}, u32[]{:S(2)}) %collective-permute-start) | collective-permute-done | bytes 2097184 | tf_op jit(solution)/shard_map/ppermute | solution.py:596
  61.9 1.9 broadcast_select_fusion.4
  63.8 2.5 pad_maximum_fusion.x_ref
  66.3 1.8 collective-permute-start.3
  68.1 8.7 %all-gather.3.cloned.1.call-done.w_ref.refs_6_ = bf16[1024,3072]{1,0:T(8,128)(2,1)} async-done(((bf16[64,3072]{1,0:T(8,128)(2,1)}), bf16[1024,3072]{1,0:T(8,128)(2,1)}) %all-gather.3.cloned.1.call-update) | async-done | bytes 6291472 | tf_op jit(solution)/shard_map/all_gather | solution.py:681
  76.8 17.3 %project.1 = (bf16[1024,2048]{1,0:T(8,128)(2,1)}, bf16[2048,2048]{1,0:T(8,128)(2,1)}, bf16[2048,2048]{1,0:T(8,128)(2,1)}) custom-call(bf16[2048,1024]{1,0:T(8,128)(2,1)} %pad_maximum_fusion.x_ref, f32[1,1024]{1,0:T(1,128)} %bitcast.48, bf16[1024,3072]{1,0:T(8,128)(2,1)} %all-gather.3.cloned.1.call-done.w_ref.refs_6_, f32[1,128]{1,0:T(1,128)} %bitcast.53, ...), custom_call_target="tpu_custom_call" | custom-call | flops 17179869184 | tf_op jit(solution)/shard_map/project/pallas_call | solution.py:88
  94.1 13.3 %attend.2 = (bf16[1024,1024]{1,0:T(8,128)(2,1)}, bf16[1024,1024]{1,0:T(8,128)(2,1)}) custom-call(bf16[2048,2048]{1,0:T(8,128)(2,1)} %get-tuple-element.54.refs_0_.refs_1_.refs_2_.rot_ref, bf16[2048,2048]{1,0:T(8,128)(2,1)} %get-tuple-element.54.refs_0_.refs_1_.refs_2_.rot_ref, bf16[2048,2048]{1,0:T(8,128)(2,1)} %get-tuple-element.54.refs_0_.refs_1_.refs_2_.rot_ref), custom_call_target="tpu_custom_call" | custom-call | flops 8589934592 | tf_op jit(solution)/shard_map/attend/pallas_call | solution.py:172
  107.4 6.1 %out_project.2.own_ref = bf16[1024,1024]{1,0:T(8,128)(2,1)} custom-call(bf16[1024,1024]{1,0:T(8,128)(2,1)} %get-tuple-element.53.mixed_ref.out_a.refs_4_, bf16[1024,3072]{1,0:T(8,128)(2,1)} %all-gather.3.cloned.1.call-done.w_ref.refs_6_), custom_call_target="tpu_custom_call" | custom-call | flops 6135667712 | tf_op jit(solution)/shard_map/out_project/pallas_call | solution.py:205
  113.5 1.5 collective-permute-start.1
  115.0 3.8 broadcast_select_fusion.1
  118.8 26.8 %attend.3 = (bf16[1024,1024]{1,0:T(8,128)(2,1)}, bf16[1024,1024]{1,0:T(8,128)(2,1)}) custom-call(bf16[2048,2048]{1,0:T(8,128)(2,1)} %get-tuple-element.54.refs_0_.refs_1_.refs_2_.rot_ref, bf16[2048,2048]{1,0:T(8,128)(2,1)} %get-tuple-element.54.refs_0_.refs_1_.refs_2_.rot_ref, bf16[2048,2048]{1,0:T(8,128)(2,1)} %get-tuple-element.54.refs_0_.refs_1_.refs_2_.rot_ref), custom_call_target="tpu_custom_call" | custom-call | flops 17179869184 | tf_op jit(solution)/shard_map/attend/pallas_call | solution.py:172
  145.6 6.1 %out_project.3.own_ref = bf16[1024,1024]{1,0:T(8,128)(2,1)} custom-call(bf16[1024,1024]{1,0:T(8,128)(2,1)} %get-tuple-element.55.mixed_ref.out_b.refs_5_, bf16[1024,3072]{1,0:T(8,128)(2,1)} %all-gather.3.cloned.1.call-done.w_ref.refs_6_), custom_call_target="tpu_custom_call" | custom-call | flops 6135667712 | tf_op jit(solution)/shard_map/out_project/pallas_call | solution.py:205
  151.7 9.9 %collective-permute-done.1.other_ref = bf16[1024,1024]{1,0:T(8,128)(2,1)} collective-permute-done((bf16[1024,1024]{1,0:T(8,128)(2,1)}, bf16[1024,1024]{1,0:T(8,128)(2,1)}, u32[]{:S(2)}, u32[]{:S(2)}) %collective-permute-start.1) | collective-permute-done | bytes 2097184 | tf_op jit(solution)/shard_map/ppermute | solution.py:596
  161.6 1.4 collective-permute-start.2
  163.1 4.0 pad_maximum_fusion.1.grad_ref
  167.1 30.8 %middle.2 = (bf16[1024,1024]{1,0:T(8,128)(2,1)}, bf16[2,1024,1024]{2,1,0:T(8,128)(2,1)}, bf16[1024,4608]{1,0:T(8,128)(2,1)}, bf16[1024,1024]{1,0:T(8,128)(2,1)}) custom-call(bf16[2048,1024]{1,0:T(8,128)(2,1)} %pad_maximum_fusion.x_ref, bf16[1024,1024]{1,0:T(8,128)(2,1)} %out_project.2.own_ref, bf16[1024,1024]{1,0:T(8,128)(2,1)} %collective-permute-done.1.other_ref, ...), custom_call_target="tpu_custom_call" | custom-call | flops 7730940928 | tf_op jit(solution)/shard_map/middle/pallas_call | solution.py:411
  197.9 0.6 collective-permute-start.4
  198.5 12.0 %collective-permute-done.2.other_ref = bf16[1024,1024]{1,0:T(8,128)(2,1)} collective-permute-done((bf16[1024,1024]{1,0:T(8,128)(2,1)}, bf16[1024,1024]{1,0:T(8,128)(2,1)}, u32[]{:S(2)}, u32[]{:S(2)}) %collective-permute-start.2) | collective-permute-done | bytes 2097184 | tf_op jit(solution)/shard_map/ppermute | solution.py:596
  210.5 30.9 %middle.3 = (bf16[1024,1024]{1,0:T(8,128)(2,1)}, bf16[2,1024,1024]{2,1,0:T(8,128)(2,1)}, bf16[1024,4608]{1,0:T(8,128)(2,1)}, bf16[1024,1024]{1,0:T(8,128)(2,1)}) custom-call(bf16[2048,1024]{1,0:T(8,128)(2,1)} %pad_maximum_fusion.x_ref, bf16[1024,1024]{1,0:T(8,128)(2,1)} %out_project.3.own_ref, bf16[1024,1024]{1,0:T(8,128)(2,1)} %collective-permute-done.2.other_ref, ...), custom_call_target="tpu_custom_call" | custom-call | flops 7730940928 | tf_op jit(solution)/shard_map/middle/pallas_call | solution.py:411
  241.4 10.9 %down_weights.1.refs_4_ = bf16[1024,4608]{1,0:T(8,128)(2,1)} custom-call(bf16[2,1024,1024]{2,1,0:T(8,128)(2,1)} %get-tuple-element.66.refs_0_, bf16[2,1024,1024]{2,1,0:T(8,128)(2,1)} %get-tuple-element.67.refs_1_, bf16[1024,4608]{1,0:T(8,128)(2,1)} %get-tuple-element.68.refs_2_, bf16[1024,4608]{1,0:T(8,128)(2,1)} %get-tuple-element.69.refs_3_), custom_call_target="tpu_custom_call" | custom-call | flops 2147483648 | tf_op jit(solution)/shard_map/down_weights/pallas_call | solution.py:504
  252.3 1.6 collective-permute-done.4.fg_other_ref
  253.9 1.4 collective-permute-start.5
  255.3 18.1 %gate_up_weights.1 = bf16[1024,4608]{1,0:T(8,128)(2,1)} custom-call(bf16[2,1024,1024]{2,1,0:T(8,128)(2,1)} %get-tuple-element.66.refs_0_, bf16[2,1024,1024]{2,1,0:T(8,128)(2,1)} %get-tuple-element.67.refs_1_, bf16[1024,4608]{1,0:T(8,128)(2,1)} %get-tuple-element.68.refs_2_, ...), custom_call_target="tpu_custom_call", output_to_operand_aliasing={{}: (4, {})} | custom-call | flops 4294967296 | tf_op jit(solution)/shard_map/gate_up_weights/pallas_call | solution.py:504
  273.5 1.5 copy-done.2
  275.0 3.2 broadcast_select_fusion.2
  278.2 12.6 %residual_back.2 = (f32[1024,1024]{1,0:T(8,128)}, bf16[1024,1024]{1,0:T(8,128)(2,1)}, bf16[1024,1024]{1,0:T(8,128)(2,1)}, f32[8,1024]{1,0:T(8,128)}) custom-call(bf16[2048,1024]{1,0:T(8,128)(2,1)} %pad_maximum_fusion.x_ref, bf16[1024,1024]{1,0:T(8,128)(2,1)} %out_project.2.own_ref, bf16[1024,1024]{1,0:T(8,128)(2,1)} %collective-permute-done.1.other_ref, ...), custom_call_target="tpu_custom_call" | custom-call | flops 11302545408 | tf_op jit(solution)/shard_map/residual_back/pallas_call | solution.py:463
  290.8 9.5 %collective-permute-done.5.fg_other_ref = bf16[1024,1024]{1,0:T(8,128)(2,1)} collective-permute-done((bf16[1024,1024]{1,0:T(8,128)(2,1)}, bf16[1024,1024]{1,0:T(8,128)(2,1)}, u32[]{:S(2)}, u32[]{:S(2)}) %collective-permute-start.5) | collective-permute-done | bytes 2097184 | tf_op jit(solution)/shard_map/ppermute | solution.py:596
  300.3 11.4 %residual_back.3 = (f32[1024,1024]{1,0:T(8,128)}, bf16[1024,1024]{1,0:T(8,128)(2,1)}, bf16[1024,1024]{1,0:T(8,128)(2,1)}, f32[8,1024]{1,0:T(8,128)}) custom-call(bf16[2048,1024]{1,0:T(8,128)(2,1)} %pad_maximum_fusion.x_ref, bf16[1024,1024]{1,0:T(8,128)(2,1)} %out_project.3.own_ref, bf16[1024,1024]{1,0:T(8,128)(2,1)} %collective-permute-done.2.other_ref, ...), custom_call_target="tpu_custom_call" | custom-call | flops 11302545408 | tf_op jit(solution)/shard_map/residual_back/pallas_call | solution.py:463
  311.7 1.4 collective-permute-start.6
  313.1 83.6 %attend_back.1 = (bf16[2048,2048]{1,0:T(8,128)(2,1)}, f32[4,8,128]{2,1,0:T(8,128)}, f32[4,8,128]{2,1,0:T(8,128)}) custom-call(bf16[2048,2048]{1,0:T(8,128)(2,1)} %get-tuple-element.54.refs_0_.refs_1_.refs_2_.rot_ref, bf16[2048,2048]{1,0:T(8,128)(2,1)} %get-tuple-element.76.raw_ref, bf16[1024,1024]{1,0:T(8,128)(2,1)} %get-tuple-element.77.do_a, ...), custom_call_target="tpu_custom_call" | custom-call | flops 268435456000 | tf_op jit(solution)/shard_map/attend_back/pallas_call | solution.py:326
  396.7 20.5 %attention_weights.1 = (bf16[1024,3072]{1,0:T(8,128)(2,1)}, f32[1024,128]{1,0:T(8,128)}) custom-call(bf16[1024,2048]{1,0:T(8,128)(2,1)} %get-tuple-element.83.refs_0_, bf16[1024,1024]{1,0:T(8,128)(2,1)} %get-tuple-element.63.refs_1_, bf16[1024,1024]{1,0:T(8,128)(2,1)} %get-tuple-element.84.refs_2_, bf16[2048,2048]{1,0:T(8,128)(2,1)} %get-tuple-element.82.bits_ref.refs_3_, ...), custom_call_target="tpu_custom_call" | custom-call | flops 20132659200 | tf_op jit(solution)/shard_map/attention_weights/pallas_call | solution.py:545
  417.3 1.6 copy-done.1
  418.9 0.5 fusion.8
  420.2 0.7 collective-permute-start.8
  420.9 3.0 collective-permute-done.8
  424.0 9.1 %input_back.3 = bf16[1024,1024]{1,0:T(8,128)(2,1)} custom-call(s32[1]{0:T(128)} %bitcast.7.place_ref, bf16[2048,2048]{1,0:T(8,128)(2,1)} %get-tuple-element.82.bits_ref.refs_3_, bf16[1024,3072]{1,0:T(8,128)(2,1)} %all-gather.3.cloned.1.call-done.w_ref.refs_6_), custom_call_target="tpu_custom_call" | custom-call | flops 8947848192 | tf_op jit(solution)/shard_map/input_back/pallas_call | solution.py:577
  433.1 0.6 collective-permute-start.7
  433.8 1.1 collective-permute-start.10
  434.8 9.2 %input_back.2 = bf16[1024,1024]{1,0:T(8,128)(2,1)} custom-call(s32[1]{0:T(128)} %bitcast.6.place_ref, bf16[2048,2048]{1,0:T(8,128)(2,1)} %get-tuple-element.82.bits_ref.refs_3_, bf16[1024,3072]{1,0:T(8,128)(2,1)} %all-gather.3.cloned.1.call-done.w_ref.refs_6_), custom_call_target="tpu_custom_call" | custom-call | flops 8947848192 | tf_op jit(solution)/shard_map/input_back/pallas_call | solution.py:577
  444.0 1.7 collective-permute-start.11
  445.7 1.0 fusion.11
  446.8 1.0 collective-permute-done.11
  447.8 2.3 collective-permute-start.12
  450.1 0.8 slice_bitcast_fusion
  450.9 1.9 collective-permute-done.12
  452.8 0.5 slice_bitcast_fusion.4
  453.3 0.6 slice_bitcast_fusion.2
  453.9 27.6 %collective-permute-done.7 = bf16[1024,1024]{1,0:T(8,128)(2,1)} collective-permute-done((bf16[1024,1024]{1,0:T(8,128)(2,1)}, bf16[1024,1024]{1,0:T(8,128)(2,1)}, u32[]{:S(2)}, u32[]{:S(2)}) %collective-permute-start.7) | collective-permute-done | bytes 2097184 | tf_op jit(solution)/shard_map/ppermute | solution.py:596
  481.5 2.8 fusion.2
  484.3 10.3 %fusion.5 = (f32[1024,1024]{1,0:T(8,128)}, bf16[1024,1024]{1,0:T(8,128)(2,1)}) fusion(bf16[1024,1024]{1,0:T(8,128)(2,1)S(1)} %copy-done.1, f32[1024,1024]{1,0:T(8,128)S(1)} %copy-done.6, f32[1024,1024]{1,0:T(8,128)} %get-tuple-element.75, bf16[1024,1024]{1,0:T(8,128)(2,1)} %collective-permute-done.7, bf16[1024,1024]{1,0:T(8,128)(2,1)S(1)} %copy-done.5, ...), kind=kLoop, calls=%fused_computation.8 | loop fusion | flops 24117248 | bytes 35663872 | tf_op jit(solution)/shard_map/add | solution.py:774
  494.7 6.6 %reduce-scatter.5.cloned.1.call-done = bf16[64,3072]{1,0:T(8,128)(2,1)} async-done(((bf16[1024,3072]{1,0:T(8,128)(2,1)}), bf16[64,3072]{1,0:T(8,128)(2,1)}) %reduce-scatter.5.cloned.1.call-update) | async-done | bytes 393232 | tf_op jit(solution)/shard_map/reduce_scatter | solution.py:756
  501.3 1.1 slice.36
  502.8 0.8 copy.28
  503.5 0.7 copy.34
  504.2 0.7 copy.33
  504.9 0.7 slice_bitcast_fusion.1
  (75 shorter events, 1.9 us)
Async XLA Ops:
  7.2 5.0 copy-start.11
  7.2 5.0 copy-start.12
  7.2 5.0 copy-start.13
  7.2 69.6 %all-gather.3.cloned.1.call-start = ((), (), s32[]{:S(2)}) async-start(), calls=%async_computation.2 | async-start | bytes 6684672 | tf_op jit(solution)/shard_map/all_gather | solution.py:681
  9.1 4.1 copy-start
  12.1 154.9 %all-gather.5.cloned.1.call-start = ((), (), s32[]{:S(2)}) async-start(), calls=%async_computation.3 | async-start | bytes 10027008 | tf_op jit(solution)/shard_map/all_gather | solution.py:685
  13.1 383.6 %reduce-scatter.3.cloned.1.call-start = ((), (), s32[]{:S(2)}) async-start(), calls=%async_computation.4 | async-start | bytes 10027008 | tf_op jit(solution)/shard_map/reduce_scatter | solution.py:718
  13.2 48.7 %collective-permute-start = (bf16[1024,1024]{1,0:T(8,128)(2,1)S(1)}, bf16[1024,1024]{1,0:T(8,128)(2,1)}, u32[]{:S(2)}, u32[]{:S(2)}) collective-permute-start(bf16[1024,1024]{1,0:T(8,128)(2,1)S(1)} %copy-done), channel_id=1, source_target_pairs={{0,1},{1,0},{2,3},{3,2},{4,5},{5,4},{6,7},{7,6},{8,9},{9,8},{10,11... | collective-permute-start | bytes 6291464 | tf_op jit(solution)/shard_map/ppermute | solution.py:596
  63.8 2.5 copy-start.9
  66.3 48.7 %collective-permute-start.3 = (bf16[1024,1024]{1,0:T(8,128)(2,1)S(1)}, bf16[1024,1024]{1,0:T(8,128)(2,1)}, u32[]{:S(2)}, u32[]{:S(2)}) collective-permute-start(bf16[1024,1024]{1,0:T(8,128)(2,1)S(1)} %copy-done.9), channel_id=1, source_target_pairs={{0,1},{1,0},{2,3},{3,2},{4,5},{5,4},{6,7},{7,6},{8,9},{9,8},{10,11... | collective-permute-start | bytes 6291464 | tf_op jit(solution)/shard_map/ppermute | solution.py:596
  113.5 48.1 %collective-permute-start.1 = (bf16[1024,1024]{1,0:T(8,128)(2,1)}, bf16[1024,1024]{1,0:T(8,128)(2,1)}, u32[]{:S(2)}, u32[]{:S(2)}) collective-permute-start(bf16[1024,1024]{1,0:T(8,128)(2,1)} %out_project.2.own_ref), channel_id=1, source_target_pairs={{0,1},{1,0},{2,3},{3,2},{4,5},{5,4},{6,7},{7,6},{8,9},{9,8},{10,11... | collective-permute-start | bytes 6291464 | tf_op jit(solution)/shard_map/ppermute | solution.py:596
  161.6 48.9 %collective-permute-start.2 = (bf16[1024,1024]{1,0:T(8,128)(2,1)}, bf16[1024,1024]{1,0:T(8,128)(2,1)}, u32[]{:S(2)}, u32[]{:S(2)}) collective-permute-start(bf16[1024,1024]{1,0:T(8,128)(2,1)} %out_project.3.own_ref), channel_id=1, source_target_pairs={{0,1},{1,0},{2,3},{3,2},{4,5},{5,4},{6,7},{7,6},{8,9},{9,8},{10,11... | collective-permute-start | bytes 6291464 | tf_op jit(solution)/shard_map/ppermute | solution.py:596
  197.9 56.0 %collective-permute-start.4 = (bf16[1024,1024]{1,0:T(8,128)(2,1)}, bf16[1024,1024]{1,0:T(8,128)(2,1)}, u32[]{:S(2)}, u32[]{:S(2)}) collective-permute-start(bf16[1024,1024]{1,0:T(8,128)(2,1)} %get-tuple-element.62.fg_ref), channel_id=1, source_target_pairs={{0,1},{1,0},{2,3},{3,2},{4,5},{5,4},{6,7},{7,6},{8,9},{9,8},{10,11... | collective-permute-start | bytes 6291464 | tf_op jit(solution)/shard_map/ppermute | solution.py:596
  253.9 46.4 %collective-permute-start.5 = (bf16[1024,1024]{1,0:T(8,128)(2,1)}, bf16[1024,1024]{1,0:T(8,128)(2,1)}, u32[]{:S(2)}, u32[]{:S(2)}) collective-permute-start(bf16[1024,1024]{1,0:T(8,128)(2,1)} %get-tuple-element.70.fg_ref), channel_id=1, source_target_pairs={{0,1},{1,0},{2,3},{3,2},{4,5},{5,4},{6,7},{7,6},{8,9},{9,8},{10,11... | collective-permute-start | bytes 6291464 | tf_op jit(solution)/shard_map/ppermute | solution.py:596
  273.4 1.6 copy-start.2
  273.4 227.9 %reduce-scatter.5.cloned.1.call-start = ((), (), s32[]{:S(2)}) async-start(), calls=%async_computation.5 | async-start | bytes 6684672 | tf_op jit(solution)/shard_map/reduce_scatter | solution.py:756
  311.7 85.0 %collective-permute-start.6 = (bf16[1024,1024]{1,0:T(8,128)(2,1)}, bf16[1024,1024]{1,0:T(8,128)(2,1)}, u32[]{:S(2)}, u32[]{:S(2)}) collective-permute-start(bf16[1024,1024]{1,0:T(8,128)(2,1)} %broadcast_select_fusion.2), channel_id=1, source_target_pairs={{0,1},{1,0},{2,3},{3,2},{4,5},{5,4},{6,7},{7,6},{8,9},{9,8},{10,11... | collective-permute-start | bytes 6291464 | tf_op jit(solution)/shard_map/ppermute | solution.py:596
  417.3 1.6 copy-start.1
  418.9 0.8 copy-start.15
  418.9 0.8 copy-start.18
  418.9 0.8 copy-start.17
  418.9 0.8 copy-start.16
  418.9 1.1 copy-start.10
  418.9 1.3 copy-start.14
  420.2 3.8 collective-permute-start.8
  424.0 9.8 %collective-permute-start.9 = (f32[18,128]{1,0:T(8,128)S(1)}, f32[18,128]{1,0:T(8,128)S(1)}, u32[]{:S(2)}, u32[]{:S(2)}) collective-permute-start(f32[18,128]{1,0:T(8,128)S(1)} %fusion.10), channel_id=1, source_target_pairs={{0,2},{1,3},{2,0},{3,1},{4,6},{5,7},{6,4},{7,5},{8,10},{9,11},{10,... | collective-permute-start | bytes 27656 | tf_op jit(solution)/shard_map/ppermute | solution.py:635
  433.1 48.3 %collective-permute-start.7 = (bf16[1024,1024]{1,0:T(8,128)(2,1)}, bf16[1024,1024]{1,0:T(8,128)(2,1)}, u32[]{:S(2)}, u32[]{:S(2)}) collective-permute-start(bf16[1024,1024]{1,0:T(8,128)(2,1)} %input_back.3), channel_id=1, source_target_pairs={{0,1},{1,0},{2,3},{3,2},{4,5},{5,4},{6,7},{7,6},{8,9},{9,8},{10,11... | collective-permute-start | bytes 6291464 | tf_op jit(solution)/shard_map/ppermute | solution.py:596
  433.8 10.2 %collective-permute-start.10 = (f32[18,128]{1,0:T(8,128)S(1)}, f32[18,128]{1,0:T(8,128)S(1)}, u32[]{:S(2)}, u32[]{:S(2)}) collective-permute-start(f32[18,128]{1,0:T(8,128)S(1)} %fusion.13), channel_id=1, source_target_pairs={{0,4},{1,5},{2,6},{3,7},{4,0},{5,1},{6,2},{7,3},{8,12},{9,13},{10,... | collective-permute-start | bytes 27656 | tf_op jit(solution)/shard_map/ppermute | solution.py:635
  434.8 10.9 %copy-start.7 = (bf16[64,4608]{1,0:T(8,128)(2,1)S(1)}, bf16[64,4608]{1,0:T(8,128)(2,1)}, u32[]{:S(2)}) copy-start(bf16[64,4608]{1,0:T(8,128)(2,1)} %reduce-scatter.3.cloned.1.call-done) | copy-start | bytes 1769476
  444.0 37.5 %copy-start.5 = (bf16[1024,1024]{1,0:T(8,128)(2,1)S(1)}, bf16[1024,1024]{1,0:T(8,128)(2,1)}, u32[]{:S(2)}) copy-start(bf16[1024,1024]{1,0:T(8,128)(2,1)} %input_back.2) | copy-start | bytes 6291460
  444.0 3.8 collective-permute-start.11
  446.7 37.6 %copy-start.6 = (f32[1024,1024]{1,0:T(8,128)S(1)}, f32[1024,1024]{1,0:T(8,128)}, u32[]{:S(2)}) copy-start(f32[1024,1024]{1,0:T(8,128)} %get-tuple-element.74) | copy-start | bytes 12582916
  447.8 5.0 collective-permute-start.12
  453.9 30.4 %copy-start.3 = (bf16[1024,1024]{1,0:T(8,128)(2,1)S(1)}, bf16[1024,1024]{1,0:T(8,128)(2,1)}, u32[]{:S(2)}) copy-start(bf16[1024,1024]{1,0:T(8,128)(2,1)} %get-tuple-element.59) | copy-start | bytes 6291460
  453.9 30.4 %copy-start.4 = (bf16[1024,1024]{1,0:T(8,128)(2,1)S(1)}, bf16[1024,1024]{1,0:T(8,128)(2,1)}, u32[]{:S(2)}) copy-start(bf16[1024,1024]{1,0:T(8,128)(2,1)} %get-tuple-element.61) | copy-start | bytes 6291460
  501.3 3.6 copy-start.8
Sparse Core Ops, SparseCore 0:
  12.3 64.5 all-gather.2
  79.1 80.0 all-gather.4
  273.5 109.1 reduce-scatter.2
  417.4 83.7 reduce-scatter.4
